TPU v7x, 32 devices: a whole 2x2x4 slice. The times are simulated.
32 devices in a mesh: dp: 16 (over z, y, core), tensor: 2 (over x).
Axes of the slice: x: 2, y: 2, z: 4, core: 2. Of those that a mesh axis runs over, the one named last changes fastest.
Arguments:
- residual: bfloat16 [2048, 4096], P(('dp', 'tensor')), may hold values from -6 to 6
- queries: bfloat16 [2048, 2048], P('dp', 'tensor'), may hold values from -6 to 6
- new_kv: bfloat16 [2, 2048, 2048], P(None, 'dp', 'tensor'), may hold values from -6 to 6
- kv_pool: bfloat16 [64, 2, 16, 2048], P('dp', None, None, 'tensor'), may hold values from -6 to 6
- fetch_pages: int32 [16, 16, 2], replicated, may hold values from 0 to 3
- page_owner: int32 [16, 32], P('dp'), may hold values from 0 to 7
- segment_ids: int32 [16, 128], P('dp'), may hold values from 0 to 7, never falling along the last dimension, each value on 1 to 32 neighbouring positions
- out_weight: bfloat16 [2048, 4096], P('tensor'), may hold values from -0.125 to 0.125
- out_bias: bfloat16 [4096], replicated, may hold values from -3 to 3
Outputs:
- hidden_out: bfloat16 [2048, 4096], P(('dp', 'tensor'))
- key_cache: bfloat16 [2048, 2048], P('dp', 'tensor')
All inputs are finite; a program needn't handle non-finite values.
Results may differ from a plain program's by a relative error of at most 0.0055.
Values may be sent and summed in bfloat16 or wider, within the bound.
No kernel may reach another device: no remote copies, remote signals or barrier semaphores. Data moves between devices by JAX's collectives and lax.ppermute only.
A program may use at most 64 MiB of HBM per device.

v0:
```python
import math

import jax
import jax.numpy as jnp
from jax import lax
from jax.sharding import PartitionSpec as P

HD = 128
ROT = 32
PAGE = 16


def rotary(values, positions):
    half_rot = ROT // 2
    frequency = jnp.exp(-jnp.log(10000.0) * (2.0 * jnp.arange(half_rot, dtype=jnp.float32) / ROT))
    angles = positions.astype(jnp.float32)[:, None] * frequency[None, :]
    cosine = jnp.cos(angles)[:, None, :]
    sine_part = jnp.sin(angles)[:, None, :]
    first_half = values[..., :half_rot]
    second_half = values[..., half_rot:ROT]
    return jnp.concatenate(
        [
            first_half * cosine - second_half * sine_part,
            second_half * cosine + first_half * sine_part,
            values[..., ROT:],
        ],
        axis=-1,
    )


def body(
    residual, queries, new_kv, kv_pool, fetch_pages, page_owner, segment_ids, out_weight, out_bias
):
    group_index = lax.axis_index("dp")
    group_count = lax.axis_size("dp")
    token_count = queries.shape[0]
    feature = queries.shape[1]
    local_heads = feature // HD
    per_peer = fetch_pages.shape[2]
    segments = segment_ids[0]
    owners = page_owner[0]
    number = jnp.arange(token_count, dtype=jnp.int32)
    earlier = jnp.sum((segments[None, :] < segments[:, None]).astype(jnp.int32), axis=1)
    cached = PAGE * jnp.sum((owners[None, :] == segments[:, None]).astype(jnp.int32), axis=1)
    positions = cached + number - earlier
    rot_query = rotary(
        queries.astype(jnp.float32).reshape(token_count, local_heads, HD), positions
    ).astype(jnp.bfloat16)
    rot_key = rotary(
        new_kv[0].astype(jnp.float32).reshape(token_count, local_heads, HD), positions
    ).astype(jnp.bfloat16)
    new_values = new_kv[1].reshape(token_count, local_heads, HD)
    wanted = lax.dynamic_index_in_dim(fetch_pages, group_index, axis=1, keepdims=False)
    outgoing = jnp.take(kv_pool, wanted, axis=0)
    fetched = lax.all_to_all(outgoing, "dp", split_axis=0, concat_axis=0, tiled=True)
    prefix_len = group_count * per_peer * PAGE
    all_keys = jnp.concatenate(
        [fetched[:, :, 0].reshape(prefix_len, local_heads, HD), rot_key], axis=0
    )
    all_values = jnp.concatenate(
        [fetched[:, :, 1].reshape(prefix_len, local_heads, HD), new_values], axis=0
    )
    key_owner = jnp.repeat(owners, PAGE)
    visible = jnp.concatenate(
        [
            segments[:, None] == key_owner[None, :],
            (segments[:, None] == segments[None, :]) & (number[None, :] <= number[:, None]),
        ],
        axis=1,
    )
    score_scale = 1.0 / math.sqrt(HD)
    scores = (
        jnp.einsum("qhd,khd->hqk", rot_query, all_keys, preferred_element_type=jnp.float32)
        * score_scale
    )
    scores = jnp.where(visible[None], scores, -jnp.inf)
    row_max = jnp.max(scores, axis=-1, keepdims=True)
    lifted = jnp.exp(scores - row_max)
    weights_bf = (lifted / jnp.sum(lifted, axis=-1, keepdims=True)).astype(jnp.bfloat16)
    context = jnp.einsum(
        "hqk,khd->qhd", weights_bf, all_values, preferred_element_type=jnp.float32
    ).astype(jnp.bfloat16)
    context = context.reshape(token_count, feature)
    summed = lax.psum_scatter(
        jnp.dot(context, out_weight, preferred_element_type=jnp.float32).astype(jnp.bfloat16),
        "tensor",
        scatter_dimension=0,
        tiled=True,
    ).astype(jnp.float32)
    hidden = (residual.astype(jnp.float32) + summed + out_bias.astype(jnp.float32)[None, :]).astype(
        jnp.bfloat16
    )
    return (hidden, rot_key.reshape(token_count, feature))


def solution(mesh):
    return jax.shard_map(
        body,
        mesh=mesh,
        in_specs=(
            P(("dp", "tensor"), None),
            P("dp", "tensor"),
            P(None, "dp", "tensor"),
            P("dp", None, None, "tensor"),
            P(),
            P("dp", None),
            P("dp", None),
            P("tensor", None),
            P(),
        ),
        out_specs=(P(("dp", "tensor"), None), P("dp", "tensor")),
        check_vma=False,
    )
```

profile of v0, /device:TPU:0, one launch (start us, length us, event | category | flops | bytes accessed | tf_op | source)
XLA Modules:
  0.0 109.2 jit_solution(63796643040090833)
XLA Ops:
  7.2 0.8 constant_dynamic-slice_fusion
  8.4 0.7 gather_fusion
  9.1 0.3 broadcast_select_fusion
  9.4 1.6 %copy.88 = bf16[16,2,2,16,1024]{4,3,1,2,0:T(8,128)(2,1)} copy(bf16[16,2,2,16,1024]{4,3,2,1,0:T(8,128)(2,1)S(1)} %broadcast_select_fusion) | data formatting | bytes 4194304 | tf_op jit(solution)/shard_map/jit(_take)/select_n | solution.py:54
  11.0 7.5 %all-to-all-start = ((bf16[16,2,2,16,1024]{4,3,1,2,0:T(8,128)(2,1)}), bf16[16,2,2,16,1024]{4,3,1,2,0:T(8,128)(2,1)S(1)}, u32[]{:S(2)}, u32[]{:S(2)}) async-start(bf16[16,2,2,16,1024]{4,3,1,2,0:T(8,128)(2,1)} %copy.88), calls=%async_computation | async-start | bytes 4194304 | tf_op jit(solution)/shard_map/all_to_all | solution.py:55
  18.8 0.2 copy.92
  19.0 0.8 slice.46
  20.5 1.8 %fusion.30 = (bf16[1,128,1024]{2,1,0:T(8,128)(2,1)}, bf16[1,128,1024]{2,1,0:T(8,128)(2,1)S(1)}) fusion(bf16[2,128,1024]{2,1,0:T(8,128)(2,1)} %param.11), kind=kLoop, calls=%fused_computation.48 | loop fusion | bytes 1048576 | tf_op jit(solution)/shard_map/slice | solution.py:52
  22.4 0.7 slice.50
  23.1 0.7 fusion.31
  23.8 1.0 copy.104
  24.8 1.8 %copy.105 = f32[128,8,16]{2,0,1:T(8,128)} copy(f32[128,8,16]{0,2,1:T(8,128)} %get-tuple-element.20) | data formatting | bytes 131072
  26.6 1.8 %copy.106 = bf16[128,8,96]{2,0,1:T(8,128)(2,1)} copy(bf16[128,8,96]{0,2,1:T(8,128)(2,1)} %slice.50) | data formatting | bytes 393216
  28.4 0.7 broadcast_in_dim.26
  29.1 0.6 eq.45
  29.8 1.8 %copy.89 = bf16[1,128,1024]{1,2,0:T(8,128)(2,1)} copy(bf16[1,128,1024]{2,1,0:T(8,128)(2,1)} %get-tuple-element.18) | data formatting | bytes 524288 | tf_op jit(solution)/shard_map/slice | solution.py:52
  31.6 0.8 fusion.20
  32.4 0.8 broadcast_compare_fusion
  33.2 0.6 pad_add_fusion
  33.8 1.2 %multiply_subtract_fusion = (bf16[128,8,16]{2,0,1:T(8,128)(2,1)S(1)}, bf16[128,8,16]{2,0,1:T(8,128)(2,1)S(1)}) fusion(f32[128,8,16]{2,0,1:T(8,128)} %copy.105, f32[128,8,16]{2,0,1:T(8,128)S(1)} %copy.104, f32[128,16]{1,0:T(8,128)S(1)} %copy.94, f32[128,16]{1,0:T(8,128)S(1)} %copy.93), kind=kLoop, calls=%fused_computation.23 | loop fusion | flops 131072 | bytes 212992 | tf_op jit(solution)/shard_map/sub | solution.py:23
  35.0 1.9 %maximum_convert_fusion = bf16[128,8,128]{2,0,1:T(8,128)(2,1)} fusion(bf16[128,8,96]{2,0,1:T(8,128)(2,1)} %copy.106, bf16[128,8,16]{2,0,1:T(8,128)(2,1)S(1)} %get-tuple-element.15, bf16[128,8,16]{2,0,1:T(8,128)(2,1)S(1)} %get-tuple-element.14), kind=kLoop, calls=%fused_computation.21 | loop fusion | flops 786432 | bytes 524288 | tf_op jit(solution)/shard_map/convert_element_type | solution.py:51
  36.9 1.0 subtract_convert_fusion
  37.9 21.7 %all-to-all-done = bf16[16,2,2,16,1024]{4,3,1,2,0:T(8,128)(2,1)S(1)} async-done(((bf16[16,2,2,16,1024]{4,3,1,2,0:T(8,128)(2,1)}), bf16[16,2,2,16,1024]{4,3,1,2,0:T(8,128)(2,1)S(1)}, u32[]{:S(2)}, u32[]{:S(2)}) %all-to-all-start) | async-done | bytes 2097184 | tf_op jit(solution)/shard_map/all_to_all | solution.py:55
  59.8 0.3 copy.108
  60.2 0.3 copy.107
  60.5 0.7 copy.90
  61.2 3.9 %fusion.32 = (f32[8,128]{1,0:T(8,128)S(1)}, f32[8,128,640]{2,1,0:T(8,128)}) fusion(pred[128,640]{1,0:T(8,128)(4,1)S(1)} %copy-done.5, bf16[128,8,128]{2,0,1:T(8,128)(2,1)} %maximum_convert_fusion, bf16[512,8,128]{2,0,1:T(8,128)(2,1)S(1)} %copy.100, bf16[128,8,96]{2,0,1:T(8,128)(2,1)} %slice.46, bf16[128,8,16]{2,0,1:T(8,128)(2,1)} %get-tuple-element.17, ...), kind=kOutput, calls=%fused_computation.50 | convolution fusion | flops 173802112 | bytes 4280320 | tf_op jit(solution)/shard_map/sub | solution.py:78
  65.2 2.4 %fusion.13 = bf16[8,128,128]{2,1,0:T(8,128)(2,1)S(1)} fusion(f32[8,128,640]{2,1,0:T(8,128)} %get-tuple-element.25, f32[8,128]{1,0:T(8,128)S(1)} %get-tuple-element.24, bf16[128,8,128]{0,2,1:T(8,128)(2,1)S(1)} %bitcast.39, bf16[512,8,128]{0,2,1:T(8,128)(2,1)S(1)} %copy.90), kind=kOutput, calls=%fused_computation.19 | convolution fusion | flops 171835392 | bytes 4198400 | tf_op jit(solution)/shard_map/hqk,khd->qhd/dot_general | solution.py:80
  67.6 5.7 %convolution_convert_fusion = bf16[128,4096]{1,0:T(8,128)(2,1)} fusion(bf16[128,1024]{0,1:T(8,128)(2,1)S(1)} %bitcast.38, bf16[1024,4096]{1,0:T(8,128)(2,1)} %param.16), kind=kOutput, calls=%fused_computation.2 | convolution fusion | flops 1074266112 | bytes 9699328 | tf_op jit(solution)/shard_map/dot_general | solution.py:85
  73.6 0.9 copy.102
  74.4 25.9 %reduce-scatter.2.cloned.1.call-done = bf16[64,4096]{1,0:T(8,128)(2,1)} async-done(((bf16[128,4096]{1,0:T(8,128)(2,1)}), bf16[64,4096]{1,0:T(8,128)(2,1)}) %reduce-scatter.2.cloned.1.call-update) | async-done | bytes 524304 | tf_op jit(solution)/shard_map/reduce_scatter | solution.py:84
  100.3 2.0 %add_convert_fusion = bf16[64,4096]{1,0:T(8,128)(2,1)} fusion(bf16[64,4096]{1,0:T(8,128)(2,1)} %reduce-scatter.2.cloned.1.call-done, bf16[64,4096]{1,0:T(8,128)(2,1)S(1)} %copy-done.2, f32[4096]{0:T(1024)S(1)} %convert_element_type.66), kind=kLoop, calls=%fused_computation.20 | loop fusion | flops 1310720 | bytes 1589248 | tf_op jit(solution)/shard_map/convert_element_type | solution.py:90
  (41 shorter events, 2.0 us)
Async XLA Ops:
  7.2 1.3 %copy-start = (bf16[4,2,16,1024]{3,2,1,0:T(8,128)(2,1)S(1)}, bf16[4,2,16,1024]{3,2,1,0:T(8,128)(2,1)}, u32[]{:S(2)}) copy-start(bf16[4,2,16,1024]{3,2,1,0:T(8,128)(2,1)} %param.12) | copy-start | bytes 786436
  11.0 7.6 %copy-start.3 = (bf16[128,1024]{1,0:T(8,128)(2,1)S(1)}, bf16[128,1024]{1,0:T(8,128)(2,1)}, u32[]{:S(2)}) copy-start(bf16[128,1024]{1,0:T(8,128)(2,1)} %param.10) | copy-start | bytes 786436
  11.0 8.8 %copy-start.7 = (s32[1,128]{1,0:T(1,128)S(1)}, s32[1,128]{1,0:T(1,128)}, u32[]{:S(2)}) copy-start(s32[1,128]{1,0:T(1,128)} %param.15) | copy-start | bytes 1540
  11.0 9.0 %copy-start.8 = (s32[1,32]{1,0:T(1,128)S(1)}, s32[1,32]{1,0:T(1,128)}, u32[]{:S(2)}) copy-start(s32[1,32]{1,0:T(1,128)} %param.14) | copy-start | bytes 388
  11.0 48.6 %all-to-all-start = ((bf16[16,2,2,16,1024]{4,3,1,2,0:T(8,128)(2,1)}), bf16[16,2,2,16,1024]{4,3,1,2,0:T(8,128)(2,1)S(1)}, u32[]{:S(2)}, u32[]{:S(2)}) async-start(bf16[16,2,2,16,1024]{4,3,1,2,0:T(8,128)(2,1)} %copy.88), calls=%async_computation | async-start | bytes 4194304 | tf_op jit(solution)/shard_map/all_to_all | solution.py:55
  18.5 81.8 %reduce-scatter.2.cloned.1.call-start = ((), (), s32[]{:S(2)}) async-start(), calls=%async_computation.2 | async-start | bytes 1572864 | tf_op jit(solution)/shard_map/reduce_scatter | solution.py:84
  60.2 1.0 copy-start.5
  61.2 3.9 %copy-start.4 = (bf16[1,128,1024]{1,2,0:T(8,128)(2,1)S(1)}, bf16[1,128,1024]{1,2,0:T(8,128)(2,1)}, u32[]{:S(2)}) copy-start(bf16[1,128,1024]{1,2,0:T(8,128)(2,1)} %copy.89) | copy-start | bytes 786436
  67.6 5.8 %copy-start.1 = (bf16[128,8,128]{2,0,1:T(8,128)(2,1)S(1)}, bf16[128,8,128]{2,0,1:T(8,128)(2,1)}, u32[]{:S(2)}) copy-start(bf16[128,8,128]{2,0,1:T(8,128)(2,1)} %maximum_convert_fusion) | copy-start | bytes 786436
  67.6 6.0 %copy-start.6 = (bf16[4096]{0:T(1024)(128)(2,1)S(1)}, bf16[4096]{0:T(1024)(128)(2,1)}, u32[]{:S(2)}) copy-start(bf16[4096]{0:T(1024)(128)(2,1)} %param.17) | copy-start | bytes 24580
  67.6 32.7 %copy-start.2 = (bf16[64,4096]{1,0:T(8,128)(2,1)S(1)}, bf16[64,4096]{1,0:T(8,128)(2,1)}, u32[]{:S(2)}) copy-start(bf16[64,4096]{1,0:T(8,128)(2,1)} %param.9) | copy-start | bytes 1572868
Sparse Core Ops, SparseCore 0:
  73.5 26.8 reduce-scatter.1
where the time goes:
time: 110 us; the launch traced here: 109 us
  waiting for transfers between devices  47.6 us (43%)
  local copies, waits for them, and re-layouts  18.6 us (17%)
  between operations  14.3 us (13%)
  matrix products  12.1 us (11%)
  other arithmetic  9.03 us (8%)
  starting transfers between devices  7.56 us (7%)
    reduce_scatter x1, waiting for transfers between devices, body(): lax.psum_scatter(jnp.dot(context, out_weight, preferred_element_type=jnp....  25.9 us
    all_to_all x1, waiting for transfers between devices, body(): lax.all_to_all(outgoing, 'dp', split_axis=0, concat_axis=0, tiled=True)  21.7 us
    all_to_all x1, starting transfers between devices, body(): lax.all_to_all(outgoing, 'dp', split_axis=0, concat_axis=0, tiled=True)  7.52 us
    unnamed x26, local copies, waits for them, and re-layouts  6.4 us
    dot_general x1, matrix products, body(): jnp.dot(context, out_weight, preferred_element_type=jnp.float32)  5.7 us
    sub x1, matrix products, body(): lifted = jnp.exp(scores - row_max)  3.93 us
    slice x2, local copies, waits for them, and re-layouts, body(): new_values = new_kv[1].reshape(token_count, local_heads, HD)  3.58 us
    dot_general x1, matrix products, body(): jnp.einsum('hqk,khd->qhd', weights_bf, all_values, preferred_element_type...  2.43 us
  transfers between devices with their start and end apart: 2, of which 2 were waited for; matrix products, arithmetic and copies ran while one was open for 19% of the time, Pallas kernels for 0%

commit v1 on v0

v1 whole, which is shorter than its diff:
```python
import functools
import math

import jax
import jax.numpy as jnp
from jax import lax
from jax.experimental import pallas as pl
from jax.experimental.pallas import tpu as pltpu
from jax.sharding import PartitionSpec as P

HD = 128
ROT = 32
LOWEST = -1e30
VMEM_LIMIT = 48 << 20


def vmem():
    return pl.BlockSpec(memory_space=pltpu.VMEM)


def smem():
    return pl.BlockSpec(memory_space=pltpu.SMEM)


def column_of(row, size):
    rows = lax.broadcasted_iota(jnp.int32, (size, size), 0)
    cols = lax.broadcasted_iota(jnp.int32, (size, size), 1)
    spread = jnp.broadcast_to(row, (size, size))
    return jnp.sum(jnp.where(rows == cols, spread, 0.0), axis=1, keepdims=True)


def rotary_kernel(page, segments_ref, owners_ref, query_ref, kv_ref, rot_query_ref, rot_key_ref):
    tokens, feature = query_ref.shape
    segments = segments_ref[...].astype(jnp.float32)
    column = column_of(segments, tokens)
    earlier = jnp.sum(jnp.where(segments < column, 1.0, 0.0), axis=1, keepdims=True)
    owners = owners_ref[...].astype(jnp.float32)
    cached = jnp.sum(jnp.where(owners == column, 1.0, 0.0), axis=1, keepdims=True)
    number = lax.broadcasted_iota(jnp.int32, (tokens, 1), 0).astype(jnp.float32)
    positions = page * cached + number - earlier
    half = ROT // 2
    lane = lax.broadcasted_iota(jnp.int32, (tokens, HD), 1)
    pair = (lane % half).astype(jnp.float32)
    angles = positions * jnp.exp(-math.log(10000.0) * (2.0 * pair / ROT))
    cosine, sine = jnp.cos(angles), jnp.sin(angles)
    keep = jnp.where(lane < ROT, cosine, 1.0)
    from_above = jnp.where(lane < half, -sine, 0.0)
    from_below = jnp.where((lane >= half) & (lane < ROT), sine, 0.0)
    for start in range(0, feature, HD):
        for source, target in ((query_ref, rot_query_ref), (kv_ref.at[0], rot_key_ref)):
            values = source[:, start : start + HD].astype(jnp.float32)
            turned = (
                values * keep
                + pltpu.roll(values, HD - half, 1) * from_above
                + pltpu.roll(values, half, 1) * from_below
            )
            target[:, start : start + HD] = turned.astype(jnp.bfloat16)


def rotate(page, segment_ids, page_owner, queries, new_kv):
    tokens, feature = queries.shape
    shape = jax.ShapeDtypeStruct((tokens, feature), jnp.bfloat16)
    return pl.pallas_call(
        functools.partial(rotary_kernel, page),
        out_shape=(shape, shape),
        grid=(1,),
        in_specs=[
            pl.BlockSpec(segment_ids.shape, lambda i: (0, 0)),
            pl.BlockSpec(page_owner.shape, lambda i: (0, 0)),
            pl.BlockSpec((tokens, feature), lambda i: (0, 0)),
            pl.BlockSpec((1, tokens, feature), lambda i: (0, 0, 0)),
        ],
        out_specs=(
            pl.BlockSpec((tokens, feature), lambda i: (0, 0)),
            pl.BlockSpec((tokens, feature), lambda i: (0, 0)),
        ),
        cost_estimate=pl.CostEstimate(
            flops=12 * tokens * feature, bytes_accessed=8 * tokens * feature, transcendentals=0
        ),
        name="rotary",
    )(segment_ids, page_owner, queries, new_kv)


def attention_kernel(
    blocks,
    per_peer,
    wanted_ref,
    owner_ref,
    source_ref,
    segments_ref,
    query_ref,
    key_ref,
    value_ref,
    *refs,
):
    block_refs = refs[:blocks]
    out_ref, keys, values = refs[blocks:]
    tokens, feature = query_ref.shape
    page = block_refs[0].shape[2]
    prefix = blocks * per_peer * page
    place = lax.broadcasted_iota(jnp.int32, (1, prefix), 1) // page
    key_owner = jnp.full((1, prefix), -1, jnp.int32)
    for index in range(blocks):
        holder = source_ref[index]
        for slot in range(per_peer):
            piece = index * per_peer + slot
            held = wanted_ref[holder * per_peer + slot]
            keys[pl.ds(piece * page, page), :] = block_refs[index][held, 0]
            values[pl.ds(piece * page, page), :] = block_refs[index][held, 1]
            key_owner = jnp.where(
                place == piece, owner_ref[holder * per_peer + slot], key_owner
            )
    segments = segments_ref[...].astype(jnp.float32)
    column = column_of(segments, tokens)
    rows = lax.broadcasted_iota(jnp.int32, (tokens, tokens), 0)
    cols = lax.broadcasted_iota(jnp.int32, (tokens, tokens), 1)
    see_new = (column == segments) & (cols <= rows)
    see_prefix = column == key_owner.astype(jnp.float32)
    factor = math.log2(math.e) / math.sqrt(HD)
    contract = (((1,), (1,)), ((), ()))
    for start in range(0, feature, HD):
        head = slice(start, start + HD)
        query = query_ref[:, head]
        new = lax.dot_general(
            query, key_ref[:, head], contract, preferred_element_type=jnp.float32
        )
        old = lax.dot_general(query, keys[:, head], contract, preferred_element_type=jnp.float32)
        new = jnp.where(see_new, new * factor, LOWEST)
        old = jnp.where(see_prefix, old * factor, LOWEST)
        top = jnp.maximum(
            jnp.max(new, axis=1, keepdims=True), jnp.max(old, axis=1, keepdims=True)
        )
        new = jnp.exp2(new - top)
        old = jnp.exp2(old - top)
        total = jnp.sum(new, axis=1, keepdims=True) + jnp.sum(old, axis=1, keepdims=True)
        mixed = jnp.dot(
            new.astype(jnp.bfloat16), value_ref[0, :, head], preferred_element_type=jnp.float32
        ) + jnp.dot(
            old.astype(jnp.bfloat16), values[:, head], preferred_element_type=jnp.float32
        )
        out_ref[:, head] = (mixed / total).astype(jnp.bfloat16)


def attend(wanted, owners, sources, segment_ids, rot_query, rot_key, new_kv, blocks, per_peer):
    tokens, feature = rot_query.shape
    prefix = len(blocks) * per_peer * blocks[0].shape[2]
    return pl.pallas_call(
        functools.partial(attention_kernel, len(blocks), per_peer),
        out_shape=jax.ShapeDtypeStruct((tokens, feature), jnp.bfloat16),
        grid=(1,),
        in_specs=[smem()] * 3
        + [vmem()] * 3
        + [pl.BlockSpec((1, tokens, feature), lambda i: (1, 0, 0))]
        + [vmem()] * len(blocks),
        out_specs=vmem(),
        scratch_shapes=[pltpu.VMEM((prefix, feature), jnp.bfloat16)] * 2,
        compiler_params=pltpu.CompilerParams(vmem_limit_bytes=VMEM_LIMIT),
        cost_estimate=pl.CostEstimate(
            flops=4 * tokens * (prefix + tokens) * feature,
            bytes_accessed=8 * prefix * feature,
            transcendentals=0,
        ),
        name="attention",
    )(wanted, owners, sources, segment_ids, rot_query, rot_key, new_kv, *blocks)


def project_kernel(peers, context_ref, weight_ref, own_ref, *send_refs):
    rows = own_ref.shape[0]
    me = lax.axis_index("tensor")
    product = jnp.dot(
        context_ref[...], weight_ref[...], preferred_element_type=jnp.float32
    ).astype(jnp.bfloat16)
    scratch = send_refs[-1]
    scratch[...] = product
    own_ref[...] = scratch[pl.ds(pl.multiple_of(me * rows, rows), rows), :]
    for shift in range(1, peers):
        other = lax.rem(me + shift, peers)
        send_refs[shift - 1][...] = scratch[pl.ds(pl.multiple_of(other * rows, rows), rows), :]


def project(context, out_weight, peers, width):
    tokens, feature = context.shape
    columns = out_weight.shape[1]
    rows = tokens // peers
    shape = jax.ShapeDtypeStruct((rows, columns), jnp.bfloat16)
    spec = pl.BlockSpec((rows, width), lambda i: (0, i))
    return pl.pallas_call(
        functools.partial(project_kernel, peers),
        out_shape=(shape,) * peers,
        grid=(columns // width,),
        in_specs=[vmem(), pl.BlockSpec((feature, width), lambda i: (0, i))],
        out_specs=(spec,) * peers,
        scratch_shapes=[pltpu.VMEM((tokens, width), jnp.bfloat16)],
        compiler_params=pltpu.CompilerParams(vmem_limit_bytes=VMEM_LIMIT),
        cost_estimate=pl.CostEstimate(
            flops=2 * tokens * feature * columns,
            bytes_accessed=2 * feature * columns,
            transcendentals=0,
        ),
        name="project",
    )(context, out_weight)


def body(
    residual, queries, new_kv, kv_pool, fetch_pages, page_owner, segment_ids, out_weight, out_bias
):
    group = lax.axis_index("dp")
    groups = lax.axis_size("dp")
    peers = lax.axis_size("tensor")
    per_peer = fetch_pages.shape[2]
    page = kv_pool.shape[2]
    planes = groups // 4

    def along(values, shift):
        pairs = [(d, (d + 4 * shift) % groups) for d in range(groups)]
        return lax.ppermute(values, "dp", pairs)

    def across(values):
        return lax.ppermute(values, "dp", [(d, d ^ 2) for d in range(groups)])

    def beside(values):
        return lax.ppermute(values, "dp", [(d, d ^ 1) for d in range(groups)])

    found = [(kv_pool, group)]
    up = down = kv_pool
    for step in range(1, planes // 2 + 1):
        up = along(up, 1)
        found.append((up, (group - 4 * step) % groups))
        if 2 * step < planes:
            down = along(down, -1)
            found.append((down, (group + 4 * step) % groups))
    found += [(across(values), holder ^ 2) for values, holder in found]
    found += [(beside(values), holder ^ 1) for values, holder in found]
    blocks = [values for values, _ in found]
    sources = jnp.stack([holder for _, holder in found]).astype(jnp.int32)

    wanted = lax.dynamic_index_in_dim(fetch_pages, group, axis=0, keepdims=False).reshape(-1)
    rot_query, rot_key = rotate(page, segment_ids, page_owner, queries, new_kv)
    context = attend(
        wanted,
        page_owner.reshape(-1),
        sources,
        segment_ids,
        rot_query,
        rot_key,
        new_kv,
        blocks,
        per_peer,
    )
    own, *sends = project(context, out_weight, peers, 512)
    summed = residual.astype(jnp.float32) + own.astype(jnp.float32)
    for shift, values in enumerate(sends, 1):
        pairs = [(t, (t + shift) % peers) for t in range(peers)]
        summed = summed + lax.ppermute(values, "tensor", pairs).astype(jnp.float32)
    hidden = (summed + out_bias.astype(jnp.float32)[None, :]).astype(jnp.bfloat16)
    return (hidden, rot_key)


def solution(mesh):
    return jax.shard_map(
        body,
        mesh=mesh,
        in_specs=(
            P(("dp", "tensor"), None),
            P("dp", "tensor"),
            P(None, "dp", "tensor"),
            P("dp", None, None, "tensor"),
            P(),
            P("dp", None),
            P("dp", None),
            P("tensor", None),
            P(),
        ),
        out_specs=(P(("dp", "tensor"), None), P("dp", "tensor")),
        check_vma=False,
    )
```

time: 110 us -> 67.6 us (0.61)
  the two profiles are of different devices: /device:TPU:0 before, /device:TPU:10 now
where the time goes in v1:
time: 67.6 us; the launch traced here: 67.2 us
  waiting for transfers between devices  31.7 us (47%)
  starting transfers between devices  14.7 us (22%)
  Pallas kernels  13.5 us (20%)
  local copies, waits for them, and re-layouts  5.48 us (8%)
  other arithmetic  1.02 us (2%)
  between operations  0.73 us (1%)
    ppermute x1, waiting for transfers between devices, body(): summed = summed + lax.ppermute(values, 'tensor', pairs).astype(jnp.float32)  13.8 us
    ppermute x4, waiting for transfers between devices, across(): return lax.ppermute(values, 'dp', [(d, d ^ 2) for d in range(groups)])  10.3 us
    ppermute x3, waiting for transfers between devices, along(): return lax.ppermute(values, 'dp', pairs)  7.6 us
    ppermute x3, starting transfers between devices, along(): return lax.ppermute(values, 'dp', pairs)  7.03 us
    pallas_call x1, Pallas kernels, project(): pl.pallas_call(functools.partial(project_kernel, peers), out_shape=(shape...  6.99 us
    ppermute x4, starting transfers between devices, across(): return lax.ppermute(values, 'dp', [(d, d ^ 2) for d in range(groups)])  5.95 us
    unnamed x18, local copies, waits for them, and re-layouts  5.21 us
    pallas_call x1, Pallas kernels, attend(): pl.pallas_call(functools.partial(attention_kernel, len(blocks), per_peer)...  3.87 us
  transfers between devices with their start and end apart: 16, of which 6 were waited for; matrix products, arithmetic and copies ran while one was open for 0% of the time, Pallas kernels for 4%

profile of v1, /device:TPU:10, one launch (start us, length us, event | category | flops | bytes accessed | tf_op | source)
XLA Modules:
  0.0 67.2 jit_solution(8498342094398236751)
XLA Ops:
  0.6 0.0 copy-start
  0.7 1.6 %collective-permute-start = (bf16[4,2,16,1024]{3,2,1,0:T(8,128)(2,1)}, bf16[4,2,16,1024]{3,2,1,0:T(8,128)(2,1)S(1)}, u32[]{:S(2)}, u32[]{:S(2)}) collective-permute-start(bf16[4,2,16,1024]{3,2,1,0:T(8,128)(2,1)} %refs_0_.1), channel_id=1, source_target_pairs={{0,8},{2,10},{4,12},{6,14},{8,16},{10,18},{12,20},{14,22},{16,24},... | collective-permute-start | bytes 786440 | tf_op jit(solution)/shard_map/ppermute | solution.py:216
  2.3 0.4 collective-permute-start.1
  2.7 1.5 %collective-permute-start.3 = (bf16[4,2,16,1024]{3,2,1,0:T(8,128)(2,1)}, bf16[4,2,16,1024]{3,2,1,0:T(8,128)(2,1)S(1)}, u32[]{:S(2)}, u32[]{:S(2)}) collective-permute-start(bf16[4,2,16,1024]{3,2,1,0:T(8,128)(2,1)} %refs_0_.1), channel_id=1, source_target_pairs={{0,4},{2,6},{4,0},{6,2},{8,12},{10,14},{12,8},{14,10},{16,20},{18,... | collective-permute-start | bytes 786440 | tf_op jit(solution)/shard_map/ppermute | solution.py:219
  4.3 5.9 %collective-permute-done.refs_1_ = bf16[4,2,16,1024]{3,2,1,0:T(8,128)(2,1)S(1)} collective-permute-done((bf16[4,2,16,1024]{3,2,1,0:T(8,128)(2,1)}, bf16[4,2,16,1024]{3,2,1,0:T(8,128)(2,1)S(1)}, u32[]{:S(2)}, u32[]{:S(2)}) %collective-permute-start) | collective-permute-done | bytes 262176 | tf_op jit(solution)/shard_map/ppermute | solution.py:216
  10.1 5.0 %collective-permute-start.2 = (bf16[4,2,16,1024]{3,2,1,0:T(8,128)(2,1)S(1)}, bf16[4,2,16,1024]{3,2,1,0:T(8,128)(2,1)S(1)}, u32[]{:S(2)}, u32[]{:S(2)}) collective-permute-start(bf16[4,2,16,1024]{3,2,1,0:T(8,128)(2,1)S(1)} %collective-permute-done.refs_1_), channel_id=1, source_target_pairs={{0,8},{2,10},{4,12},{6,14},{8,16},{10,18},{12,20},{14,22},{16,24},... | collective-permute-start | bytes 786440 | tf_op jit(solution)/shard_map/ppermute | solution.py:216
  15.1 1.5 %collective-permute-start.4 = (bf16[4,2,16,1024]{3,2,1,0:T(8,128)(2,1)S(1)}, bf16[4,2,16,1024]{3,2,1,0:T(8,128)(2,1)S(1)}, u32[]{:S(2)}, u32[]{:S(2)}) collective-permute-start(bf16[4,2,16,1024]{3,2,1,0:T(8,128)(2,1)S(1)} %collective-permute-done.refs_1_), channel_id=1, source_target_pairs={{0,4},{2,6},{4,0},{6,2},{8,12},{10,14},{12,8},{14,10},{16,20},{18,... | collective-permute-start | bytes 786440 | tf_op jit(solution)/shard_map/ppermute | solution.py:219
  16.6 1.4 %collective-permute-start.5 = (bf16[4,2,16,1024]{3,2,1,0:T(8,128)(2,1)S(1)}, bf16[4,2,16,1024]{3,2,1,0:T(8,128)(2,1)S(1)}, u32[]{:S(2)}, u32[]{:S(2)}) collective-permute-start(bf16[4,2,16,1024]{3,2,1,0:T(8,128)(2,1)S(1)} %collective-permute-done.1.refs_2_), channel_id=1, source_target_pairs={{0,4},{2,6},{4,0},{6,2},{8,12},{10,14},{12,8},{14,10},{16,20},{18,... | collective-permute-start | bytes 786440 | tf_op jit(solution)/shard_map/ppermute | solution.py:219
  18.0 0.5 collective-permute-start.9
  18.5 1.7 %collective-permute-done.2.refs_3_ = bf16[4,2,16,1024]{3,2,1,0:T(8,128)(2,1)S(1)} collective-permute-done((bf16[4,2,16,1024]{3,2,1,0:T(8,128)(2,1)S(1)}, bf16[4,2,16,1024]{3,2,1,0:T(8,128)(2,1)S(1)}, u32[]{:S(2)}, u32[]{:S(2)}) %collective-permute-start.2) | collective-permute-done | bytes 262176 | tf_op jit(solution)/shard_map/ppermute | solution.py:216
  20.2 1.5 %collective-permute-start.6 = (bf16[4,2,16,1024]{3,2,1,0:T(8,128)(2,1)S(1)}, bf16[4,2,16,1024]{3,2,1,0:T(8,128)(2,1)S(1)}, u32[]{:S(2)}, u32[]{:S(2)}) collective-permute-start(bf16[4,2,16,1024]{3,2,1,0:T(8,128)(2,1)S(1)} %collective-permute-done.2.refs_3_), channel_id=1, source_target_pairs={{0,4},{2,6},{4,0},{6,2},{8,12},{10,14},{12,8},{14,10},{16,20},{18,... | collective-permute-start | bytes 786440 | tf_op jit(solution)/shard_map/ppermute | solution.py:219
  21.8 2.1 %collective-permute-done.4.refs_5_ = bf16[4,2,16,1024]{3,2,1,0:T(8,128)(2,1)S(1)} collective-permute-done((bf16[4,2,16,1024]{3,2,1,0:T(8,128)(2,1)S(1)}, bf16[4,2,16,1024]{3,2,1,0:T(8,128)(2,1)S(1)}, u32[]{:S(2)}, u32[]{:S(2)}) %collective-permute-start.4) | collective-permute-done | bytes 262176 | tf_op jit(solution)/shard_map/ppermute | solution.py:219
  23.9 5.6 %collective-permute-done.5.refs_6_ = bf16[4,2,16,1024]{3,2,1,0:T(8,128)(2,1)S(1)} collective-permute-done((bf16[4,2,16,1024]{3,2,1,0:T(8,128)(2,1)S(1)}, bf16[4,2,16,1024]{3,2,1,0:T(8,128)(2,1)S(1)}, u32[]{:S(2)}, u32[]{:S(2)}) %collective-permute-start.5) | collective-permute-done | bytes 262176 | tf_op jit(solution)/shard_map/ppermute | solution.py:219
  29.5 0.5 collective-permute-start.12
  30.0 0.1 collective-permute-start.13
  30.1 2.6 %collective-permute-done.6.refs_7_ = bf16[4,2,16,1024]{3,2,1,0:T(8,128)(2,1)S(1)} collective-permute-done((bf16[4,2,16,1024]{3,2,1,0:T(8,128)(2,1)S(1)}, bf16[4,2,16,1024]{3,2,1,0:T(8,128)(2,1)S(1)}, u32[]{:S(2)}, u32[]{:S(2)}) %collective-permute-start.6) | collective-permute-done | bytes 262176 | tf_op jit(solution)/shard_map/ppermute | solution.py:219
  32.7 0.1 copy.12
  32.8 0.1 reshape.12.wanted_ref
  32.9 0.1 stack.67.source_ref
  33.0 2.6 %rotary.1 = (bf16[128,1024]{1,0:T(8,128)(2,1)}, bf16[128,1024]{1,0:T(8,128)(2,1)}) custom-call(s32[1,128]{1,0:T(1,128)} %segments_ref.3, s32[1,32]{1,0:T(1,128)} %owners_ref.1, bf16[128,1024]{1,0:T(8,128)(2,1)} %query_ref.1, bf16[2,128,1024]{2,1,0:T(8,128)(2,1)} %value_ref.1), custom_call_target="tpu_custom_call" | custom-call | flops 1572864 | bytes 1048576 | tf_op jit(solution)/shard_map/rotary/pallas_call | solution.py:63
  35.6 0.0 copy-start.1
  35.7 1.0 %copy-done.1 = bf16[2,128,1024]{2,1,0:T(8,128)(2,1)S(1)} copy-done((bf16[2,128,1024]{2,1,0:T(8,128)(2,1)S(1)}, bf16[2,128,1024]{2,1,0:T(8,128)(2,1)}, u32[]{:S(2)}) %copy-start.1) | copy-done | bytes 524312
  36.7 0.9 %copy-done.2 = bf16[4,2,16,1024]{3,2,1,0:T(8,128)(2,1)S(1)} copy-done((bf16[4,2,16,1024]{3,2,1,0:T(8,128)(2,1)S(1)}, bf16[4,2,16,1024]{3,2,1,0:T(8,128)(2,1)}, u32[]{:S(2)}) %copy-start.2) | copy-done | bytes 262168
  37.6 0.9 %copy-done.3 = bf16[128,1024]{1,0:T(8,128)(2,1)S(1)} copy-done((bf16[128,1024]{1,0:T(8,128)(2,1)S(1)}, bf16[128,1024]{1,0:T(8,128)(2,1)}, u32[]{:S(2)}) %copy-start.3) | copy-done | bytes 262168
  38.6 0.9 %copy-done.4 = bf16[128,1024]{1,0:T(8,128)(2,1)S(1)} copy-done((bf16[128,1024]{1,0:T(8,128)(2,1)S(1)}, bf16[128,1024]{1,0:T(8,128)(2,1)}, u32[]{:S(2)}) %copy-start.4) | copy-done | bytes 262168
  39.5 0.7 copy-done.5
  40.2 0.7 copy-done.6
  40.9 3.9 %attention.1.context_ref = bf16[128,1024]{1,0:T(8,128)(2,1)S(1)} custom-call(s32[32]{0:T(128)S(1)} %reshape.12.wanted_ref, s32[32]{0:T(128)S(1)} %bitcast.17, s32[16]{0:T(128)S(1)} %stack.67.source_ref, s32[1,128]{1,0:T(1,128)S(1)} %copy-done.6, bf16[128,1024]{1,0:T(8,128)(2,1)S(1)} %copy-done.4, bf16[128,1024]{1,0:T(8,128)(2,1)S(1)} %copy-done.3, ...), custom_call_target="tpu_custom_call" | custom-call | flops 335544320 | bytes 4194304 | tf_op jit(solution)/shard_map/attention/pallas_call | solution.py:147
  44.7 7.0 %project.1 = (bf16[64,4096]{1,0:T(8,128)(2,1)S(1)}, bf16[64,4096]{1,0:T(8,128)(2,1)S(1)}) custom-call(bf16[128,1024]{1,0:T(8,128)(2,1)S(1)} %attention.1.context_ref, bf16[1024,4096]{1,0:T(8,128)(2,1)} %weight_ref.1), custom_call_target="tpu_custom_call" | custom-call | flops 1073741824 | bytes 8388608 | tf_op jit(solution)/shard_map/project/pallas_call | solution.py:187
  51.7 0.6 collective-permute-start.15
  52.3 13.8 %collective-permute-done.15 = bf16[64,4096]{1,0:T(8,128)(2,1)S(1)} collective-permute-done((bf16[64,4096]{1,0:T(8,128)(2,1)S(1)}, bf16[64,4096]{1,0:T(8,128)(2,1)S(1)}, u32[]{:S(2)}, u32[]{:S(2)}) %collective-permute-start.15) | collective-permute-done | bytes 524320 | tf_op jit(solution)/shard_map/ppermute | solution.py:254
  66.1 1.0 %add_convert_fusion = bf16[64,4096]{1,0:T(8,128)(2,1)} fusion(bf16[64,4096]{1,0:T(8,128)(2,1)S(1)} %collective-permute-done.15, bf16[64,4096]{1,0:T(8,128)(2,1)S(1)} %get-tuple-element.8, bf16[64,4096]{1,0:T(8,128)(2,1)S(1)} %copy-done.7, f32[4096]{0:T(1024)S(1)} %convert_element_type.18), kind=kLoop, calls=%fused_computation | loop fusion | flops 1835008 | bytes 2113536 | tf_op jit(solution)/shard_map/convert_element_type | solution.py:255
  (27 shorter events, 0.1 us)
Async XLA Ops:
  0.6 32.0 %copy-start = (s32[16,16,2]{1,2,0:T(2,128)S(1)}, s32[16,16,2]{1,2,0:T(2,128)}, u32[]{:S(2)}) copy-start(s32[16,16,2]{1,2,0:T(2,128)} %param.13) | copy-start | bytes 6148
  0.6 51.7 %copy-start.8 = (bf16[4096]{0:T(1024)(128)(2,1)S(1)}, bf16[4096]{0:T(1024)(128)(2,1)}, u32[]{:S(2)}) copy-start(bf16[4096]{0:T(1024)(128)(2,1)} %param.17) | copy-start | bytes 24580
  0.7 9.5 %collective-permute-start = (bf16[4,2,16,1024]{3,2,1,0:T(8,128)(2,1)}, bf16[4,2,16,1024]{3,2,1,0:T(8,128)(2,1)S(1)}, u32[]{:S(2)}, u32[]{:S(2)}) collective-permute-start(bf16[4,2,16,1024]{3,2,1,0:T(8,128)(2,1)} %refs_0_.1), channel_id=1, source_target_pairs={{0,8},{2,10},{4,12},{6,14},{8,16},{10,18},{12,20},{14,22},{16,24},... | collective-permute-start | bytes 786440 | tf_op jit(solution)/shard_map/ppermute | solution.py:216
  2.3 14.3 %collective-permute-start.1 = (bf16[4,2,16,1024]{3,2,1,0:T(8,128)(2,1)}, bf16[4,2,16,1024]{3,2,1,0:T(8,128)(2,1)S(1)}, u32[]{:S(2)}, u32[]{:S(2)}) collective-permute-start(bf16[4,2,16,1024]{3,2,1,0:T(8,128)(2,1)} %refs_0_.1), channel_id=1, source_target_pairs={{0,24},{2,26},{4,28},{6,30},{8,0},{10,2},{12,4},{14,6},{16,8},{18,... | collective-permute-start | bytes 786440 | tf_op jit(solution)/shard_map/ppermute | solution.py:216
  2.7 15.2 %collective-permute-start.3 = (bf16[4,2,16,1024]{3,2,1,0:T(8,128)(2,1)}, bf16[4,2,16,1024]{3,2,1,0:T(8,128)(2,1)S(1)}, u32[]{:S(2)}, u32[]{:S(2)}) collective-permute-start(bf16[4,2,16,1024]{3,2,1,0:T(8,128)(2,1)} %refs_0_.1), channel_id=1, source_target_pairs={{0,4},{2,6},{4,0},{6,2},{8,12},{10,14},{12,8},{14,10},{16,20},{18,... | collective-permute-start | bytes 786440 | tf_op jit(solution)/shard_map/ppermute | solution.py:219
  4.3 13.7 %collective-permute-start.7 = (bf16[4,2,16,1024]{3,2,1,0:T(8,128)(2,1)}, bf16[4,2,16,1024]{3,2,1,0:T(8,128)(2,1)S(1)}, u32[]{:S(2)}, u32[]{:S(2)}) collective-permute-start(bf16[4,2,16,1024]{3,2,1,0:T(8,128)(2,1)} %refs_0_.1), channel_id=1, source_target_pairs={{0,2},{2,0},{4,6},{6,4},{8,10},{10,8},{12,14},{14,12},{16,18},{18,... | collective-permute-start | bytes 786440 | tf_op jit(solution)/shard_map/ppermute | solution.py:222
  10.1 10.1 %collective-permute-start.2 = (bf16[4,2,16,1024]{3,2,1,0:T(8,128)(2,1)S(1)}, bf16[4,2,16,1024]{3,2,1,0:T(8,128)(2,1)S(1)}, u32[]{:S(2)}, u32[]{:S(2)}) collective-permute-start(bf16[4,2,16,1024]{3,2,1,0:T(8,128)(2,1)S(1)} %collective-permute-done.refs_1_), channel_id=1, source_target_pairs={{0,8},{2,10},{4,12},{6,14},{8,16},{10,18},{12,20},{14,22},{16,24},... | collective-permute-start | bytes 786440 | tf_op jit(solution)/shard_map/ppermute | solution.py:216
  15.1 8.8 %collective-permute-start.4 = (bf16[4,2,16,1024]{3,2,1,0:T(8,128)(2,1)S(1)}, bf16[4,2,16,1024]{3,2,1,0:T(8,128)(2,1)S(1)}, u32[]{:S(2)}, u32[]{:S(2)}) collective-permute-start(bf16[4,2,16,1024]{3,2,1,0:T(8,128)(2,1)S(1)} %collective-permute-done.refs_1_), channel_id=1, source_target_pairs={{0,4},{2,6},{4,0},{6,2},{8,12},{10,14},{12,8},{14,10},{16,20},{18,... | collective-permute-start | bytes 786440 | tf_op jit(solution)/shard_map/ppermute | solution.py:219
  16.6 12.9 %collective-permute-start.5 = (bf16[4,2,16,1024]{3,2,1,0:T(8,128)(2,1)S(1)}, bf16[4,2,16,1024]{3,2,1,0:T(8,128)(2,1)S(1)}, u32[]{:S(2)}, u32[]{:S(2)}) collective-permute-start(bf16[4,2,16,1024]{3,2,1,0:T(8,128)(2,1)S(1)} %collective-permute-done.1.refs_2_), channel_id=1, source_target_pairs={{0,4},{2,6},{4,0},{6,2},{8,12},{10,14},{12,8},{14,10},{16,20},{18,... | collective-permute-start | bytes 786440 | tf_op jit(solution)/shard_map/ppermute | solution.py:219
  18.0 11.5 %collective-permute-start.8 = (bf16[4,2,16,1024]{3,2,1,0:T(8,128)(2,1)S(1)}, bf16[4,2,16,1024]{3,2,1,0:T(8,128)(2,1)S(1)}, u32[]{:S(2)}, u32[]{:S(2)}) collective-permute-start(bf16[4,2,16,1024]{3,2,1,0:T(8,128)(2,1)S(1)} %collective-permute-done.refs_1_), channel_id=1, source_target_pairs={{0,2},{2,0},{4,6},{6,4},{8,10},{10,8},{12,14},{14,12},{16,18},{18,... | collective-permute-start | bytes 786440 | tf_op jit(solution)/shard_map/ppermute | solution.py:222
  18.0 12.0 %collective-permute-start.9 = (bf16[4,2,16,1024]{3,2,1,0:T(8,128)(2,1)S(1)}, bf16[4,2,16,1024]{3,2,1,0:T(8,128)(2,1)S(1)}, u32[]{:S(2)}, u32[]{:S(2)}) collective-permute-start(bf16[4,2,16,1024]{3,2,1,0:T(8,128)(2,1)S(1)} %collective-permute-done.1.refs_2_), channel_id=1, source_target_pairs={{0,2},{2,0},{4,6},{6,4},{8,10},{10,8},{12,14},{14,12},{16,18},{18,... | collective-permute-start | bytes 786440 | tf_op jit(solution)/shard_map/ppermute | solution.py:222
  20.2 12.4 %collective-permute-start.6 = (bf16[4,2,16,1024]{3,2,1,0:T(8,128)(2,1)S(1)}, bf16[4,2,16,1024]{3,2,1,0:T(8,128)(2,1)S(1)}, u32[]{:S(2)}, u32[]{:S(2)}) collective-permute-start(bf16[4,2,16,1024]{3,2,1,0:T(8,128)(2,1)S(1)} %collective-permute-done.2.refs_3_), channel_id=1, source_target_pairs={{0,4},{2,6},{4,0},{6,2},{8,12},{10,14},{12,8},{14,10},{16,20},{18,... | collective-permute-start | bytes 786440 | tf_op jit(solution)/shard_map/ppermute | solution.py:219
  23.9 11.7 %collective-permute-start.11 = (bf16[4,2,16,1024]{3,2,1,0:T(8,128)(2,1)S(1)}, bf16[4,2,16,1024]{3,2,1,0:T(8,128)(2,1)S(1)}, u32[]{:S(2)}, u32[]{:S(2)}) collective-permute-start(bf16[4,2,16,1024]{3,2,1,0:T(8,128)(2,1)S(1)} %collective-permute-done.3.refs_4_), channel_id=1, source_target_pairs={{0,2},{2,0},{4,6},{6,4},{8,10},{10,8},{12,14},{14,12},{16,18},{18,... | collective-permute-start | bytes 786440 | tf_op jit(solution)/shard_map/ppermute | solution.py:222
  29.5 6.1 %collective-permute-start.10 = (bf16[4,2,16,1024]{3,2,1,0:T(8,128)(2,1)S(1)}, bf16[4,2,16,1024]{3,2,1,0:T(8,128)(2,1)S(1)}, u32[]{:S(2)}, u32[]{:S(2)}) collective-permute-start(bf16[4,2,16,1024]{3,2,1,0:T(8,128)(2,1)S(1)} %collective-permute-done.2.refs_3_), channel_id=1, source_target_pairs={{0,2},{2,0},{4,6},{6,4},{8,10},{10,8},{12,14},{14,12},{16,18},{18,... | collective-permute-start | bytes 786440 | tf_op jit(solution)/shard_map/ppermute | solution.py:222
  29.5 6.1 %collective-permute-start.12 = (bf16[4,2,16,1024]{3,2,1,0:T(8,128)(2,1)S(1)}, bf16[4,2,16,1024]{3,2,1,0:T(8,128)(2,1)S(1)}, u32[]{:S(2)}, u32[]{:S(2)}) collective-permute-start(bf16[4,2,16,1024]{3,2,1,0:T(8,128)(2,1)S(1)} %collective-permute-done.4.refs_5_), channel_id=1, source_target_pairs={{0,2},{2,0},{4,6},{6,4},{8,10},{10,8},{12,14},{14,12},{16,18},{18,... | collective-permute-start | bytes 786440 | tf_op jit(solution)/shard_map/ppermute | solution.py:222
  30.0 5.6 %collective-permute-start.13 = (bf16[4,2,16,1024]{3,2,1,0:T(8,128)(2,1)S(1)}, bf16[4,2,16,1024]{3,2,1,0:T(8,128)(2,1)}, u32[]{:S(2)}, u32[]{:S(2)}) collective-permute-start(bf16[4,2,16,1024]{3,2,1,0:T(8,128)(2,1)S(1)} %collective-permute-done.5.refs_6_), channel_id=1, source_target_pairs={{0,2},{2,0},{4,6},{6,4},{8,10},{10,8},{12,14},{14,12},{16,18},{18,... | collective-permute-start | bytes 786440 | tf_op jit(solution)/shard_map/ppermute | solution.py:222
  32.7 3.0 %collective-permute-start.14 = (bf16[4,2,16,1024]{3,2,1,0:T(8,128)(2,1)S(1)}, bf16[4,2,16,1024]{3,2,1,0:T(8,128)(2,1)}, u32[]{:S(2)}, u32[]{:S(2)}) collective-permute-start(bf16[4,2,16,1024]{3,2,1,0:T(8,128)(2,1)S(1)} %collective-permute-done.6.refs_7_), channel_id=1, source_target_pairs={{0,2},{2,0},{4,6},{6,4},{8,10},{10,8},{12,14},{14,12},{16,18},{18,... | collective-permute-start | bytes 786440 | tf_op jit(solution)/shard_map/ppermute | solution.py:222
  35.6 1.0 %copy-start.1 = (bf16[2,128,1024]{2,1,0:T(8,128)(2,1)S(1)}, bf16[2,128,1024]{2,1,0:T(8,128)(2,1)}, u32[]{:S(2)}) copy-start(bf16[2,128,1024]{2,1,0:T(8,128)(2,1)} %value_ref.1) | copy-start | bytes 1572868
  36.7 0.9 %copy-start.2 = (bf16[4,2,16,1024]{3,2,1,0:T(8,128)(2,1)S(1)}, bf16[4,2,16,1024]{3,2,1,0:T(8,128)(2,1)}, u32[]{:S(2)}) copy-start(bf16[4,2,16,1024]{3,2,1,0:T(8,128)(2,1)} %refs_0_.1) | copy-start | bytes 786436
  37.6 0.9 %copy-start.3 = (bf16[128,1024]{1,0:T(8,128)(2,1)S(1)}, bf16[128,1024]{1,0:T(8,128)(2,1)}, u32[]{:S(2)}) copy-start(bf16[128,1024]{1,0:T(8,128)(2,1)} %get-tuple-element.5.key_ref) | copy-start | bytes 786436
  38.6 0.9 %copy-start.4 = (bf16[128,1024]{1,0:T(8,128)(2,1)S(1)}, bf16[128,1024]{1,0:T(8,128)(2,1)}, u32[]{:S(2)}) copy-start(bf16[128,1024]{1,0:T(8,128)(2,1)} %get-tuple-element.6.query_ref) | copy-start | bytes 786436
  39.5 0.7 copy-start.5
  40.2 0.7 copy-start.6
  40.9 25.3 %copy-start.7 = (bf16[64,4096]{1,0:T(8,128)(2,1)S(1)}, bf16[64,4096]{1,0:T(8,128)(2,1)}, u32[]{:S(2)}) copy-start(bf16[64,4096]{1,0:T(8,128)(2,1)} %param.9) | copy-start | bytes 1572868
  51.7 14.4 %collective-permute-start.15 = (bf16[64,4096]{1,0:T(8,128)(2,1)S(1)}, bf16[64,4096]{1,0:T(8,128)(2,1)S(1)}, u32[]{:S(2)}, u32[]{:S(2)}) collective-permute-start(bf16[64,4096]{1,0:T(8,128)(2,1)S(1)} %get-tuple-element.9), channel_id=1, source_target_pairs={{0,1},{1,0},{2,3},{3,2},{4,5},{5,4},{6,7},{7,6},{8,9},{9,8},{10,11... | collective-permute-start | bytes 1572872 | tf_op jit(solution)/shard_map/ppermute | solution.py:254

commit v2 on v1

v2 whole, which is shorter than its diff:
```python
import functools
import math

import jax
import jax.numpy as jnp
from jax import lax
from jax.experimental import pallas as pl
from jax.experimental.pallas import tpu as pltpu
from jax.sharding import PartitionSpec as P

HD = 128
ROT = 32
LOWEST = -1e30
VMEM_LIMIT = 24 << 20
LATE_LIMIT = 24 << 20
ROTARY_LIMIT = 60 << 20


def vmem():
    return pl.BlockSpec(memory_space=pltpu.VMEM)


def smem():
    return pl.BlockSpec(memory_space=pltpu.SMEM)


def column_of(row, size):
    rows = lax.broadcasted_iota(jnp.int32, (size, size), 0)
    cols = lax.broadcasted_iota(jnp.int32, (size, size), 1)
    spread = jnp.broadcast_to(row, (size, size))
    return jnp.sum(jnp.where(rows == cols, spread, 0.0), axis=1, keepdims=True)


def rotary_kernel(
    page,
    segments_ref,
    owners_ref,
    query_ref,
    kv_ref,
    all_kv_ref,
    pool_ref,
    column_ref,
    rot_query_ref,
    rot_key_ref,
    value_ref,
    held_ref,
    cache_ref,
    done,
):
    copies = [
        pltpu.make_async_copy(all_kv_ref.at[1], value_ref, done.at[0]),
        pltpu.make_async_copy(pool_ref, held_ref, done.at[1]),
    ]
    for copy in copies:
        copy.start()
    tokens, feature = query_ref.shape
    segments = segments_ref[...].astype(jnp.float32)
    column = column_of(segments, tokens)
    column_ref[...] = jnp.broadcast_to(column, column_ref.shape)
    earlier = jnp.sum(jnp.where(segments < column, 1.0, 0.0), axis=1, keepdims=True)
    owners = owners_ref[...].astype(jnp.float32)
    cached = jnp.sum(jnp.where(owners == column, 1.0, 0.0), axis=1, keepdims=True)
    number = lax.broadcasted_iota(jnp.int32, (tokens, 1), 0).astype(jnp.float32)
    positions = page * cached + number - earlier
    half = ROT // 2
    lane = lax.broadcasted_iota(jnp.int32, (tokens, HD), 1)
    pair = (lane % half).astype(jnp.float32)
    angles = positions * jnp.exp(-math.log(10000.0) * (2.0 * pair / ROT))
    cosine, sine = jnp.cos(angles), jnp.sin(angles)
    keep = jnp.where(lane < ROT, cosine, 1.0)
    from_above = jnp.where(lane < half, -sine, 0.0)
    from_below = jnp.where((lane >= half) & (lane < ROT), sine, 0.0)
    for start in range(0, feature, HD):
        for source, target in ((kv_ref.at[0], rot_key_ref), (query_ref, rot_query_ref)):
            values = source[:, start : start + HD].astype(jnp.float32)
            turned = (
                values * keep
                + pltpu.roll(values, HD - half, 1) * from_above
                + pltpu.roll(values, half, 1) * from_below
            )
            target[:, start : start + HD] = turned.astype(jnp.bfloat16)
    copies.append(pltpu.make_async_copy(rot_key_ref, cache_ref, done.at[2]))
    copies[-1].start()
    for copy in copies:
        copy.wait()


def anywhere():
    return pl.BlockSpec(memory_space=pltpu.HBM)


def cheap():
    return pl.CostEstimate(flops=1, bytes_accessed=1, transcendentals=0)


def rotate(page, segment_ids, page_owner, queries, new_kv, kv_pool):
    tokens, feature = queries.shape
    shape = jax.ShapeDtypeStruct((tokens, feature), jnp.bfloat16)
    return pl.pallas_call(
        functools.partial(rotary_kernel, page),
        out_shape=(
            jax.ShapeDtypeStruct((tokens, HD), jnp.float32),
            shape,
            shape,
            shape,
            jax.ShapeDtypeStruct(kv_pool.shape, jnp.bfloat16),
            shape,
        ),
        grid=(1,),
        in_specs=[
            pl.BlockSpec(segment_ids.shape, lambda i: (0, 0)),
            pl.BlockSpec(page_owner.shape, lambda i: (0, 0)),
            pl.BlockSpec((tokens, feature), lambda i: (0, 0)),
            pl.BlockSpec((1, tokens, feature), lambda i: (0, 0, 0)),
            anywhere(),
            anywhere(),
        ],
        out_specs=(vmem(),) * 5 + (anywhere(),),
        scratch_shapes=[pltpu.SemaphoreType.DMA((3,))],
        compiler_params=params(ROTARY_LIMIT),
        cost_estimate=cheap(),
        name="rotary",
    )(segment_ids, page_owner, queries, new_kv, new_kv, kv_pool)


def stage_kernel(source_ref, target_ref, done):
    pieces = done.shape[0]
    rows = source_ref.shape[0] // pieces
    copies = []
    for piece in range(pieces):
        part = pl.ds(piece * rows, rows)
        copies.append(
            pltpu.make_async_copy(source_ref.at[part], target_ref.at[part], done.at[piece])
        )
        copies[-1].start()
    for copy in copies:
        copy.wait()


def stage(values):
    return pl.pallas_call(
        stage_kernel,
        out_shape=jax.ShapeDtypeStruct(values.shape, values.dtype),
        in_specs=[pl.BlockSpec(memory_space=pl.ANY)],
        out_specs=vmem(),
        scratch_shapes=[pltpu.SemaphoreType.DMA((8,))],
        compiler_params=params(),
        cost_estimate=cheap(),
        name="stage",
    )(values)


def gather_pages(blocks, refs, per_peer, table_ref, keys, values):
    group = lax.axis_index("dp")
    groups = lax.axis_size("dp")
    page = refs[0].shape[2]
    length = len(blocks) * per_peer * page
    place = lax.broadcasted_iota(jnp.int32, (1, length), 1) // page
    key_owner = jnp.full((1, length), -1, jnp.int32)
    used = 0
    for index, (shift, flip, cuts) in enumerate(blocks):
        holder = lax.rem(group + (4 * shift) % groups, groups) ^ flip
        parts = refs[used : used + len(cuts)]
        used += len(cuts)
        for slot in range(per_peer):
            piece = index * per_peer + slot
            held = table_ref[holder * per_peer + slot]
            rows = pl.ds(piece * page, page)
            for part, low in zip(parts, cuts):
                count = part.shape[0]

                def take(part=part, low=low, count=count):
                    at = jnp.clip(held - low, 0, count - 1)
                    keys[rows, :] = part[at, 0]
                    values[rows, :] = part[at, 1]

                if len(cuts) == 1:
                    take()
                else:
                    pl.when((held >= low) & (held < low + count))(take)
            key_owner = jnp.where(
                place == piece, table_ref[(groups + holder) * per_peer + slot], key_owner
            )
    return key_owner.astype(jnp.float32)


FACTOR = math.log2(math.e) / math.sqrt(HD)
CONTRACT = (((1,), (1,)), ((), ()))


def scores_of(query, keys, seen):
    scores = lax.dot_general(query, keys, CONTRACT, preferred_element_type=jnp.float32)
    return jnp.where(seen, scores * FACTOR, LOWEST)


def weigh(weights, values):
    return jnp.dot(weights.astype(jnp.bfloat16), values, preferred_element_type=jnp.float32)


def early_kernel(
    blocks, per_peer, table_ref, segments_ref, column_ref, query_ref, key_ref, value_ref, *refs
):
    *block_refs, mixed_ref, stats_ref, keys, values = refs
    tokens, feature = query_ref.shape
    key_owner = gather_pages(blocks, block_refs, per_peer, table_ref, keys, values)
    segments = segments_ref[...].astype(jnp.float32)
    column = column_ref[:, :1]
    rows = lax.broadcasted_iota(jnp.int32, (tokens, tokens), 0)
    cols = lax.broadcasted_iota(jnp.int32, (tokens, tokens), 1)
    see_new = (column == segments) & (cols <= rows)
    see_old = column == key_owner
    lane = lax.broadcasted_iota(jnp.int32, (tokens, HD), 1)
    tops = totals = jnp.zeros((tokens, HD), jnp.float32)
    for number, start in enumerate(range(0, feature, HD)):
        head = slice(start, start + HD)
        query = query_ref[:, head]
        new = scores_of(query, key_ref[:, head], see_new)
        old = scores_of(query, keys[:, head], see_old)
        top = jnp.maximum(
            jnp.max(new, axis=1, keepdims=True), jnp.max(old, axis=1, keepdims=True)
        )
        new = jnp.exp2(new - top)
        old = jnp.exp2(old - top)
        total = jnp.sum(new, axis=1, keepdims=True) + jnp.sum(old, axis=1, keepdims=True)
        mixed_ref[:, head] = weigh(new, value_ref[:, head]) + weigh(old, values[:, head])
        tops = jnp.where(lane == number, top, tops)
        totals = jnp.where(lane == number, total, totals)
    stats_ref[:, :HD] = tops
    stats_ref[:, HD:] = totals


def late_kernel(
    blocks,
    per_peer,
    peers,
    table_ref,
    column_ref,
    query_ref,
    mixed_ref,
    stats_ref,
    weight_ref,
    *refs,
):
    count = sum(len(cuts) for _, _, cuts in blocks)
    block_refs = refs[:count]
    own_ref, *send_refs = refs[count : count + peers]
    keys, values, context_ref, product = refs[count + peers :]
    tokens, feature = query_ref.shape
    key_owner = gather_pages(blocks, block_refs, per_peer, table_ref, keys, values)
    seen = column_ref[:, :1] == key_owner
    for number, start in enumerate(range(0, feature, HD)):
        head = slice(start, start + HD)
        scores = scores_of(query_ref[:, head], keys[:, head], seen)
        before = stats_ref[:, number : number + 1]
        top = jnp.maximum(before, jnp.max(scores, axis=1, keepdims=True))
        weights = jnp.exp2(scores - top)
        fade = jnp.exp2(before - top)
        total = stats_ref[:, HD + number : HD + number + 1] * fade + jnp.sum(
            weights, axis=1, keepdims=True
        )
        mixed = mixed_ref[:, head] * fade + weigh(weights, values[:, head])
        context_ref[:, head] = (mixed / total).astype(jnp.bfloat16)
    project_rows(peers, context_ref, weight_ref, product, own_ref, send_refs)


def project_rows(peers, context_ref, weight_ref, product, own_ref, send_refs):
    rows, width = own_ref.shape
    me = lax.axis_index("tensor")
    step = min(512, width)
    for start in range(0, width, step):
        product[:, start : start + step] = jnp.dot(
            context_ref[...],
            weight_ref[:, start : start + step],
            preferred_element_type=jnp.float32,
        ).astype(jnp.bfloat16)
    own_ref[...] = product[pl.ds(pl.multiple_of(me * rows, rows), rows), :]
    for shift in range(1, peers):
        other = lax.rem(me + shift, peers)
        send_refs[shift - 1][...] = product[pl.ds(pl.multiple_of(other * rows, rows), rows), :]


def shares(tokens, peers, width):
    return (jax.ShapeDtypeStruct((tokens // peers, width), jnp.bfloat16),) * peers


def params(limit=VMEM_LIMIT):
    return pltpu.CompilerParams(vmem_limit_bytes=limit)


def attend_early(layout, table, segment_ids, column, rot_query, rot_key, value, parts, per_peer):
    tokens, feature = rot_query.shape
    prefix = len(layout) * per_peer * parts[0].shape[2]
    return pl.pallas_call(
        functools.partial(early_kernel, layout, per_peer),
        out_shape=(
            jax.ShapeDtypeStruct((tokens, feature), jnp.float32),
            jax.ShapeDtypeStruct((tokens, 2 * HD), jnp.float32),
        ),
        grid=(1,),
        in_specs=[smem()] + [vmem()] * (5 + len(parts)),
        out_specs=(vmem(), vmem()),
        scratch_shapes=[pltpu.VMEM((prefix, feature), jnp.bfloat16)] * 2,
        compiler_params=params(),
        cost_estimate=cheap(),
        name="early",
    )(table, segment_ids, column, rot_query, rot_key, value, *parts)


def attend_late(
    layout, table, column, rot_query, mixed, stats, weight, parts, per_peer, peers
):
    tokens, feature = rot_query.shape
    prefix = len(layout) * per_peer * parts[0].shape[2]
    return pl.pallas_call(
        functools.partial(late_kernel, layout, per_peer, peers),
        out_shape=shares(tokens, peers, weight.shape[1]),
        grid=(1,),
        in_specs=[smem()] + [vmem()] * (5 + len(parts)),
        out_specs=(vmem(),) * peers,
        scratch_shapes=[pltpu.VMEM((prefix, feature), jnp.bfloat16)] * 2
        + [
            pltpu.VMEM((tokens, feature), jnp.bfloat16),
            pltpu.VMEM((tokens, weight.shape[1]), jnp.bfloat16),
        ],
        compiler_params=params(LATE_LIMIT),
        cost_estimate=cheap(),
        name="late",
    )(table, column, rot_query, mixed, stats, weight, *parts)


def body(
    residual, queries, new_kv, kv_pool, fetch_pages, page_owner, segment_ids, out_weight, out_bias
):
    group = lax.axis_index("dp")
    groups = lax.axis_size("dp")
    peers = lax.axis_size("tensor")
    per_peer = fetch_pages.shape[2]
    page = kv_pool.shape[2]
    planes = groups // 4
    reach = planes // 2

    def along(values, shift):
        pairs = [(d, (d + 4 * shift) % groups) for d in range(groups)]
        return lax.ppermute(values, "dp", pairs)

    def across(values):
        return lax.ppermute(values, "dp", [(d, d ^ 2) for d in range(groups)])

    def beside(values):
        return lax.ppermute(values, "dp", [(d, d ^ 1) for d in range(groups)])

    wanted = lax.dynamic_index_in_dim(fetch_pages, group, axis=0, keepdims=False).reshape(-1)
    table = jnp.concatenate([wanted, page_owner.reshape(-1)])
    after = lax.optimization_barrier
    ups = {0: kv_pool, 1: along(kv_pool, 1)}
    over = {0: across(kv_pool)}
    column, rot_query, rot_key, value, pool, key_cache = rotate(
        page, segment_ids, page_owner, queries, new_kv, kv_pool
    )
    later, column = after((kv_pool, column))
    ups[-1] = along(later, -1)
    ups[1], column = after((ups[1], column))
    for step in range(2, reach):
        ups[step] = along(ups[step - 1], 1)
        ups[-step] = along(ups[1 - step], -1)
    ups[reach] = along(ups[reach - 1], 1)
    first, over[0], out_weight = after((ups[1], over[0], out_weight))
    over[1] = across(first)
    weight = stage(out_weight)
    ups[-1], weight, table = after((ups[-1], weight, table))
    for step in range(2, reach):
        over[step] = across(ups[step])
    for step in range(1, reach):
        over[-step] = across(ups[-step])
    crossed, ups[reach] = after((over[reach - 1], ups[reach]))
    far = along(crossed, 1)

    early = [(-s, 0, v) for s, v in ups.items() if s] + [(0, 0, pool)]
    early += [(-s, 2, v) for s, v in over.items()]
    layout, parts = [], []
    last = min(over)
    for shift, flip, values in early:
        if values is not over[last]:
            layout += [(shift, flip, (0,)), (shift, flip ^ 1, (0,))]
            parts += [values, beside(kv_pool if values is pool else values)]
    mixed, stats = attend_early(
        layout, table, segment_ids, column, rot_query, rot_key, value, parts, per_peer
    )
    near, mixed = after((over[last], mixed))
    far, mixed = after((far, mixed))
    layout = [(-last, 2, (0,)), (-last, 3, (0,)), (-reach, 2, (0,)), (-reach, 3, (0,))]
    parts = [near, beside(near), far, beside(far)]
    own, *sends = attend_late(
        layout, table, column, rot_query, mixed, stats, weight, parts, per_peer, peers
    )
    summed = residual.astype(jnp.float32) + own.astype(jnp.float32)
    for shift, values in enumerate(sends, 1):
        pairs = [(t, (t + shift) % peers) for t in range(peers)]
        summed = summed + lax.ppermute(values, "tensor", pairs).astype(jnp.float32)
    hidden = (summed + out_bias.astype(jnp.float32)[None, :]).astype(jnp.bfloat16)
    return (hidden, key_cache)


def solution(mesh):
    return jax.shard_map(
        body,
        mesh=mesh,
        in_specs=(
            P(("dp", "tensor"), None),
            P("dp", "tensor"),
            P(None, "dp", "tensor"),
            P("dp", None, None, "tensor"),
            P(),
            P("dp", None),
            P("dp", None),
            P("tensor", None),
            P(),
        ),
        out_specs=(P(("dp", "tensor"), None), P("dp", "tensor")),
        check_vma=False,
    )
```

time: 67.6 us -> 57.4 us (0.85)
  the two profiles are of different devices: /device:TPU:10 before, /device:TPU:0 now
where the time goes in v2:
time: 57.4 us; the launch traced here: 57.2 us
  waiting for transfers between devices  26.2 us (46%)
  starting transfers between devices  12.6 us (22%)
  Pallas kernels  12.3 us (21%)
  local copies, waits for them, and re-layouts  3.6 us (6%)
  other arithmetic  1.75 us (3%)
  between operations  0.76 us (1%)
    ppermute x1, waiting for transfers between devices, body(): summed = summed + lax.ppermute(values, 'tensor', pairs).astype(jnp.float32)  12.5 us
    ppermute x4, waiting for transfers between devices, along(): return lax.ppermute(values, 'dp', pairs)  7.49 us
    ppermute x4, starting transfers between devices, along(): return lax.ppermute(values, 'dp', pairs)  5.48 us
    pallas_call x1, Pallas kernels, attend_late(): pl.pallas_call(functools.partial(late_kernel, layout, per_peer, peers), o...  4.89 us
    ppermute x3, waiting for transfers between devices, across(): return lax.ppermute(values, 'dp', [(d, d ^ 2) for d in range(groups)])  4.41 us
    ppermute x3, starting transfers between devices, across(): return lax.ppermute(values, 'dp', [(d, d ^ 2) for d in range(groups)])  3.97 us
    pallas_call x1, Pallas kernels, rotate(): pl.pallas_call(functools.partial(rotary_kernel, page), out_shape=(jax.Sha...  3.57 us
    unnamed x20, local copies, waits for them, and re-layouts  3.43 us
  transfers between devices with their start and end apart: 16, of which 11 were waited for; matrix products, arithmetic and copies ran while one was open for 2% of the time, Pallas kernels for 13%

profile of v2, /device:TPU:0, one launch (start us, length us, event | category | flops | bytes accessed | tf_op | source)
XLA Modules:
  0.0 57.2 jit_solution(11047383339531254867)
XLA Ops:
  0.6 0.0 copy-start
  0.6 3.1 %collective-permute-start.1 = (bf16[4,2,16,1024]{3,2,1,0:T(8,128)(2,1)}, bf16[4,2,16,1024]{3,2,1,0:T(8,128)(2,1)S(1)}, u32[]{:S(2)}, u32[]{:S(2)}) collective-permute-start(bf16[4,2,16,1024]{3,2,1,0:T(8,128)(2,1)} %pool_ref.1), channel_id=1, source_target_pairs={{0,8},{2,10},{4,12},{6,14},{8,16},{10,18},{12,20},{14,22},{16,24},... | collective-permute-start | bytes 786440 | tf_op jit(solution)/shard_map/ppermute | solution.py:344
  3.7 1.5 %collective-permute-start.2 = (bf16[4,2,16,1024]{3,2,1,0:T(8,128)(2,1)}, bf16[4,2,16,1024]{3,2,1,0:T(8,128)(2,1)S(1)}, u32[]{:S(2)}, u32[]{:S(2)}) collective-permute-start(bf16[4,2,16,1024]{3,2,1,0:T(8,128)(2,1)} %pool_ref.1), channel_id=1, source_target_pairs={{0,4},{2,6},{4,0},{6,2},{8,12},{10,14},{12,8},{14,10},{16,20},{18,... | collective-permute-start | bytes 786440 | tf_op jit(solution)/shard_map/ppermute | solution.py:347
  5.2 3.6 %rotary.1 = (f32[128,128]{1,0:T(8,128)}, bf16[128,1024]{1,0:T(8,128)(2,1)}, bf16[128,1024]{1,0:T(8,128)(2,1)}, bf16[128,1024]{1,0:T(8,128)(2,1)}, bf16[4,2,16,10...) custom-call(s32[1,128]{1,0:T(1,128)} %segments_ref.3, s32[1,32]{1,0:T(1,128)} %owners_ref.1, bf16[128,1024]{1,0:T(8,128)(2,1)} %query_ref.1, ...), custom_call_target="tpu_custom_call" | custom-call | flops 1 | bytes 1 | tf_op jit(solution)/shard_map/rotary/pallas_call | solution.py:99
  8.8 2.3 %collective-permute-start = (bf16[4,2,16,1024]{3,2,1,0:T(8,128)(2,1)}, bf16[4,2,16,1024]{3,2,1,0:T(8,128)(2,1)S(1)}, u32[]{:S(2)}, u32[]{:S(2)}) collective-permute-start(bf16[4,2,16,1024]{3,2,1,0:T(8,128)(2,1)} %pool_ref.1), channel_id=1, source_target_pairs={{0,24},{2,26},{4,28},{6,30},{8,0},{10,2},{12,4},{14,6},{16,8},{18,... | collective-permute-start | bytes 786440 | tf_op jit(solution)/shard_map/ppermute | solution.py:344
  11.1 0.1 copy.12
  11.2 0.1 reshape.12
  11.3 1.1 %collective-permute-done.1.refs_0_ = bf16[4,2,16,1024]{3,2,1,0:T(8,128)(2,1)S(1)} collective-permute-done((bf16[4,2,16,1024]{3,2,1,0:T(8,128)(2,1)}, bf16[4,2,16,1024]{3,2,1,0:T(8,128)(2,1)S(1)}, u32[]{:S(2)}, u32[]{:S(2)}) %collective-permute-start.1) | collective-permute-done | bytes 262176 | tf_op jit(solution)/shard_map/ppermute | solution.py:344
  12.4 1.6 %collective-permute-start.3 = (bf16[4,2,16,1024]{3,2,1,0:T(8,128)(2,1)S(1)}, bf16[4,2,16,1024]{3,2,1,0:T(8,128)(2,1)S(1)}, u32[]{:S(2)}, u32[]{:S(2)}) collective-permute-start(bf16[4,2,16,1024]{3,2,1,0:T(8,128)(2,1)S(1)} %collective-permute-done.1.refs_0_), channel_id=1, source_target_pairs={{0,4},{2,6},{4,0},{6,2},{8,12},{10,14},{12,8},{14,10},{16,20},{18,... | collective-permute-start | bytes 786440 | tf_op jit(solution)/shard_map/ppermute | solution.py:347
  14.0 0.7 %pad_add_fusion.table_ref = s32[64]{0:T(128)S(1)} fusion(s32[32]{0:T(128)} %bitcast.1, s32[32]{0:T(128)S(1)} %reshape.12), kind=kLoop, calls=%fused_computation.1 | loop fusion | flops 64 | bytes 512 | tf_op jit(solution)/shard_map/concatenate | solution.py:353
  14.8 3.4 %copy-done.1 = bf16[1024,4096]{1,0:T(8,128)(2,1)S(1)} copy-done((bf16[1024,4096]{1,0:T(8,128)(2,1)S(1)}, bf16[1024,4096]{1,0:T(8,128)(2,1)}, u32[]{:S(2)}) %copy-start.1) | copy-done | bytes 8388632
  18.2 0.7 %stage.1.weight_ref = bf16[1024,4096]{1,0:T(8,128)(2,1)S(1)} custom-call(bf16[1024,4096]{1,0:T(8,128)(2,1)S(1)} %copy-done.1), custom_call_target="tpu_custom_call" | custom-call | flops 1 | bytes 1 | tf_op jit(solution)/shard_map/stage/pallas_call | solution.py:141
  18.9 0.1 collective-permute-done.refs_2_
  18.9 0.0 collective-permute-start.8
  18.9 0.5 collective-permute-start.11
  19.4 0.7 %collective-permute-done.3.refs_10_ = bf16[4,2,16,1024]{3,2,1,0:T(8,128)(2,1)S(1)} collective-permute-done((bf16[4,2,16,1024]{3,2,1,0:T(8,128)(2,1)S(1)}, bf16[4,2,16,1024]{3,2,1,0:T(8,128)(2,1)S(1)}, u32[]{:S(2)}, u32[]{:S(2)}) %collective-permute-start.3) | collective-permute-done | bytes 262176 | tf_op jit(solution)/shard_map/ppermute | solution.py:347
  20.2 4.0 %collective-permute-done.4.refs_4_ = bf16[4,2,16,1024]{3,2,1,0:T(8,128)(2,1)S(1)} collective-permute-done((bf16[4,2,16,1024]{3,2,1,0:T(8,128)(2,1)S(1)}, bf16[4,2,16,1024]{3,2,1,0:T(8,128)(2,1)S(1)}, u32[]{:S(2)}, u32[]{:S(2)}) %collective-permute-start.4) | collective-permute-done | bytes 262176 | tf_op jit(solution)/shard_map/ppermute | solution.py:344
  24.2 0.5 collective-permute-start.12
  24.7 0.8 %collective-permute-start.6 = (bf16[4,2,16,1024]{3,2,1,0:T(8,128)(2,1)S(1)}, bf16[4,2,16,1024]{3,2,1,0:T(8,128)(2,1)S(1)}, u32[]{:S(2)}, u32[]{:S(2)}) collective-permute-start(bf16[4,2,16,1024]{3,2,1,0:T(8,128)(2,1)S(1)} %collective-permute-done.refs_2_), channel_id=1, source_target_pairs={{0,4},{2,6},{4,0},{6,2},{8,12},{10,14},{12,8},{14,10},{16,20},{18,... | collective-permute-start | bytes 786440 | tf_op jit(solution)/shard_map/ppermute | solution.py:347
  25.5 0.1 collective-permute-start.5
  25.7 0.1 collective-permute-done.9.refs_5_
  25.8 0.4 collective-permute-done.12.refs_11_
  26.2 3.2 %early.1 = (f32[128,1024]{1,0:T(8,128)S(1)}, f32[128,256]{1,0:T(8,128)S(1)}) custom-call(s32[64]{0:T(128)S(1)} %pad_add_fusion.table_ref, s32[1,128]{1,0:T(1,128)S(1)} %copy-done.7, f32[128,128]{1,0:T(8,128)S(1)} %copy-done.3, bf16[128,1024]{1,0:T(8,128)(2,1)S(1)} %copy-done.2, bf16[128,1024]{1,0:T(8,128)(2,1)S(1)} %copy-done.4, ...), custom_call_target="tpu_custom_call" | custom-call | flops 1 | bytes 1 | tf_op jit(solution)/shard_map/early/pallas_call | solution.py:293
  29.4 3.7 %collective-permute-done.6.refs_0_ = bf16[4,2,16,1024]{3,2,1,0:T(8,128)(2,1)S(1)} collective-permute-done((bf16[4,2,16,1024]{3,2,1,0:T(8,128)(2,1)S(1)}, bf16[4,2,16,1024]{3,2,1,0:T(8,128)(2,1)S(1)}, u32[]{:S(2)}, u32[]{:S(2)}) %collective-permute-start.6) | collective-permute-done | bytes 262176 | tf_op jit(solution)/shard_map/ppermute | solution.py:347
  33.0 2.3 %collective-permute-done.5.refs_2_ = bf16[4,2,16,1024]{3,2,1,0:T(8,128)(2,1)S(1)} collective-permute-done((bf16[4,2,16,1024]{3,2,1,0:T(8,128)(2,1)S(1)}, bf16[4,2,16,1024]{3,2,1,0:T(8,128)(2,1)S(1)}, u32[]{:S(2)}, u32[]{:S(2)}) %collective-permute-start.5) | collective-permute-done | bytes 262176 | tf_op jit(solution)/shard_map/ppermute | solution.py:344
  35.3 0.5 collective-permute-start.13
  35.9 1.0 %collective-permute-done.14.refs_3_ = bf16[4,2,16,1024]{3,2,1,0:T(8,128)(2,1)S(1)} collective-permute-done((bf16[4,2,16,1024]{3,2,1,0:T(8,128)(2,1)S(1)}, bf16[4,2,16,1024]{3,2,1,0:T(8,128)(2,1)S(1)}, u32[]{:S(2)}, u32[]{:S(2)}) %collective-permute-start.14) | collective-permute-done | bytes 262176 | tf_op jit(solution)/shard_map/ppermute | solution.py:350
  36.9 0.4 collective-permute-done.13.refs_1_
  37.3 4.9 %late.1 = (bf16[64,4096]{1,0:T(8,128)(2,1)S(1)}, bf16[64,4096]{1,0:T(8,128)(2,1)S(1)}) custom-call(s32[64]{0:T(128)S(1)} %pad_add_fusion.table_ref, f32[128,128]{1,0:T(8,128)S(1)} %copy-done.3, bf16[128,1024]{1,0:T(8,128)(2,1)S(1)} %copy-done.2, f32[128,1024]{1,0:T(8,128)S(1)} %get-tuple-element.46.mixed_ref, f32[128,256]{1,0:T(8,128)S(1)} %get-tuple-element.47.stats_ref, ...), custom_call_target="tpu_custom_call" | custom-call | flops 1 | bytes 1 | tf_op jit(solution)/shard_map/late/pallas_call | solution.py:314
  42.2 1.6 %collective-permute-start.15 = (bf16[64,4096]{1,0:T(8,128)(2,1)S(1)}, bf16[64,4096]{1,0:T(8,128)(2,1)S(1)}, u32[]{:S(2)}, u32[]{:S(2)}) collective-permute-start(bf16[64,4096]{1,0:T(8,128)(2,1)S(1)} %get-tuple-element.52), channel_id=1, source_target_pairs={{0,1},{1,0},{2,3},{3,2},{4,5},{5,4},{6,7},{7,6},{8,9},{9,8},{10,11... | collective-permute-start | bytes 1572872 | tf_op jit(solution)/shard_map/ppermute | solution.py:399
  43.7 12.5 %collective-permute-done.15 = bf16[64,4096]{1,0:T(8,128)(2,1)S(1)} collective-permute-done((bf16[64,4096]{1,0:T(8,128)(2,1)S(1)}, bf16[64,4096]{1,0:T(8,128)(2,1)S(1)}, u32[]{:S(2)}, u32[]{:S(2)}) %collective-permute-start.15) | collective-permute-done | bytes 524320 | tf_op jit(solution)/shard_map/ppermute | solution.py:399
  56.2 1.0 %add_convert_fusion = bf16[64,4096]{1,0:T(8,128)(2,1)} fusion(bf16[64,4096]{1,0:T(8,128)(2,1)S(1)} %collective-permute-done.15, bf16[64,4096]{1,0:T(8,128)(2,1)S(1)} %get-tuple-element.51, bf16[64,4096]{1,0:T(8,128)(2,1)S(1)} %copy-done.8, f32[4096]{0:T(1024)S(1)} %convert_element_type.18), kind=kLoop, calls=%fused_computation | loop fusion | flops 1835008 | bytes 2113536 | tf_op jit(solution)/shard_map/convert_element_type | solution.py:400
  (30 shorter events, 0.1 us)
Async XLA Ops:
  0.6 10.5 %copy-start = (s32[16,16,2]{1,2,0:T(2,128)S(1)}, s32[16,16,2]{1,2,0:T(2,128)}, u32[]{:S(2)}) copy-start(s32[16,16,2]{1,2,0:T(2,128)} %param.13) | copy-start | bytes 6148
  0.6 11.7 %collective-permute-start.1 = (bf16[4,2,16,1024]{3,2,1,0:T(8,128)(2,1)}, bf16[4,2,16,1024]{3,2,1,0:T(8,128)(2,1)S(1)}, u32[]{:S(2)}, u32[]{:S(2)}) collective-permute-start(bf16[4,2,16,1024]{3,2,1,0:T(8,128)(2,1)} %pool_ref.1), channel_id=1, source_target_pairs={{0,8},{2,10},{4,12},{6,14},{8,16},{10,18},{12,20},{14,22},{16,24},... | collective-permute-start | bytes 786440 | tf_op jit(solution)/shard_map/ppermute | solution.py:344
  3.7 8.7 %collective-permute-start.2 = (bf16[4,2,16,1024]{3,2,1,0:T(8,128)(2,1)}, bf16[4,2,16,1024]{3,2,1,0:T(8,128)(2,1)S(1)}, u32[]{:S(2)}, u32[]{:S(2)}) collective-permute-start(bf16[4,2,16,1024]{3,2,1,0:T(8,128)(2,1)} %pool_ref.1), channel_id=1, source_target_pairs={{0,4},{2,6},{4,0},{6,2},{8,12},{10,14},{12,8},{14,10},{16,20},{18,... | collective-permute-start | bytes 786440 | tf_op jit(solution)/shard_map/ppermute | solution.py:347
  8.8 10.1 %collective-permute-start = (bf16[4,2,16,1024]{3,2,1,0:T(8,128)(2,1)}, bf16[4,2,16,1024]{3,2,1,0:T(8,128)(2,1)S(1)}, u32[]{:S(2)}, u32[]{:S(2)}) collective-permute-start(bf16[4,2,16,1024]{3,2,1,0:T(8,128)(2,1)} %pool_ref.1), channel_id=1, source_target_pairs={{0,24},{2,26},{4,28},{6,30},{8,0},{10,2},{12,4},{14,6},{16,8},{18,... | collective-permute-start | bytes 786440 | tf_op jit(solution)/shard_map/ppermute | solution.py:344
  11.1 13.1 %collective-permute-start.10 = (bf16[4,2,16,1024]{3,2,1,0:T(8,128)(2,1)}, bf16[4,2,16,1024]{3,2,1,0:T(8,128)(2,1)S(1)}, u32[]{:S(2)}, u32[]{:S(2)}) collective-permute-start(bf16[4,2,16,1024]{3,2,1,0:T(8,128)(2,1)} %pool_ref.1), channel_id=1, source_target_pairs={{0,2},{2,0},{4,6},{6,4},{8,10},{10,8},{12,14},{14,12},{16,18},{18,... | collective-permute-start | bytes 786440 | tf_op jit(solution)/shard_map/ppermute | solution.py:350
  12.4 11.8 %collective-permute-start.4 = (bf16[4,2,16,1024]{3,2,1,0:T(8,128)(2,1)S(1)}, bf16[4,2,16,1024]{3,2,1,0:T(8,128)(2,1)S(1)}, u32[]{:S(2)}, u32[]{:S(2)}) collective-permute-start(bf16[4,2,16,1024]{3,2,1,0:T(8,128)(2,1)S(1)} %collective-permute-done.1.refs_0_), channel_id=1, source_target_pairs={{0,8},{2,10},{4,12},{6,14},{8,16},{10,18},{12,20},{14,22},{16,24},... | collective-permute-start | bytes 786440 | tf_op jit(solution)/shard_map/ppermute | solution.py:344
  12.4 7.8 %collective-permute-start.3 = (bf16[4,2,16,1024]{3,2,1,0:T(8,128)(2,1)S(1)}, bf16[4,2,16,1024]{3,2,1,0:T(8,128)(2,1)S(1)}, u32[]{:S(2)}, u32[]{:S(2)}) collective-permute-start(bf16[4,2,16,1024]{3,2,1,0:T(8,128)(2,1)S(1)} %collective-permute-done.1.refs_0_), channel_id=1, source_target_pairs={{0,4},{2,6},{4,0},{6,2},{8,12},{10,14},{12,8},{14,10},{16,20},{18,... | collective-permute-start | bytes 786440 | tf_op jit(solution)/shard_map/ppermute | solution.py:347
  14.8 3.4 %copy-start.1 = (bf16[1024,4096]{1,0:T(8,128)(2,1)S(1)}, bf16[1024,4096]{1,0:T(8,128)(2,1)}, u32[]{:S(2)}) copy-start(bf16[1024,4096]{1,0:T(8,128)(2,1)} %source_ref) | copy-start | bytes 25165828
  18.1 8.0 %copy-start.2 = (bf16[128,1024]{1,0:T(8,128)(2,1)S(1)}, bf16[128,1024]{1,0:T(8,128)(2,1)}, u32[]{:S(2)}) copy-start(bf16[128,1024]{1,0:T(8,128)(2,1)} %get-tuple-element.35.query_ref) | copy-start | bytes 786436
  18.1 8.0 %copy-start.3 = (f32[128,128]{1,0:T(8,128)S(1)}, f32[128,128]{1,0:T(8,128)}, u32[]{:S(2)}) copy-start(f32[128,128]{1,0:T(8,128)} %get-tuple-element.34.column_ref) | copy-start | bytes 196612
  18.1 8.0 %copy-start.4 = (bf16[128,1024]{1,0:T(8,128)(2,1)S(1)}, bf16[128,1024]{1,0:T(8,128)(2,1)}, u32[]{:S(2)}) copy-start(bf16[128,1024]{1,0:T(8,128)(2,1)} %get-tuple-element.39.key_ref) | copy-start | bytes 786436
  18.1 8.0 %copy-start.5 = (bf16[128,1024]{1,0:T(8,128)(2,1)S(1)}, bf16[128,1024]{1,0:T(8,128)(2,1)}, u32[]{:S(2)}) copy-start(bf16[128,1024]{1,0:T(8,128)(2,1)} %get-tuple-element.40.value_ref) | copy-start | bytes 786436
  18.1 8.0 %copy-start.6 = (bf16[4,2,16,1024]{3,2,1,0:T(8,128)(2,1)S(1)}, bf16[4,2,16,1024]{3,2,1,0:T(8,128)(2,1)}, u32[]{:S(2)}) copy-start(bf16[4,2,16,1024]{3,2,1,0:T(8,128)(2,1)} %get-tuple-element.42.refs_6_) | copy-start | bytes 786436
  18.2 8.0 %copy-start.7 = (s32[1,128]{1,0:T(1,128)S(1)}, s32[1,128]{1,0:T(1,128)}, u32[]{:S(2)}) copy-start(s32[1,128]{1,0:T(1,128)} %segments_ref.3) | copy-start | bytes 1540
  18.8 24.9 %copy-start.9 = (bf16[4096]{0:T(1024)(128)(2,1)S(1)}, bf16[4096]{0:T(1024)(128)(2,1)}, u32[]{:S(2)}) copy-start(bf16[4096]{0:T(1024)(128)(2,1)} %param.17) | copy-start | bytes 24580
  18.8 37.3 %copy-start.8 = (bf16[64,4096]{1,0:T(8,128)(2,1)S(1)}, bf16[64,4096]{1,0:T(8,128)(2,1)}, u32[]{:S(2)}) copy-start(bf16[64,4096]{1,0:T(8,128)(2,1)} %param.9) | copy-start | bytes 1572868
  18.9 5.8 %collective-permute-start.8 = (bf16[4,2,16,1024]{3,2,1,0:T(8,128)(2,1)S(1)}, bf16[4,2,16,1024]{3,2,1,0:T(8,128)(2,1)S(1)}, u32[]{:S(2)}, u32[]{:S(2)}) collective-permute-start(bf16[4,2,16,1024]{3,2,1,0:T(8,128)(2,1)S(1)} %collective-permute-done.refs_2_), channel_id=1, source_target_pairs={{0,2},{2,0},{4,6},{6,4},{8,10},{10,8},{12,14},{14,12},{16,18},{18,... | collective-permute-start | bytes 786440 | tf_op jit(solution)/shard_map/ppermute | solution.py:350
  18.9 6.6 %collective-permute-start.11 = (bf16[4,2,16,1024]{3,2,1,0:T(8,128)(2,1)S(1)}, bf16[4,2,16,1024]{3,2,1,0:T(8,128)(2,1)S(1)}, u32[]{:S(2)}, u32[]{:S(2)}) collective-permute-start(bf16[4,2,16,1024]{3,2,1,0:T(8,128)(2,1)S(1)} %collective-permute-done.2.refs_8_), channel_id=1, source_target_pairs={{0,2},{2,0},{4,6},{6,4},{8,10},{10,8},{12,14},{14,12},{16,18},{18,... | collective-permute-start | bytes 786440 | tf_op jit(solution)/shard_map/ppermute | solution.py:350
  20.2 5.5 %collective-permute-start.7 = (bf16[4,2,16,1024]{3,2,1,0:T(8,128)(2,1)S(1)}, bf16[4,2,16,1024]{3,2,1,0:T(8,128)(2,1)S(1)}, u32[]{:S(2)}, u32[]{:S(2)}) collective-permute-start(bf16[4,2,16,1024]{3,2,1,0:T(8,128)(2,1)S(1)} %collective-permute-done.1.refs_0_), channel_id=1, source_target_pairs={{0,2},{2,0},{4,6},{6,4},{8,10},{10,8},{12,14},{14,12},{16,18},{18,... | collective-permute-start | bytes 786440 | tf_op jit(solution)/shard_map/ppermute | solution.py:350
  24.2 1.5 %collective-permute-start.9 = (bf16[4,2,16,1024]{3,2,1,0:T(8,128)(2,1)S(1)}, bf16[4,2,16,1024]{3,2,1,0:T(8,128)(2,1)S(1)}, u32[]{:S(2)}, u32[]{:S(2)}) collective-permute-start(bf16[4,2,16,1024]{3,2,1,0:T(8,128)(2,1)S(1)} %collective-permute-done.4.refs_4_), channel_id=1, source_target_pairs={{0,2},{2,0},{4,6},{6,4},{8,10},{10,8},{12,14},{14,12},{16,18},{18,... | collective-permute-start | bytes 786440 | tf_op jit(solution)/shard_map/ppermute | solution.py:350
  24.2 1.9 %collective-permute-start.12 = (bf16[4,2,16,1024]{3,2,1,0:T(8,128)(2,1)S(1)}, bf16[4,2,16,1024]{3,2,1,0:T(8,128)(2,1)S(1)}, u32[]{:S(2)}, u32[]{:S(2)}) collective-permute-start(bf16[4,2,16,1024]{3,2,1,0:T(8,128)(2,1)S(1)} %collective-permute-done.3.refs_10_), channel_id=1, source_target_pairs={{0,2},{2,0},{4,6},{6,4},{8,10},{10,8},{12,14},{14,12},{16,18},{18,... | collective-permute-start | bytes 786440 | tf_op jit(solution)/shard_map/ppermute | solution.py:350
  24.7 8.3 %collective-permute-start.6 = (bf16[4,2,16,1024]{3,2,1,0:T(8,128)(2,1)S(1)}, bf16[4,2,16,1024]{3,2,1,0:T(8,128)(2,1)S(1)}, u32[]{:S(2)}, u32[]{:S(2)}) collective-permute-start(bf16[4,2,16,1024]{3,2,1,0:T(8,128)(2,1)S(1)} %collective-permute-done.refs_2_), channel_id=1, source_target_pairs={{0,4},{2,6},{4,0},{6,2},{8,12},{10,14},{12,8},{14,10},{16,20},{18,... | collective-permute-start | bytes 786440 | tf_op jit(solution)/shard_map/ppermute | solution.py:347
  25.5 9.8 %collective-permute-start.5 = (bf16[4,2,16,1024]{3,2,1,0:T(8,128)(2,1)S(1)}, bf16[4,2,16,1024]{3,2,1,0:T(8,128)(2,1)S(1)}, u32[]{:S(2)}, u32[]{:S(2)}) collective-permute-start(bf16[4,2,16,1024]{3,2,1,0:T(8,128)(2,1)S(1)} %collective-permute-done.3.refs_10_), channel_id=1, source_target_pairs={{0,8},{2,10},{4,12},{6,14},{8,16},{10,18},{12,20},{14,22},{16,24},... | collective-permute-start | bytes 786440 | tf_op jit(solution)/shard_map/ppermute | solution.py:344
  35.3 1.5 %collective-permute-start.14 = (bf16[4,2,16,1024]{3,2,1,0:T(8,128)(2,1)S(1)}, bf16[4,2,16,1024]{3,2,1,0:T(8,128)(2,1)S(1)}, u32[]{:S(2)}, u32[]{:S(2)}) collective-permute-start(bf16[4,2,16,1024]{3,2,1,0:T(8,128)(2,1)S(1)} %collective-permute-done.5.refs_2_), channel_id=1, source_target_pairs={{0,2},{2,0},{4,6},{6,4},{8,10},{10,8},{12,14},{14,12},{16,18},{18,... | collective-permute-start | bytes 786440 | tf_op jit(solution)/shard_map/ppermute | solution.py:350
  35.3 1.9 %collective-permute-start.13 = (bf16[4,2,16,1024]{3,2,1,0:T(8,128)(2,1)S(1)}, bf16[4,2,16,1024]{3,2,1,0:T(8,128)(2,1)S(1)}, u32[]{:S(2)}, u32[]{:S(2)}) collective-permute-start(bf16[4,2,16,1024]{3,2,1,0:T(8,128)(2,1)S(1)} %collective-permute-done.6.refs_0_), channel_id=1, source_target_pairs={{0,2},{2,0},{4,6},{6,4},{8,10},{10,8},{12,14},{14,12},{16,18},{18,... | collective-permute-start | bytes 786440 | tf_op jit(solution)/shard_map/ppermute | solution.py:350
  42.2 14.0 %collective-permute-start.15 = (bf16[64,4096]{1,0:T(8,128)(2,1)S(1)}, bf16[64,4096]{1,0:T(8,128)(2,1)S(1)}, u32[]{:S(2)}, u32[]{:S(2)}) collective-permute-start(bf16[64,4096]{1,0:T(8,128)(2,1)S(1)} %get-tuple-element.52), channel_id=1, source_target_pairs={{0,1},{1,0},{2,3},{3,2},{4,5},{5,4},{6,7},{7,6},{8,9},{9,8},{10,11... | collective-permute-start | bytes 1572872 | tf_op jit(solution)/shard_map/ppermute | solution.py:399

commit v3 on v2

--- a/solution.py
+++ b/solution.py
@@ -210,20 +210,24 @@
     see_new = (column == segments) & (cols <= rows)
     see_old = column == key_owner
     lane = lax.broadcasted_iota(jnp.int32, (tokens, HD), 1)
+    heads = [slice(start, start + HD) for start in range(0, feature, HD)]
+    new = [scores_of(query_ref[:, head], key_ref[:, head], see_new) for head in heads]
+    old = [scores_of(query_ref[:, head], keys[:, head], see_old) for head in heads]
+    peaks = [
+        jnp.maximum(jnp.max(a, axis=1, keepdims=True), jnp.max(b, axis=1, keepdims=True))
+        for a, b in zip(new, old)
+    ]
+    new = [jnp.exp2(a - top) for a, top in zip(new, peaks)]
+    old = [jnp.exp2(b - top) for b, top in zip(old, peaks)]
     tops = totals = jnp.zeros((tokens, HD), jnp.float32)
-    for number, start in enumerate(range(0, feature, HD)):
-        head = slice(start, start + HD)
-        query = query_ref[:, head]
-        new = scores_of(query, key_ref[:, head], see_new)
-        old = scores_of(query, keys[:, head], see_old)
-        top = jnp.maximum(
-            jnp.max(new, axis=1, keepdims=True), jnp.max(old, axis=1, keepdims=True)
+    for number, head in enumerate(heads):
+        total = jnp.sum(new[number], axis=1, keepdims=True) + jnp.sum(
+            old[number], axis=1, keepdims=True
         )
-        new = jnp.exp2(new - top)
-        old = jnp.exp2(old - top)
-        total = jnp.sum(new, axis=1, keepdims=True) + jnp.sum(old, axis=1, keepdims=True)
-        mixed_ref[:, head] = weigh(new, value_ref[:, head]) + weigh(old, values[:, head])
-        tops = jnp.where(lane == number, top, tops)
+        mixed_ref[:, head] = weigh(new[number], value_ref[:, head]) + weigh(
+            old[number], values[:, head]
+        )
+        tops = jnp.where(lane == number, peaks[number], tops)
         totals = jnp.where(lane == number, total, totals)
     stats_ref[:, :HD] = tops
     stats_ref[:, HD:] = totals
@@ -243,34 +247,37 @@
 ):
     count = sum(len(cuts) for _, _, cuts in blocks)
     block_refs = refs[:count]
-    own_ref, *send_refs = refs[count : count + peers]
-    keys, values, context_ref, product = refs[count + peers :]
+    context_ref, own_ref, *send_refs = refs[count : count + 1 + peers]
+    keys, values, product = refs[count + 1 + peers :]
     tokens, feature = query_ref.shape
     key_owner = gather_pages(blocks, block_refs, per_peer, table_ref, keys, values)
     seen = column_ref[:, :1] == key_owner
-    for number, start in enumerate(range(0, feature, HD)):
-        head = slice(start, start + HD)
-        scores = scores_of(query_ref[:, head], keys[:, head], seen)
-        before = stats_ref[:, number : number + 1]
-        top = jnp.maximum(before, jnp.max(scores, axis=1, keepdims=True))
-        weights = jnp.exp2(scores - top)
-        fade = jnp.exp2(before - top)
-        total = stats_ref[:, HD + number : HD + number + 1] * fade + jnp.sum(
-            weights, axis=1, keepdims=True
+    heads = [slice(start, start + HD) for start in range(0, feature, HD)]
+    scores = [scores_of(query_ref[:, head], keys[:, head], seen) for head in heads]
+    before = [stats_ref[:, number : number + 1] for number in range(len(heads))]
+    tops = [
+        jnp.maximum(old, jnp.max(new, axis=1, keepdims=True)) for old, new in zip(before, scores)
+    ]
+    weights = [jnp.exp2(new - top) for new, top in zip(scores, tops)]
+    fades = [jnp.exp2(old - top) for old, top in zip(before, tops)]
+    added = [weigh(part, values[:, head]) for part, head in zip(weights, heads)]
+    for number, head in enumerate(heads):
+        total = stats_ref[:, HD + number : HD + number + 1] * fades[number] + jnp.sum(
+            weights[number], axis=1, keepdims=True
         )
-        mixed = mixed_ref[:, head] * fade + weigh(weights, values[:, head])
-        context_ref[:, head] = (mixed / total).astype(jnp.bfloat16)
-    project_rows(peers, context_ref, weight_ref, product, own_ref, send_refs)
-
-
-def project_rows(peers, context_ref, weight_ref, product, own_ref, send_refs):
+        mixed = mixed_ref[:, head] * fades[number] + added[number]
+        context_ref[:, head] = (mixed * pl.reciprocal(total)).astype(jnp.bfloat16)
+    project_rows(peers, 0, context_ref, weight_ref, product, own_ref, send_refs)
+
+
+def project_rows(peers, first, context_ref, weight_ref, product, own_ref, send_refs):
     rows, width = own_ref.shape
     me = lax.axis_index("tensor")
-    step = min(512, width)
+    step = 256
     for start in range(0, width, step):
         product[:, start : start + step] = jnp.dot(
             context_ref[...],
-            weight_ref[:, start : start + step],
+            weight_ref[:, first + start : first + start + step],
             preferred_element_type=jnp.float32,
         ).astype(jnp.bfloat16)
     own_ref[...] = product[pl.ds(pl.multiple_of(me * rows, rows), rows), :]
@@ -307,25 +314,110 @@
 
 
 def attend_late(
-    layout, table, column, rot_query, mixed, stats, weight, parts, per_peer, peers
+    layout, table, column, rot_query, mixed, stats, weight, parts, per_peer, peers, width
 ):
     tokens, feature = rot_query.shape
     prefix = len(layout) * per_peer * parts[0].shape[2]
     return pl.pallas_call(
         functools.partial(late_kernel, layout, per_peer, peers),
-        out_shape=shares(tokens, peers, weight.shape[1]),
+        out_shape=(jax.ShapeDtypeStruct((tokens, feature), jnp.bfloat16),)
+        + shares(tokens, peers, width),
         grid=(1,),
         in_specs=[smem()] + [vmem()] * (5 + len(parts)),
-        out_specs=(vmem(),) * peers,
+        out_specs=(vmem(),) * (1 + peers),
         scratch_shapes=[pltpu.VMEM((prefix, feature), jnp.bfloat16)] * 2
-        + [
-            pltpu.VMEM((tokens, feature), jnp.bfloat16),
-            pltpu.VMEM((tokens, weight.shape[1]), jnp.bfloat16),
-        ],
+        + [pltpu.VMEM((tokens, width), jnp.bfloat16)],
         compiler_params=params(LATE_LIMIT),
         cost_estimate=cheap(),
         name="late",
     )(table, column, rot_query, mixed, stats, weight, *parts)
+
+
+def project_kernel(peers, first, context_ref, weight_ref, own_ref, *refs):
+    *send_refs, product = refs
+    project_rows(peers, first, context_ref, weight_ref, product, own_ref, send_refs)
+
+
+def project(context, weight, peers, first, width):
+    tokens, feature = context.shape
+    return pl.pallas_call(
+        functools.partial(project_kernel, peers, first),
+        out_shape=shares(tokens, peers, width),
+        in_specs=[vmem()] * 2,
+        out_specs=(vmem(),) * peers,
+        scratch_shapes=[pltpu.VMEM((tokens, width), jnp.bfloat16)],
+        compiler_params=params(),
+        cost_estimate=cheap(),
+        name="project",
+    )(context, weight)
+
+
+def base_kernel(residual_ref, bias_ref, *refs):
+    *own_refs, base_ref = refs
+    start = 0
+    for own_ref in own_refs:
+        columns = slice(start, start + own_ref.shape[1])
+        start += own_ref.shape[1]
+        base_ref[:, columns] = (
+            residual_ref[:, columns].astype(jnp.float32)
+            + own_ref[...].astype(jnp.float32)
+            + bias_ref[:, columns].astype(jnp.float32)
+        )
+
+
+def base_of(residual, bias, owns):
+    return pl.pallas_call(
+        base_kernel,
+        out_shape=jax.ShapeDtypeStruct(residual.shape, jnp.float32),
+        in_specs=[vmem()] * (2 + len(owns)),
+        out_specs=vmem(),
+        compiler_params=params(),
+        cost_estimate=cheap(),
+        name="base",
+    )(residual, bias, *owns)
+
+
+def finish_kernel(first, count, base_ref, *refs):
+    received = refs[:count]
+    hidden_ref, rounded, done = refs[-3:]
+    width = rounded.shape[1]
+    step = 256
+    copies = []
+    for piece in range(width // step):
+        start = piece * step
+        total = base_ref[:, first + start : first + start + step]
+        for part in received:
+            total = total + part[:, start : start + step].astype(jnp.float32)
+        rounded[:, start : start + step] = total.astype(jnp.bfloat16)
+        copies.append(
+            pltpu.make_async_copy(
+                rounded.at[:, start : start + step],
+                hidden_ref.at[:, first + start : first + start + step],
+                done.at[piece],
+            )
+        )
+        copies[-1].start()
+    for copy in copies:
+        copy.wait()
+
+
+def finish(base, received, first, hidden):
+    rows, width = received[0].shape
+    before = [] if hidden is None else [hidden]
+    return pl.pallas_call(
+        functools.partial(finish_kernel, first, len(received)),
+        out_shape=jax.ShapeDtypeStruct(base.shape, jnp.bfloat16),
+        in_specs=[vmem()] * (1 + len(received)) + [anywhere()] * len(before),
+        out_specs=anywhere(),
+        scratch_shapes=[
+            pltpu.VMEM((rows, width), jnp.bfloat16),
+            pltpu.SemaphoreType.DMA((width // 256,)),
+        ],
+        input_output_aliases={1 + len(received): 0} if before else {},
+        compiler_params=params(),
+        cost_estimate=cheap(),
+        name="finish",
+    )(base, *received, *before)
 
 
 def body(
@@ -351,12 +443,12 @@
 
     wanted = lax.dynamic_index_in_dim(fetch_pages, group, axis=0, keepdims=False).reshape(-1)
     table = jnp.concatenate([wanted, page_owner.reshape(-1)])
+    wide = out_weight.shape[1] // 16
+    widths = (6 * wide, 5 * wide, 5 * wide)
     after = lax.optimization_barrier
     ups = {0: kv_pool, 1: along(kv_pool, 1)}
     over = {0: across(kv_pool)}
-    column, rot_query, rot_key, value, pool, key_cache = rotate(
-        page, segment_ids, page_owner, queries, new_kv, kv_pool
-    )
+    column, rot_query, rot_key, value, pool, key_cache = rotate(page, segment_ids, page_owner, queries, new_kv, kv_pool)
     later, column = after((kv_pool, column))
     ups[-1] = along(later, -1)
     ups[1], column = after((ups[1], column))
@@ -364,7 +456,8 @@
         ups[step] = along(ups[step - 1], 1)
         ups[-step] = along(ups[1 - step], -1)
     ups[reach] = along(ups[reach - 1], 1)
-    first, over[0], out_weight = after((ups[1], over[0], out_weight))
+    first, out_weight = after((ups[1], out_weight))
+    first, over[0] = after((first, over[0]))
     over[1] = across(first)
     weight = stage(out_weight)
     ups[-1], weight, table = after((ups[-1], weight, table))
@@ -372,32 +465,49 @@
         over[step] = across(ups[step])
     for step in range(1, reach):
         over[-step] = across(ups[-step])
-    crossed, ups[reach] = after((over[reach - 1], ups[reach]))
-    far = along(crossed, 1)
-
-    early = [(-s, 0, v) for s, v in ups.items() if s] + [(0, 0, pool)]
-    early += [(-s, 2, v) for s, v in over.items()]
-    layout, parts = [], []
     last = min(over)
-    for shift, flip, values in early:
-        if values is not over[last]:
-            layout += [(shift, flip, (0,)), (shift, flip ^ 1, (0,))]
-            parts += [values, beside(kv_pool if values is pool else values)]
+    crossed, near = over[reach - 1], over[last]
+    crossed, ups[reach] = after((crossed, ups[reach]))
+
+    layout, parts, rest = [], [], []
+    for flip, found in ((0, ups), (2, over)):
+        for shift, values in found.items():
+            if (flip, shift) in ((0, reach), (2, reach - 1)):
+                rest.append((shift, flip, values))
+            elif (flip, shift) != (2, last):
+                layout += [(-shift, flip, (0,)), (-shift, flip ^ 1, (0,))]
+                parts += [pool if values is kv_pool else values, beside(values)]
     mixed, stats = attend_early(
         layout, table, segment_ids, column, rot_query, rot_key, value, parts, per_peer
     )
-    near, mixed = after((over[last], mixed))
+    far = along(crossed, 1)
+    near, mixed = after((near, mixed))
     far, mixed = after((far, mixed))
-    layout = [(-last, 2, (0,)), (-last, 3, (0,)), (-reach, 2, (0,)), (-reach, 3, (0,))]
-    parts = [near, beside(near), far, beside(far)]
-    own, *sends = attend_late(
-        layout, table, column, rot_query, mixed, stats, weight, parts, per_peer, peers
+    rest += [(last, 2, near), (reach, 2, far)]
+    layout, parts = [], []
+    for shift, flip, values in rest:
+        layout += [(-shift, flip, (0,)), (-shift, flip ^ 1, (0,))]
+        parts += [values, beside(values)]
+    context, *share = attend_late(
+        layout, table, column, rot_query, mixed, stats, weight, parts, per_peer, peers, widths[0]
     )
-    summed = residual.astype(jnp.float32) + own.astype(jnp.float32)
-    for shift, values in enumerate(sends, 1):
-        pairs = [(t, (t + shift) % peers) for t in range(peers)]
-        summed = summed + lax.ppermute(values, "tensor", pairs).astype(jnp.float32)
-    hidden = (summed + out_bias.astype(jnp.float32)[None, :]).astype(jnp.bfloat16)
+    owns, received = [share[0]], []
+    start = 0
+    for number, width in enumerate(widths):
+        pieces = []
+        for shift, values in enumerate(share[1:], 1):
+            pairs = [(t, (t + shift) % peers) for t in range(peers)]
+            pieces.append(lax.ppermute(values, "tensor", pairs))
+        received.append(pieces)
+        start += width
+        if number + 1 < len(widths):
+            share = project(context, weight, peers, start, widths[number + 1])
+            owns.append(share[0])
+    base = base_of(residual, out_bias.reshape(1, -1), owns)
+    hidden, start = None, 0
+    for width, pieces in zip(widths, received):
+        hidden = finish(base, pieces, start, hidden)
+        start += width
     return (hidden, key_cache)
 
 

time: 57.4 us -> 52.9 us (0.922)
  waiting for transfers between devices: 26.2 us -> 19.8 us
  starting transfers between devices: 12.6 us -> 15.5 us
  other arithmetic: 1.75 us -> 0.73 us
    ppermute x1 -> x3, waiting for transfers between devices: 12.5 us -> 7.56 us  [body(): pieces.append(lax.ppermute(values, 'tensor', pairs))]
    pallas_call x0 -> x6, Pallas kernels: none -> 3.41 us  [the longest x3 2.15 us: finish(): pl.pallas_call(functools.partial(finish_kernel, first, len(received)), ou...]
    ppermute x1 -> x3, starting transfers between devices: 1.57 us -> 3.73 us  [body(): pieces.append(lax.ppermute(values, 'tensor', pairs))]
    pallas_call x1, Pallas kernels: 4.89 us -> 2.99 us  [attend_late(): pl.pallas_call(functools.partial(late_kernel, layout, per_peer, peers), o...]
    pallas_call x1, Pallas kernels: 3.18 us -> 1.62 us  [attend_early(): pl.pallas_call(functools.partial(early_kernel, layout, per_peer), out_sha...]
    convert_element_type x2 -> x0, other arithmetic: 1.02 us -> none  [the longest x1 1.02 us: body(): (summed + out_bias.astype(jnp.float32)[None, :]).astype(jnp.bfloat16)]
    ppermute x4, waiting for transfers between devices: 7.49 us -> 6.52 us  [along(): return lax.ppermute(values, 'dp', pairs)]
    ppermute x4, starting transfers between devices: 5.48 us -> 6.22 us  [along(): return lax.ppermute(values, 'dp', pairs)]
  transfers between devices with their start and end apart: 16 -> 18, of which waited for: 11 -> 8; matrix products, arithmetic and copies ran while one was open for 2% -> 2% of each run, Pallas kernels for 13% -> 16%
where the time goes in v3:
time: 52.9 us; the launch traced here: 52.7 us
  waiting for transfers between devices  19.8 us (37%)
  starting transfers between devices  15.5 us (29%)
  Pallas kernels  12.2 us (23%)
  local copies, waits for them, and re-layouts  3.61 us (7%)
  between operations  0.82 us (2%)
  other arithmetic  0.73 us (1%)
    ppermute x3, waiting for transfers between devices, body(): pieces.append(lax.ppermute(values, 'tensor', pairs))  7.56 us
    ppermute x4, waiting for transfers between devices, along(): return lax.ppermute(values, 'dp', pairs)  6.52 us
    ppermute x4, starting transfers between devices, along(): return lax.ppermute(values, 'dp', pairs)  6.22 us
    ppermute x3, waiting for transfers between devices, across(): return lax.ppermute(values, 'dp', [(d, d ^ 2) for d in range(groups)])  4.16 us
    ppermute x3, starting transfers between devices, across(): return lax.ppermute(values, 'dp', [(d, d ^ 2) for d in range(groups)])  3.98 us
    ppermute x3, starting transfers between devices, body(): pieces.append(lax.ppermute(values, 'tensor', pairs))  3.73 us
    pallas_call x1, Pallas kernels, rotate(): pl.pallas_call(functools.partial(rotary_kernel, page), out_shape=(jax.Sha...  3.57 us
    unnamed x20, local copies, waits for them, and re-layouts  3.42 us
  transfers between devices with their start and end apart: 18, of which 8 were waited for; matrix products, arithmetic and copies ran while one was open for 2% of the time, Pallas kernels for 16%

profile of v3, /device:TPU:0, one launch (start us, length us, event | category | flops | bytes accessed | tf_op | source)
XLA Modules:
  0.0 52.7 jit_solution(8858842597901710582)
XLA Ops:
  0.6 3.1 %collective-permute-start.1 = (bf16[4,2,16,1024]{3,2,1,0:T(8,128)(2,1)}, bf16[4,2,16,1024]{3,2,1,0:T(8,128)(2,1)S(1)}, u32[]{:S(2)}, u32[]{:S(2)}) collective-permute-start(bf16[4,2,16,1024]{3,2,1,0:T(8,128)(2,1)} %pool_ref.1), channel_id=1, source_target_pairs={{0,8},{2,10},{4,12},{6,14},{8,16},{10,18},{12,20},{14,22},{16,24},... | collective-permute-start | bytes 786440 | tf_op jit(solution)/shard_map/ppermute | solution.py:436
  3.7 1.5 %collective-permute-start.2 = (bf16[4,2,16,1024]{3,2,1,0:T(8,128)(2,1)}, bf16[4,2,16,1024]{3,2,1,0:T(8,128)(2,1)S(1)}, u32[]{:S(2)}, u32[]{:S(2)}) collective-permute-start(bf16[4,2,16,1024]{3,2,1,0:T(8,128)(2,1)} %pool_ref.1), channel_id=1, source_target_pairs={{0,4},{2,6},{4,0},{6,2},{8,12},{10,14},{12,8},{14,10},{16,20},{18,... | collective-permute-start | bytes 786440 | tf_op jit(solution)/shard_map/ppermute | solution.py:439
  5.2 3.6 %rotary.1 = (f32[128,128]{1,0:T(8,128)}, bf16[128,1024]{1,0:T(8,128)(2,1)}, bf16[128,1024]{1,0:T(8,128)(2,1)}, bf16[128,1024]{1,0:T(8,128)(2,1)}, bf16[4,2,16,10...) custom-call(s32[1,128]{1,0:T(1,128)} %segments_ref.3, s32[1,32]{1,0:T(1,128)} %owners_ref.1, bf16[128,1024]{1,0:T(8,128)(2,1)} %query_ref.1, ...), custom_call_target="tpu_custom_call" | custom-call | flops 1 | bytes 1 | tf_op jit(solution)/shard_map/rotary/pallas_call | solution.py:99
  8.8 2.3 %collective-permute-start = (bf16[4,2,16,1024]{3,2,1,0:T(8,128)(2,1)}, bf16[4,2,16,1024]{3,2,1,0:T(8,128)(2,1)S(1)}, u32[]{:S(2)}, u32[]{:S(2)}) collective-permute-start(bf16[4,2,16,1024]{3,2,1,0:T(8,128)(2,1)} %pool_ref.1), channel_id=1, source_target_pairs={{0,24},{2,26},{4,28},{6,30},{8,0},{10,2},{12,4},{14,6},{16,8},{18,... | collective-permute-start | bytes 786440 | tf_op jit(solution)/shard_map/ppermute | solution.py:436
  11.1 1.3 %collective-permute-done.1.refs_2_ = bf16[4,2,16,1024]{3,2,1,0:T(8,128)(2,1)S(1)} collective-permute-done((bf16[4,2,16,1024]{3,2,1,0:T(8,128)(2,1)}, bf16[4,2,16,1024]{3,2,1,0:T(8,128)(2,1)S(1)}, u32[]{:S(2)}, u32[]{:S(2)}) %collective-permute-start.1) | collective-permute-done | bytes 262176 | tf_op jit(solution)/shard_map/ppermute | solution.py:436
  12.4 1.7 %collective-permute-start.3 = (bf16[4,2,16,1024]{3,2,1,0:T(8,128)(2,1)S(1)}, bf16[4,2,16,1024]{3,2,1,0:T(8,128)(2,1)S(1)}, u32[]{:S(2)}, u32[]{:S(2)}) collective-permute-start(bf16[4,2,16,1024]{3,2,1,0:T(8,128)(2,1)S(1)} %collective-permute-done.1.refs_2_), channel_id=1, source_target_pairs={{0,4},{2,6},{4,0},{6,2},{8,12},{10,14},{12,8},{14,10},{16,20},{18,... | collective-permute-start | bytes 786440 | tf_op jit(solution)/shard_map/ppermute | solution.py:439
  14.0 0.8 %collective-permute-start.4 = (bf16[4,2,16,1024]{3,2,1,0:T(8,128)(2,1)S(1)}, bf16[4,2,16,1024]{3,2,1,0:T(8,128)(2,1)S(1)}, u32[]{:S(2)}, u32[]{:S(2)}) collective-permute-start(bf16[4,2,16,1024]{3,2,1,0:T(8,128)(2,1)S(1)} %collective-permute-done.1.refs_2_), channel_id=1, source_target_pairs={{0,8},{2,10},{4,12},{6,14},{8,16},{10,18},{12,20},{14,22},{16,24},... | collective-permute-start | bytes 786440 | tf_op jit(solution)/shard_map/ppermute | solution.py:436
  15.0 0.7 %pad_add_fusion.table_ref = s32[64]{0:T(128)S(1)} fusion(s32[32]{0:T(128)} %bitcast.1, s32[32]{0:T(128)S(1)} %reshape.15), kind=kLoop, calls=%fused_computation | loop fusion | flops 64 | bytes 512 | tf_op jit(solution)/shard_map/concatenate | solution.py:445
  15.7 3.4 %copy-done.1 = bf16[1024,4096]{1,0:T(8,128)(2,1)S(1)} copy-done((bf16[1024,4096]{1,0:T(8,128)(2,1)S(1)}, bf16[1024,4096]{1,0:T(8,128)(2,1)}, u32[]{:S(2)}) %copy-start.1) | copy-done | bytes 8388632
  19.1 0.7 %stage.1.weight_ref = bf16[1024,4096]{1,0:T(8,128)(2,1)S(1)} custom-call(bf16[1024,4096]{1,0:T(8,128)(2,1)S(1)} %copy-done.1), custom_call_target="tpu_custom_call" | custom-call | flops 1 | bytes 1 | tf_op jit(solution)/shard_map/stage/pallas_call | solution.py:141
  19.8 0.6 %collective-permute-start.9 = (bf16[4,2,16,1024]{3,2,1,0:T(8,128)(2,1)S(1)}, bf16[4,2,16,1024]{3,2,1,0:T(8,128)(2,1)S(1)}, u32[]{:S(2)}, u32[]{:S(2)}) collective-permute-start(bf16[4,2,16,1024]{3,2,1,0:T(8,128)(2,1)S(1)} %collective-permute-done.refs_4_), channel_id=1, source_target_pairs={{0,2},{2,0},{4,6},{6,4},{8,10},{10,8},{12,14},{14,12},{16,18},{18,... | collective-permute-start | bytes 786440 | tf_op jit(solution)/shard_map/ppermute | solution.py:442
  20.5 0.4 collective-permute-start.8
  20.9 3.3 %collective-permute-done.4.refs_0_ = bf16[4,2,16,1024]{3,2,1,0:T(8,128)(2,1)S(1)} collective-permute-done((bf16[4,2,16,1024]{3,2,1,0:T(8,128)(2,1)S(1)}, bf16[4,2,16,1024]{3,2,1,0:T(8,128)(2,1)S(1)}, u32[]{:S(2)}, u32[]{:S(2)}) %collective-permute-start.4) | collective-permute-done | bytes 262176 | tf_op jit(solution)/shard_map/ppermute | solution.py:436
  24.2 0.8 %collective-permute-start.6 = (bf16[4,2,16,1024]{3,2,1,0:T(8,128)(2,1)S(1)}, bf16[4,2,16,1024]{3,2,1,0:T(8,128)(2,1)S(1)}, u32[]{:S(2)}, u32[]{:S(2)}) collective-permute-start(bf16[4,2,16,1024]{3,2,1,0:T(8,128)(2,1)S(1)} %collective-permute-done.refs_4_), channel_id=1, source_target_pairs={{0,4},{2,6},{4,0},{6,2},{8,12},{10,14},{12,8},{14,10},{16,20},{18,... | collective-permute-start | bytes 786440 | tf_op jit(solution)/shard_map/ppermute | solution.py:439
  25.2 1.6 %early.1 = (f32[128,1024]{1,0:T(8,128)S(1)}, f32[128,256]{1,0:T(8,128)S(1)}) custom-call(s32[64]{0:T(128)S(1)} %pad_add_fusion.table_ref, s32[1,128]{1,0:T(1,128)S(1)} %copy-done.8, f32[128,128]{1,0:T(8,128)S(1)} %copy-done.4, bf16[128,1024]{1,0:T(8,128)(2,1)S(1)} %copy-done.2, bf16[128,1024]{1,0:T(8,128)(2,1)S(1)} %copy-done.5, ...), custom_call_target="tpu_custom_call" | custom-call | flops 1 | bytes 1 | tf_op jit(solution)/shard_map/early/pallas_call | solution.py:300
  26.8 4.2 %collective-permute-done.6.refs_4_ = bf16[4,2,16,1024]{3,2,1,0:T(8,128)(2,1)S(1)} collective-permute-done((bf16[4,2,16,1024]{3,2,1,0:T(8,128)(2,1)S(1)}, bf16[4,2,16,1024]{3,2,1,0:T(8,128)(2,1)S(1)}, u32[]{:S(2)}, u32[]{:S(2)}) %collective-permute-start.6) | collective-permute-done | bytes 262176 | tf_op jit(solution)/shard_map/ppermute | solution.py:439
  31.0 0.5 collective-permute-start.11
  31.5 1.9 %collective-permute-done.5.refs_6_ = bf16[4,2,16,1024]{3,2,1,0:T(8,128)(2,1)S(1)} collective-permute-done((bf16[4,2,16,1024]{3,2,1,0:T(8,128)(2,1)S(1)}, bf16[4,2,16,1024]{3,2,1,0:T(8,128)(2,1)S(1)}, u32[]{:S(2)}, u32[]{:S(2)}) %collective-permute-start.5) | collective-permute-done | bytes 262176 | tf_op jit(solution)/shard_map/ppermute | solution.py:436
  33.4 1.5 %collective-permute-done.14.refs_7_ = bf16[4,2,16,1024]{3,2,1,0:T(8,128)(2,1)S(1)} collective-permute-done((bf16[4,2,16,1024]{3,2,1,0:T(8,128)(2,1)S(1)}, bf16[4,2,16,1024]{3,2,1,0:T(8,128)(2,1)S(1)}, u32[]{:S(2)}, u32[]{:S(2)}) %collective-permute-start.14) | collective-permute-done | bytes 262176 | tf_op jit(solution)/shard_map/ppermute | solution.py:442
  34.9 3.0 %late.1 = (bf16[128,1024]{1,0:T(8,128)(2,1)S(1)}, bf16[64,1536]{1,0:T(8,128)(2,1)S(1)}, bf16[64,1536]{1,0:T(8,128)(2,1)S(1)}) custom-call(s32[64]{0:T(128)S(1)} %pad_add_fusion.table_ref, f32[128,128]{1,0:T(8,128)S(1)} %copy-done.4, bf16[128,1024]{1,0:T(8,128)(2,1)S(1)} %copy-done.2, f32[128,1024]{1,0:T(8,128)S(1)} %get-tuple-element.52.mixed_ref, ...), custom_call_target="tpu_custom_call" | custom-call | flops 1 | bytes 1 | tf_op jit(solution)/shard_map/late/pallas_call | solution.py:321
  37.9 1.6 %collective-permute-start.17 = (bf16[64,1536]{1,0:T(8,128)(2,1)S(1)}, bf16[64,1536]{1,0:T(8,128)(2,1)S(1)}, u32[]{:S(2)}, u32[]{:S(2)}) collective-permute-start(bf16[64,1536]{1,0:T(8,128)(2,1)S(1)} %get-tuple-element.64), channel_id=1, source_target_pairs={{0,1},{1,0},{2,3},{3,2},{4,5},{5,4},{6,7},{7,6},{8,9},{9,8},{10,11... | collective-permute-start | bytes 589832 | tf_op jit(solution)/shard_map/ppermute | solution.py:500
  39.5 0.6 %project.2 = (bf16[64,1280]{1,0:T(8,128)(2,1)S(1)}, bf16[64,1280]{1,0:T(8,128)(2,1)S(1)}) custom-call(bf16[128,1024]{1,0:T(8,128)(2,1)S(1)} %get-tuple-element.59.context_ref, bf16[1024,4096]{1,0:T(8,128)(2,1)S(1)} %stage.1.weight_ref), custom_call_target="tpu_custom_call" | custom-call | flops 1 | bytes 1 | tf_op jit(solution)/shard_map/project/pallas_call | solution.py:343
  40.1 0.6 %collective-permute-start.16 = (bf16[64,1280]{1,0:T(8,128)(2,1)S(1)}, bf16[64,1280]{1,0:T(8,128)(2,1)S(1)}, u32[]{:S(2)}, u32[]{:S(2)}) collective-permute-start(bf16[64,1280]{1,0:T(8,128)(2,1)S(1)} %get-tuple-element.63), channel_id=1, source_target_pairs={{0,1},{1,0},{2,3},{3,2},{4,5},{5,4},{6,7},{7,6},{8,9},{9,8},{10,11... | collective-permute-start | bytes 491528 | tf_op jit(solution)/shard_map/ppermute | solution.py:500
  40.7 0.5 %project.3 = (bf16[64,1280]{1,0:T(8,128)(2,1)S(1)}, bf16[64,1280]{1,0:T(8,128)(2,1)S(1)}) custom-call(bf16[128,1024]{1,0:T(8,128)(2,1)S(1)} %get-tuple-element.59.context_ref, bf16[1024,4096]{1,0:T(8,128)(2,1)S(1)} %stage.1.weight_ref), custom_call_target="tpu_custom_call" | custom-call | flops 1 | bytes 1 | tf_op jit(solution)/shard_map/project/pallas_call | solution.py:343
  41.2 1.6 %collective-permute-start.15 = (bf16[64,1280]{1,0:T(8,128)(2,1)S(1)}, bf16[64,1280]{1,0:T(8,128)(2,1)S(1)}, u32[]{:S(2)}, u32[]{:S(2)}) collective-permute-start(bf16[64,1280]{1,0:T(8,128)(2,1)S(1)} %get-tuple-element.62), channel_id=1, source_target_pairs={{0,1},{1,0},{2,3},{3,2},{4,5},{5,4},{6,7},{7,6},{8,9},{9,8},{10,11... | collective-permute-start | bytes 491528 | tf_op jit(solution)/shard_map/ppermute | solution.py:500
  42.8 0.2 base.1.base_ref
  43.0 2.8 %collective-permute-done.17.refs_0_ = bf16[64,1536]{1,0:T(8,128)(2,1)S(1)} collective-permute-done((bf16[64,1536]{1,0:T(8,128)(2,1)S(1)}, bf16[64,1536]{1,0:T(8,128)(2,1)S(1)}, u32[]{:S(2)}, u32[]{:S(2)}) %collective-permute-start.17) | collective-permute-done | bytes 196640 | tf_op jit(solution)/shard_map/ppermute | solution.py:500
  45.8 0.7 %finish.3.refs_1_ = bf16[64,4096]{1,0:T(8,128)(2,1)} custom-call(f32[64,4096]{1,0:T(8,128)S(1)} %base.1.base_ref, bf16[64,1536]{1,0:T(8,128)(2,1)S(1)} %collective-permute-done.17.refs_0_), custom_call_target="tpu_custom_call" | custom-call | flops 1 | bytes 1 | tf_op jit(solution)/shard_map/finish/pallas_call | solution.py:407
  46.5 2.8 %collective-permute-done.16.refs_0_ = bf16[64,1280]{1,0:T(8,128)(2,1)S(1)} collective-permute-done((bf16[64,1280]{1,0:T(8,128)(2,1)S(1)}, bf16[64,1280]{1,0:T(8,128)(2,1)S(1)}, u32[]{:S(2)}, u32[]{:S(2)}) %collective-permute-start.16) | collective-permute-done | bytes 163872 | tf_op jit(solution)/shard_map/ppermute | solution.py:500
  49.3 0.7 %finish.4.refs_1_ = bf16[64,4096]{1,0:T(8,128)(2,1)} custom-call(f32[64,4096]{1,0:T(8,128)S(1)} %base.1.base_ref, bf16[64,1280]{1,0:T(8,128)(2,1)S(1)} %collective-permute-done.16.refs_0_, bf16[64,4096]{1,0:T(8,128)(2,1)} %finish.3.refs_1_), custom_call_target="tpu_custom_call", output_to_operand_aliasing={{}: (2, {})} | custom-call | flops 1 | bytes 1 | tf_op jit(solution)/shard_map/finish/pallas_call | solution.py:407
  50.0 2.0 %collective-permute-done.15.refs_0_ = bf16[64,1280]{1,0:T(8,128)(2,1)S(1)} collective-permute-done((bf16[64,1280]{1,0:T(8,128)(2,1)S(1)}, bf16[64,1280]{1,0:T(8,128)(2,1)S(1)}, u32[]{:S(2)}, u32[]{:S(2)}) %collective-permute-start.15) | collective-permute-done | bytes 163872 | tf_op jit(solution)/shard_map/ppermute | solution.py:500
  52.0 0.7 %finish.5 = bf16[64,4096]{1,0:T(8,128)(2,1)} custom-call(f32[64,4096]{1,0:T(8,128)S(1)} %base.1.base_ref, bf16[64,1280]{1,0:T(8,128)(2,1)S(1)} %collective-permute-done.15.refs_0_, bf16[64,4096]{1,0:T(8,128)(2,1)} %finish.4.refs_1_), custom_call_target="tpu_custom_call", output_to_operand_aliasing={{}: (2, {})} | custom-call | flops 1 | bytes 1 | tf_op jit(solution)/shard_map/finish/pallas_call | solution.py:407
  (39 shorter events, 0.4 us)
Async XLA Ops:
  0.6 14.2 %copy-start = (s32[16,16,2]{1,2,0:T(2,128)S(1)}, s32[16,16,2]{1,2,0:T(2,128)}, u32[]{:S(2)}) copy-start(s32[16,16,2]{1,2,0:T(2,128)} %param.13) | copy-start | bytes 6148
  0.6 11.7 %collective-permute-start.1 = (bf16[4,2,16,1024]{3,2,1,0:T(8,128)(2,1)}, bf16[4,2,16,1024]{3,2,1,0:T(8,128)(2,1)S(1)}, u32[]{:S(2)}, u32[]{:S(2)}) collective-permute-start(bf16[4,2,16,1024]{3,2,1,0:T(8,128)(2,1)} %pool_ref.1), channel_id=1, source_target_pairs={{0,8},{2,10},{4,12},{6,14},{8,16},{10,18},{12,20},{14,22},{16,24},... | collective-permute-start | bytes 786440 | tf_op jit(solution)/shard_map/ppermute | solution.py:436
  3.7 8.7 %collective-permute-start.2 = (bf16[4,2,16,1024]{3,2,1,0:T(8,128)(2,1)}, bf16[4,2,16,1024]{3,2,1,0:T(8,128)(2,1)S(1)}, u32[]{:S(2)}, u32[]{:S(2)}) collective-permute-start(bf16[4,2,16,1024]{3,2,1,0:T(8,128)(2,1)} %pool_ref.1), channel_id=1, source_target_pairs={{0,4},{2,6},{4,0},{6,2},{8,12},{10,14},{12,8},{14,10},{16,20},{18,... | collective-permute-start | bytes 786440 | tf_op jit(solution)/shard_map/ppermute | solution.py:439
  8.8 11.0 %collective-permute-start = (bf16[4,2,16,1024]{3,2,1,0:T(8,128)(2,1)}, bf16[4,2,16,1024]{3,2,1,0:T(8,128)(2,1)S(1)}, u32[]{:S(2)}, u32[]{:S(2)}) collective-permute-start(bf16[4,2,16,1024]{3,2,1,0:T(8,128)(2,1)} %pool_ref.1), channel_id=1, source_target_pairs={{0,24},{2,26},{4,28},{6,30},{8,0},{10,2},{12,4},{14,6},{16,8},{18,... | collective-permute-start | bytes 786440 | tf_op jit(solution)/shard_map/ppermute | solution.py:436
  12.4 8.1 %collective-permute-start.3 = (bf16[4,2,16,1024]{3,2,1,0:T(8,128)(2,1)S(1)}, bf16[4,2,16,1024]{3,2,1,0:T(8,128)(2,1)S(1)}, u32[]{:S(2)}, u32[]{:S(2)}) collective-permute-start(bf16[4,2,16,1024]{3,2,1,0:T(8,128)(2,1)S(1)} %collective-permute-done.1.refs_2_), channel_id=1, source_target_pairs={{0,4},{2,6},{4,0},{6,2},{8,12},{10,14},{12,8},{14,10},{16,20},{18,... | collective-permute-start | bytes 786440 | tf_op jit(solution)/shard_map/ppermute | solution.py:439
  14.0 10.2 %collective-permute-start.4 = (bf16[4,2,16,1024]{3,2,1,0:T(8,128)(2,1)S(1)}, bf16[4,2,16,1024]{3,2,1,0:T(8,128)(2,1)S(1)}, u32[]{:S(2)}, u32[]{:S(2)}) collective-permute-start(bf16[4,2,16,1024]{3,2,1,0:T(8,128)(2,1)S(1)} %collective-permute-done.1.refs_2_), channel_id=1, source_target_pairs={{0,8},{2,10},{4,12},{6,14},{8,16},{10,18},{12,20},{14,22},{16,24},... | collective-permute-start | bytes 786440 | tf_op jit(solution)/shard_map/ppermute | solution.py:436
  14.8 10.2 %collective-permute-start.7 = (bf16[4,2,16,1024]{3,2,1,0:T(8,128)(2,1)}, bf16[4,2,16,1024]{3,2,1,0:T(8,128)(2,1)S(1)}, u32[]{:S(2)}, u32[]{:S(2)}) collective-permute-start(bf16[4,2,16,1024]{3,2,1,0:T(8,128)(2,1)} %pool_ref.1), channel_id=1, source_target_pairs={{0,2},{2,0},{4,6},{6,4},{8,10},{10,8},{12,14},{14,12},{16,18},{18,... | collective-permute-start | bytes 786440 | tf_op jit(solution)/shard_map/ppermute | solution.py:442
  15.7 3.4 %copy-start.1 = (bf16[1024,4096]{1,0:T(8,128)(2,1)S(1)}, bf16[1024,4096]{1,0:T(8,128)(2,1)}, u32[]{:S(2)}) copy-start(bf16[1024,4096]{1,0:T(8,128)(2,1)} %source_ref) | copy-start | bytes 25165828
  19.1 6.0 %copy-start.2 = (bf16[128,1024]{1,0:T(8,128)(2,1)S(1)}, bf16[128,1024]{1,0:T(8,128)(2,1)}, u32[]{:S(2)}) copy-start(bf16[128,1024]{1,0:T(8,128)(2,1)} %get-tuple-element.41.query_ref) | copy-start | bytes 786436
  19.1 6.0 %copy-start.4 = (f32[128,128]{1,0:T(8,128)S(1)}, f32[128,128]{1,0:T(8,128)}, u32[]{:S(2)}) copy-start(f32[128,128]{1,0:T(8,128)} %get-tuple-element.40.column_ref) | copy-start | bytes 196612
  19.1 6.0 %copy-start.5 = (bf16[128,1024]{1,0:T(8,128)(2,1)S(1)}, bf16[128,1024]{1,0:T(8,128)(2,1)}, u32[]{:S(2)}) copy-start(bf16[128,1024]{1,0:T(8,128)(2,1)} %get-tuple-element.46.key_ref) | copy-start | bytes 786436
  19.1 6.0 %copy-start.6 = (bf16[128,1024]{1,0:T(8,128)(2,1)S(1)}, bf16[128,1024]{1,0:T(8,128)(2,1)}, u32[]{:S(2)}) copy-start(bf16[128,1024]{1,0:T(8,128)(2,1)} %get-tuple-element.47.value_ref) | copy-start | bytes 786436
  19.1 6.0 %copy-start.7 = (bf16[4,2,16,1024]{3,2,1,0:T(8,128)(2,1)S(1)}, bf16[4,2,16,1024]{3,2,1,0:T(8,128)(2,1)}, u32[]{:S(2)}) copy-start(bf16[4,2,16,1024]{3,2,1,0:T(8,128)(2,1)} %get-tuple-element.48.refs_0_) | copy-start | bytes 786436
  19.1 6.0 %copy-start.8 = (s32[1,128]{1,0:T(1,128)S(1)}, s32[1,128]{1,0:T(1,128)}, u32[]{:S(2)}) copy-start(s32[1,128]{1,0:T(1,128)} %segments_ref.3) | copy-start | bytes 1540
  19.8 5.3 %collective-permute-start.9 = (bf16[4,2,16,1024]{3,2,1,0:T(8,128)(2,1)S(1)}, bf16[4,2,16,1024]{3,2,1,0:T(8,128)(2,1)S(1)}, u32[]{:S(2)}, u32[]{:S(2)}) collective-permute-start(bf16[4,2,16,1024]{3,2,1,0:T(8,128)(2,1)S(1)} %collective-permute-done.refs_4_), channel_id=1, source_target_pairs={{0,2},{2,0},{4,6},{6,4},{8,10},{10,8},{12,14},{14,12},{16,18},{18,... | collective-permute-start | bytes 786440 | tf_op jit(solution)/shard_map/ppermute | solution.py:442
  20.4 4.7 %collective-permute-start.10 = (bf16[4,2,16,1024]{3,2,1,0:T(8,128)(2,1)S(1)}, bf16[4,2,16,1024]{3,2,1,0:T(8,128)(2,1)S(1)}, u32[]{:S(2)}, u32[]{:S(2)}) collective-permute-start(bf16[4,2,16,1024]{3,2,1,0:T(8,128)(2,1)S(1)} %collective-permute-done.2.refs_6_), channel_id=1, source_target_pairs={{0,2},{2,0},{4,6},{6,4},{8,10},{10,8},{12,14},{14,12},{16,18},{18,... | collective-permute-start | bytes 786440 | tf_op jit(solution)/shard_map/ppermute | solution.py:442
  20.5 4.7 %collective-permute-start.8 = (bf16[4,2,16,1024]{3,2,1,0:T(8,128)(2,1)S(1)}, bf16[4,2,16,1024]{3,2,1,0:T(8,128)(2,1)S(1)}, u32[]{:S(2)}, u32[]{:S(2)}) collective-permute-start(bf16[4,2,16,1024]{3,2,1,0:T(8,128)(2,1)S(1)} %collective-permute-done.1.refs_2_), channel_id=1, source_target_pairs={{0,2},{2,0},{4,6},{6,4},{8,10},{10,8},{12,14},{14,12},{16,18},{18,... | collective-permute-start | bytes 786440 | tf_op jit(solution)/shard_map/ppermute | solution.py:442
  24.2 6.7 %collective-permute-start.6 = (bf16[4,2,16,1024]{3,2,1,0:T(8,128)(2,1)S(1)}, bf16[4,2,16,1024]{3,2,1,0:T(8,128)(2,1)S(1)}, u32[]{:S(2)}, u32[]{:S(2)}) collective-permute-start(bf16[4,2,16,1024]{3,2,1,0:T(8,128)(2,1)S(1)} %collective-permute-done.refs_4_), channel_id=1, source_target_pairs={{0,4},{2,6},{4,0},{6,2},{8,12},{10,14},{12,8},{14,10},{16,20},{18,... | collective-permute-start | bytes 786440 | tf_op jit(solution)/shard_map/ppermute | solution.py:439
  25.0 8.4 %collective-permute-start.5 = (bf16[4,2,16,1024]{3,2,1,0:T(8,128)(2,1)S(1)}, bf16[4,2,16,1024]{3,2,1,0:T(8,128)(2,1)S(1)}, u32[]{:S(2)}, u32[]{:S(2)}) collective-permute-start(bf16[4,2,16,1024]{3,2,1,0:T(8,128)(2,1)S(1)} %collective-permute-done.3.refs_2_), channel_id=1, source_target_pairs={{0,8},{2,10},{4,12},{6,14},{8,16},{10,18},{12,20},{14,22},{16,24},... | collective-permute-start | bytes 786440 | tf_op jit(solution)/shard_map/ppermute | solution.py:436
  30.9 2.5 %collective-permute-start.13 = (bf16[4,2,16,1024]{3,2,1,0:T(8,128)(2,1)S(1)}, bf16[4,2,16,1024]{3,2,1,0:T(8,128)(2,1)S(1)}, u32[]{:S(2)}, u32[]{:S(2)}) collective-permute-start(bf16[4,2,16,1024]{3,2,1,0:T(8,128)(2,1)S(1)} %collective-permute-done.6.refs_4_), channel_id=1, source_target_pairs={{0,2},{2,0},{4,6},{6,4},{8,10},{10,8},{12,14},{14,12},{16,18},{18,... | collective-permute-start | bytes 786440 | tf_op jit(solution)/shard_map/ppermute | solution.py:442
  31.0 2.5 %collective-permute-start.11 = (bf16[4,2,16,1024]{3,2,1,0:T(8,128)(2,1)S(1)}, bf16[4,2,16,1024]{3,2,1,0:T(8,128)(2,1)S(1)}, u32[]{:S(2)}, u32[]{:S(2)}) collective-permute-start(bf16[4,2,16,1024]{3,2,1,0:T(8,128)(2,1)S(1)} %collective-permute-done.4.refs_0_), channel_id=1, source_target_pairs={{0,2},{2,0},{4,6},{6,4},{8,10},{10,8},{12,14},{14,12},{16,18},{18,... | collective-permute-start | bytes 786440 | tf_op jit(solution)/shard_map/ppermute | solution.py:442
  31.5 2.0 %collective-permute-start.12 = (bf16[4,2,16,1024]{3,2,1,0:T(8,128)(2,1)S(1)}, bf16[4,2,16,1024]{3,2,1,0:T(8,128)(2,1)S(1)}, u32[]{:S(2)}, u32[]{:S(2)}) collective-permute-start(bf16[4,2,16,1024]{3,2,1,0:T(8,128)(2,1)S(1)} %collective-permute-done.3.refs_2_), channel_id=1, source_target_pairs={{0,2},{2,0},{4,6},{6,4},{8,10},{10,8},{12,14},{14,12},{16,18},{18,... | collective-permute-start | bytes 786440 | tf_op jit(solution)/shard_map/ppermute | solution.py:442
  33.4 1.5 %collective-permute-start.14 = (bf16[4,2,16,1024]{3,2,1,0:T(8,128)(2,1)S(1)}, bf16[4,2,16,1024]{3,2,1,0:T(8,128)(2,1)S(1)}, u32[]{:S(2)}, u32[]{:S(2)}) collective-permute-start(bf16[4,2,16,1024]{3,2,1,0:T(8,128)(2,1)S(1)} %collective-permute-done.5.refs_6_), channel_id=1, source_target_pairs={{0,2},{2,0},{4,6},{6,4},{8,10},{10,8},{12,14},{14,12},{16,18},{18,... | collective-permute-start | bytes 786440 | tf_op jit(solution)/shard_map/ppermute | solution.py:442
  37.9 7.8 %collective-permute-start.17 = (bf16[64,1536]{1,0:T(8,128)(2,1)S(1)}, bf16[64,1536]{1,0:T(8,128)(2,1)S(1)}, u32[]{:S(2)}, u32[]{:S(2)}) collective-permute-start(bf16[64,1536]{1,0:T(8,128)(2,1)S(1)} %get-tuple-element.64), channel_id=1, source_target_pairs={{0,1},{1,0},{2,3},{3,2},{4,5},{5,4},{6,7},{7,6},{8,9},{9,8},{10,11... | collective-permute-start | bytes 589832 | tf_op jit(solution)/shard_map/ppermute | solution.py:500
  39.5 3.3 %copy-start.9 = (bf16[4096]{0:T(1024)(128)(2,1)S(1)}, bf16[4096]{0:T(1024)(128)(2,1)}, u32[]{:S(2)}) copy-start(bf16[4096]{0:T(1024)(128)(2,1)} %param.17) | copy-start | bytes 24580
  39.5 3.3 %copy-start.3 = (bf16[64,4096]{1,0:T(8,128)(2,1)S(1)}, bf16[64,4096]{1,0:T(8,128)(2,1)}, u32[]{:S(2)}) copy-start(bf16[64,4096]{1,0:T(8,128)(2,1)} %residual_ref.1) | copy-start | bytes 1572868
  40.1 9.2 %collective-permute-start.16 = (bf16[64,1280]{1,0:T(8,128)(2,1)S(1)}, bf16[64,1280]{1,0:T(8,128)(2,1)S(1)}, u32[]{:S(2)}, u32[]{:S(2)}) collective-permute-start(bf16[64,1280]{1,0:T(8,128)(2,1)S(1)} %get-tuple-element.63), channel_id=1, source_target_pairs={{0,1},{1,0},{2,3},{3,2},{4,5},{5,4},{6,7},{7,6},{8,9},{9,8},{10,11... | collective-permute-start | bytes 491528 | tf_op jit(solution)/shard_map/ppermute | solution.py:500
  41.2 10.8 %collective-permute-start.15 = (bf16[64,1280]{1,0:T(8,128)(2,1)S(1)}, bf16[64,1280]{1,0:T(8,128)(2,1)S(1)}, u32[]{:S(2)}, u32[]{:S(2)}) collective-permute-start(bf16[64,1280]{1,0:T(8,128)(2,1)S(1)} %get-tuple-element.62), channel_id=1, source_target_pairs={{0,1},{1,0},{2,3},{3,2},{4,5},{5,4},{6,7},{7,6},{8,9},{9,8},{10,11... | collective-permute-start | bytes 491528 | tf_op jit(solution)/shard_map/ppermute | solution.py:500

commit v4 on v3

--- a/solution.py
+++ b/solution.py
@@ -194,13 +194,14 @@
 
 
 def weigh(weights, values):
-    return jnp.dot(weights.astype(jnp.bfloat16), values, preferred_element_type=jnp.float32)
+    both = jnp.concatenate([values, jnp.ones_like(values)], axis=1)
+    return jnp.dot(weights.astype(jnp.bfloat16), both, preferred_element_type=jnp.float32)
 
 
 def early_kernel(
     blocks, per_peer, table_ref, segments_ref, column_ref, query_ref, key_ref, value_ref, *refs
 ):
-    *block_refs, mixed_ref, stats_ref, keys, values = refs
+    *block_refs, mixed_ref, tops_ref, keys, values = refs
     tokens, feature = query_ref.shape
     key_owner = gather_pages(blocks, block_refs, per_peer, table_ref, keys, values)
     segments = segments_ref[...].astype(jnp.float32)
@@ -209,7 +210,6 @@
     cols = lax.broadcasted_iota(jnp.int32, (tokens, tokens), 1)
     see_new = (column == segments) & (cols <= rows)
     see_old = column == key_owner
-    lane = lax.broadcasted_iota(jnp.int32, (tokens, HD), 1)
     heads = [slice(start, start + HD) for start in range(0, feature, HD)]
     new = [scores_of(query_ref[:, head], key_ref[:, head], see_new) for head in heads]
     old = [scores_of(query_ref[:, head], keys[:, head], see_old) for head in heads]
@@ -219,18 +219,12 @@
     ]
     new = [jnp.exp2(a - top) for a, top in zip(new, peaks)]
     old = [jnp.exp2(b - top) for b, top in zip(old, peaks)]
-    tops = totals = jnp.zeros((tokens, HD), jnp.float32)
     for number, head in enumerate(heads):
-        total = jnp.sum(new[number], axis=1, keepdims=True) + jnp.sum(
-            old[number], axis=1, keepdims=True
-        )
-        mixed_ref[:, head] = weigh(new[number], value_ref[:, head]) + weigh(
+        pair = slice(2 * head.start, 2 * head.stop)
+        mixed_ref[:, pair] = weigh(new[number], value_ref[:, head]) + weigh(
             old[number], values[:, head]
         )
-        tops = jnp.where(lane == number, peaks[number], tops)
-        totals = jnp.where(lane == number, total, totals)
-    stats_ref[:, :HD] = tops
-    stats_ref[:, HD:] = totals
+        tops_ref[:, head] = jnp.broadcast_to(peaks[number], (tokens, HD))
 
 
 def late_kernel(
@@ -241,7 +235,7 @@
     column_ref,
     query_ref,
     mixed_ref,
-    stats_ref,
+    tops_ref,
     weight_ref,
     *refs,
 ):
@@ -254,19 +248,21 @@
     seen = column_ref[:, :1] == key_owner
     heads = [slice(start, start + HD) for start in range(0, feature, HD)]
     scores = [scores_of(query_ref[:, head], keys[:, head], seen) for head in heads]
-    before = [stats_ref[:, number : number + 1] for number in range(len(heads))]
+    before = [tops_ref[:, head] for head in heads]
     tops = [
         jnp.maximum(old, jnp.max(new, axis=1, keepdims=True)) for old, new in zip(before, scores)
     ]
-    weights = [jnp.exp2(new - top) for new, top in zip(scores, tops)]
+    repeat = scores[0].shape[1] // HD
+    weights = [
+        jnp.exp2(new - jnp.concatenate([top] * repeat, axis=1)) for new, top in zip(scores, tops)
+    ]
     fades = [jnp.exp2(old - top) for old, top in zip(before, tops)]
     added = [weigh(part, values[:, head]) for part, head in zip(weights, heads)]
     for number, head in enumerate(heads):
-        total = stats_ref[:, HD + number : HD + number + 1] * fades[number] + jnp.sum(
-            weights[number], axis=1, keepdims=True
-        )
-        mixed = mixed_ref[:, head] * fades[number] + added[number]
-        context_ref[:, head] = (mixed * pl.reciprocal(total)).astype(jnp.bfloat16)
+        pair = 2 * head.start
+        total = mixed_ref[:, pair + HD : pair + 2 * HD] * fades[number] + added[number][:, HD:]
+        mixed = mixed_ref[:, pair : pair + HD] * fades[number] + added[number][:, :HD]
+        context_ref[:, head] = (mixed / total).astype(jnp.bfloat16)
     project_rows(peers, 0, context_ref, weight_ref, product, own_ref, send_refs)
 
 
@@ -300,8 +296,8 @@
     return pl.pallas_call(
         functools.partial(early_kernel, layout, per_peer),
         out_shape=(
+            jax.ShapeDtypeStruct((tokens, 2 * feature), jnp.float32),
             jax.ShapeDtypeStruct((tokens, feature), jnp.float32),
-            jax.ShapeDtypeStruct((tokens, 2 * HD), jnp.float32),
         ),
         grid=(1,),
         in_specs=[smem()] + [vmem()] * (5 + len(parts)),
@@ -314,7 +310,7 @@
 
 
 def attend_late(
-    layout, table, column, rot_query, mixed, stats, weight, parts, per_peer, peers, width
+    layout, table, column, rot_query, mixed, tops, weight, parts, per_peer, peers, width
 ):
     tokens, feature = rot_query.shape
     prefix = len(layout) * per_peer * parts[0].shape[2]
@@ -330,7 +326,7 @@
         compiler_params=params(LATE_LIMIT),
         cost_estimate=cheap(),
         name="late",
-    )(table, column, rot_query, mixed, stats, weight, *parts)
+    )(table, column, rot_query, mixed, tops, weight, *parts)
 
 
 def project_kernel(peers, first, context_ref, weight_ref, own_ref, *refs):
@@ -446,18 +442,15 @@
     wide = out_weight.shape[1] // 16
     widths = (6 * wide, 5 * wide, 5 * wide)
     after = lax.optimization_barrier
-    ups = {0: kv_pool, 1: along(kv_pool, 1)}
+    ups = {0: kv_pool, 1: along(kv_pool, 1), -1: along(kv_pool, -1)}
     over = {0: across(kv_pool)}
     column, rot_query, rot_key, value, pool, key_cache = rotate(page, segment_ids, page_owner, queries, new_kv, kv_pool)
-    later, column = after((kv_pool, column))
-    ups[-1] = along(later, -1)
     ups[1], column = after((ups[1], column))
     for step in range(2, reach):
         ups[step] = along(ups[step - 1], 1)
         ups[-step] = along(ups[1 - step], -1)
     ups[reach] = along(ups[reach - 1], 1)
-    first, out_weight = after((ups[1], out_weight))
-    first, over[0] = after((first, over[0]))
+    first, over[0], out_weight = after((ups[1], over[0], out_weight))
     over[1] = across(first)
     weight = stage(out_weight)
     ups[-1], weight, table = after((ups[-1], weight, table))
@@ -477,7 +470,7 @@
             elif (flip, shift) != (2, last):
                 layout += [(-shift, flip, (0,)), (-shift, flip ^ 1, (0,))]
                 parts += [pool if values is kv_pool else values, beside(values)]
-    mixed, stats = attend_early(
+    mixed, tops = attend_early(
         layout, table, segment_ids, column, rot_query, rot_key, value, parts, per_peer
     )
     far = along(crossed, 1)
@@ -489,7 +482,7 @@
         layout += [(-shift, flip, (0,)), (-shift, flip ^ 1, (0,))]
         parts += [values, beside(values)]
     context, *share = attend_late(
-        layout, table, column, rot_query, mixed, stats, weight, parts, per_peer, peers, widths[0]
+        layout, table, column, rot_query, mixed, tops, weight, parts, per_peer, peers, widths[0]
     )
     owns, received = [share[0]], []
     start = 0

time: 52.9 us -> 51.7 us (0.977)
  Pallas kernels: 12.2 us -> 11.1 us
    ppermute x3, waiting for transfers between devices: 4.16 us -> 3.04 us  [across(): return lax.ppermute(values, 'dp', [(d, d ^ 2) for d in range(groups)])]
    pallas_call x1, Pallas kernels: 2.99 us -> 1.96 us  [attend_late(): pl.pallas_call(functools.partial(late_kernel, layout, per_peer, peers), o...]
    ppermute x4, waiting for transfers between devices: 6.52 us -> 7.45 us  [along(): return lax.ppermute(values, 'dp', pairs)]
where the time goes in v4:
time: 51.7 us; the launch traced here: 51.5 us
  waiting for transfers between devices  19.6 us (38%)
  starting transfers between devices  15.6 us (30%)
  Pallas kernels  11.1 us (21%)
  local copies, waits for them, and re-layouts  3.61 us (7%)
  between operations  0.83 us (2%)
  other arithmetic  0.73 us (1%)
    ppermute x3, waiting for transfers between devices, body(): pieces.append(lax.ppermute(values, 'tensor', pairs))  7.58 us
    ppermute x4, waiting for transfers between devices, along(): return lax.ppermute(values, 'dp', pairs)  7.45 us
    ppermute x4, starting transfers between devices, along(): return lax.ppermute(values, 'dp', pairs)  6.46 us
    ppermute x3, starting transfers between devices, across(): return lax.ppermute(values, 'dp', [(d, d ^ 2) for d in range(groups)])  3.82 us
    ppermute x3, starting transfers between devices, body(): pieces.append(lax.ppermute(values, 'tensor', pairs))  3.71 us
    pallas_call x1, Pallas kernels, rotate(): pl.pallas_call(functools.partial(rotary_kernel, page), out_shape=(jax.Sha...  3.57 us
    unnamed x20, local copies, waits for them, and re-layouts  3.42 us
    ppermute x3, waiting for transfers between devices, across(): return lax.ppermute(values, 'dp', [(d, d ^ 2) for d in range(groups)])  3.04 us
  transfers between devices with their start and end apart: 18, of which 8 were waited for; matrix products, arithmetic and copies ran while one was open for 2% of the time, Pallas kernels for 16%

profile of v4, /device:TPU:0, one launch (start us, length us, event | category | flops | bytes accessed | tf_op | source)
XLA Modules:
  0.0 51.5 jit_solution(2825939739199590067)
XLA Ops:
  0.6 3.1 %collective-permute-start.1 = (bf16[4,2,16,1024]{3,2,1,0:T(8,128)(2,1)}, bf16[4,2,16,1024]{3,2,1,0:T(8,128)(2,1)S(1)}, u32[]{:S(2)}, u32[]{:S(2)}) collective-permute-start(bf16[4,2,16,1024]{3,2,1,0:T(8,128)(2,1)} %pool_ref.1), channel_id=1, source_target_pairs={{0,8},{2,10},{4,12},{6,14},{8,16},{10,18},{12,20},{14,22},{16,24},... | collective-permute-start | bytes 786440 | tf_op jit(solution)/shard_map/ppermute | solution.py:432
  3.7 1.5 %collective-permute-start.2 = (bf16[4,2,16,1024]{3,2,1,0:T(8,128)(2,1)}, bf16[4,2,16,1024]{3,2,1,0:T(8,128)(2,1)S(1)}, u32[]{:S(2)}, u32[]{:S(2)}) collective-permute-start(bf16[4,2,16,1024]{3,2,1,0:T(8,128)(2,1)} %pool_ref.1), channel_id=1, source_target_pairs={{0,4},{2,6},{4,0},{6,2},{8,12},{10,14},{12,8},{14,10},{16,20},{18,... | collective-permute-start | bytes 786440 | tf_op jit(solution)/shard_map/ppermute | solution.py:435
  5.2 2.2 %collective-permute-start = (bf16[4,2,16,1024]{3,2,1,0:T(8,128)(2,1)}, bf16[4,2,16,1024]{3,2,1,0:T(8,128)(2,1)S(1)}, u32[]{:S(2)}, u32[]{:S(2)}) collective-permute-start(bf16[4,2,16,1024]{3,2,1,0:T(8,128)(2,1)} %pool_ref.1), channel_id=1, source_target_pairs={{0,24},{2,26},{4,28},{6,30},{8,0},{10,2},{12,4},{14,6},{16,8},{18,... | collective-permute-start | bytes 786440 | tf_op jit(solution)/shard_map/ppermute | solution.py:432
  7.5 3.6 %rotary.1 = (f32[128,128]{1,0:T(8,128)}, bf16[128,1024]{1,0:T(8,128)(2,1)}, bf16[128,1024]{1,0:T(8,128)(2,1)}, bf16[128,1024]{1,0:T(8,128)(2,1)}, bf16[4,2,16,10...) custom-call(s32[1,128]{1,0:T(1,128)} %segments_ref.3, s32[1,32]{1,0:T(1,128)} %owners_ref.1, bf16[128,1024]{1,0:T(8,128)(2,1)} %query_ref.1, ...), custom_call_target="tpu_custom_call" | custom-call | flops 1 | bytes 1 | tf_op jit(solution)/shard_map/rotary/pallas_call | solution.py:99
  11.1 2.1 %collective-permute-done.1.refs_2_ = bf16[4,2,16,1024]{3,2,1,0:T(8,128)(2,1)S(1)} collective-permute-done((bf16[4,2,16,1024]{3,2,1,0:T(8,128)(2,1)}, bf16[4,2,16,1024]{3,2,1,0:T(8,128)(2,1)S(1)}, u32[]{:S(2)}, u32[]{:S(2)}) %collective-permute-start.1) | collective-permute-done | bytes 262176 | tf_op jit(solution)/shard_map/ppermute | solution.py:432
  13.1 1.8 %collective-permute-start.3 = (bf16[4,2,16,1024]{3,2,1,0:T(8,128)(2,1)S(1)}, bf16[4,2,16,1024]{3,2,1,0:T(8,128)(2,1)S(1)}, u32[]{:S(2)}, u32[]{:S(2)}) collective-permute-start(bf16[4,2,16,1024]{3,2,1,0:T(8,128)(2,1)S(1)} %collective-permute-done.1.refs_2_), channel_id=1, source_target_pairs={{0,4},{2,6},{4,0},{6,2},{8,12},{10,14},{12,8},{14,10},{16,20},{18,... | collective-permute-start | bytes 786440 | tf_op jit(solution)/shard_map/ppermute | solution.py:435
  15.1 0.7 %pad_add_fusion.table_ref = s32[64]{0:T(128)S(1)} fusion(s32[32]{0:T(128)} %bitcast.1, s32[32]{0:T(128)S(1)} %reshape.15), kind=kLoop, calls=%fused_computation | loop fusion | flops 64 | bytes 512 | tf_op jit(solution)/shard_map/concatenate | solution.py:441
  15.8 3.4 %copy-done.1 = bf16[1024,4096]{1,0:T(8,128)(2,1)S(1)} copy-done((bf16[1024,4096]{1,0:T(8,128)(2,1)S(1)}, bf16[1024,4096]{1,0:T(8,128)(2,1)}, u32[]{:S(2)}) %copy-start.1) | copy-done | bytes 8388632
  19.3 0.7 %stage.1.weight_ref = bf16[1024,4096]{1,0:T(8,128)(2,1)S(1)} custom-call(bf16[1024,4096]{1,0:T(8,128)(2,1)S(1)} %copy-done.1), custom_call_target="tpu_custom_call" | custom-call | flops 1 | bytes 1 | tf_op jit(solution)/shard_map/stage/pallas_call | solution.py:141
  19.9 0.6 %collective-permute-start.9 = (bf16[4,2,16,1024]{3,2,1,0:T(8,128)(2,1)S(1)}, bf16[4,2,16,1024]{3,2,1,0:T(8,128)(2,1)S(1)}, u32[]{:S(2)}, u32[]{:S(2)}) collective-permute-start(bf16[4,2,16,1024]{3,2,1,0:T(8,128)(2,1)S(1)} %collective-permute-done.refs_4_), channel_id=1, source_target_pairs={{0,2},{2,0},{4,6},{6,4},{8,10},{10,8},{12,14},{14,12},{16,18},{18,... | collective-permute-start | bytes 786440 | tf_op jit(solution)/shard_map/ppermute | solution.py:438
  20.6 0.4 collective-permute-start.8
  21.0 3.5 %collective-permute-done.4.refs_0_ = bf16[4,2,16,1024]{3,2,1,0:T(8,128)(2,1)S(1)} collective-permute-done((bf16[4,2,16,1024]{3,2,1,0:T(8,128)(2,1)S(1)}, bf16[4,2,16,1024]{3,2,1,0:T(8,128)(2,1)S(1)}, u32[]{:S(2)}, u32[]{:S(2)}) %collective-permute-start.4) | collective-permute-done | bytes 262176 | tf_op jit(solution)/shard_map/ppermute | solution.py:432
  24.5 0.5 %collective-permute-start.6 = (bf16[4,2,16,1024]{3,2,1,0:T(8,128)(2,1)S(1)}, bf16[4,2,16,1024]{3,2,1,0:T(8,128)(2,1)S(1)}, u32[]{:S(2)}, u32[]{:S(2)}) collective-permute-start(bf16[4,2,16,1024]{3,2,1,0:T(8,128)(2,1)S(1)} %collective-permute-done.refs_4_), channel_id=1, source_target_pairs={{0,4},{2,6},{4,0},{6,2},{8,12},{10,14},{12,8},{14,10},{16,20},{18,... | collective-permute-start | bytes 786440 | tf_op jit(solution)/shard_map/ppermute | solution.py:435
  25.1 1.1 %collective-permute-start.5 = (bf16[4,2,16,1024]{3,2,1,0:T(8,128)(2,1)S(1)}, bf16[4,2,16,1024]{3,2,1,0:T(8,128)(2,1)S(1)}, u32[]{:S(2)}, u32[]{:S(2)}) collective-permute-start(bf16[4,2,16,1024]{3,2,1,0:T(8,128)(2,1)S(1)} %collective-permute-done.3.refs_2_), channel_id=1, source_target_pairs={{0,8},{2,10},{4,12},{6,14},{8,16},{10,18},{12,20},{14,22},{16,24},... | collective-permute-start | bytes 786440 | tf_op jit(solution)/shard_map/ppermute | solution.py:432
  26.3 1.6 %early.1 = (f32[128,2048]{1,0:T(8,128)S(1)}, f32[128,1024]{1,0:T(8,128)S(1)}) custom-call(s32[64]{0:T(128)S(1)} %pad_add_fusion.table_ref, s32[1,128]{1,0:T(1,128)S(1)} %copy-done.8, f32[128,128]{1,0:T(8,128)S(1)} %copy-done.4, bf16[128,1024]{1,0:T(8,128)(2,1)S(1)} %copy-done.2, bf16[128,1024]{1,0:T(8,128)(2,1)S(1)} %copy-done.5, ...), custom_call_target="tpu_custom_call" | custom-call | flops 1 | bytes 1 | tf_op jit(solution)/shard_map/early/pallas_call | solution.py:296
  27.9 3.0 %collective-permute-done.6.refs_4_ = bf16[4,2,16,1024]{3,2,1,0:T(8,128)(2,1)S(1)} collective-permute-done((bf16[4,2,16,1024]{3,2,1,0:T(8,128)(2,1)S(1)}, bf16[4,2,16,1024]{3,2,1,0:T(8,128)(2,1)S(1)}, u32[]{:S(2)}, u32[]{:S(2)}) %collective-permute-start.6) | collective-permute-done | bytes 262176 | tf_op jit(solution)/shard_map/ppermute | solution.py:435
  30.9 0.5 collective-permute-start.11
  31.4 1.8 %collective-permute-done.5.refs_6_ = bf16[4,2,16,1024]{3,2,1,0:T(8,128)(2,1)S(1)} collective-permute-done((bf16[4,2,16,1024]{3,2,1,0:T(8,128)(2,1)S(1)}, bf16[4,2,16,1024]{3,2,1,0:T(8,128)(2,1)S(1)}, u32[]{:S(2)}, u32[]{:S(2)}) %collective-permute-start.5) | collective-permute-done | bytes 262176 | tf_op jit(solution)/shard_map/ppermute | solution.py:432
  33.3 1.5 %collective-permute-done.14.refs_7_ = bf16[4,2,16,1024]{3,2,1,0:T(8,128)(2,1)S(1)} collective-permute-done((bf16[4,2,16,1024]{3,2,1,0:T(8,128)(2,1)S(1)}, bf16[4,2,16,1024]{3,2,1,0:T(8,128)(2,1)S(1)}, u32[]{:S(2)}, u32[]{:S(2)}) %collective-permute-start.14) | collective-permute-done | bytes 262176 | tf_op jit(solution)/shard_map/ppermute | solution.py:438
  34.8 2.0 %late.1 = (bf16[128,1024]{1,0:T(8,128)(2,1)S(1)}, bf16[64,1536]{1,0:T(8,128)(2,1)S(1)}, bf16[64,1536]{1,0:T(8,128)(2,1)S(1)}) custom-call(s32[64]{0:T(128)S(1)} %pad_add_fusion.table_ref, f32[128,128]{1,0:T(8,128)S(1)} %copy-done.4, bf16[128,1024]{1,0:T(8,128)(2,1)S(1)} %copy-done.2, f32[128,2048]{1,0:T(8,128)S(1)} %get-tuple-element.46.mixed_ref, ...), custom_call_target="tpu_custom_call" | custom-call | flops 1 | bytes 1 | tf_op jit(solution)/shard_map/late/pallas_call | solution.py:317
  36.8 1.5 %collective-permute-start.17 = (bf16[64,1536]{1,0:T(8,128)(2,1)S(1)}, bf16[64,1536]{1,0:T(8,128)(2,1)S(1)}, u32[]{:S(2)}, u32[]{:S(2)}) collective-permute-start(bf16[64,1536]{1,0:T(8,128)(2,1)S(1)} %get-tuple-element.58), channel_id=1, source_target_pairs={{0,1},{1,0},{2,3},{3,2},{4,5},{5,4},{6,7},{7,6},{8,9},{9,8},{10,11... | collective-permute-start | bytes 589832 | tf_op jit(solution)/shard_map/ppermute | solution.py:493
  38.3 0.6 %project.2 = (bf16[64,1280]{1,0:T(8,128)(2,1)S(1)}, bf16[64,1280]{1,0:T(8,128)(2,1)S(1)}) custom-call(bf16[128,1024]{1,0:T(8,128)(2,1)S(1)} %get-tuple-element.53.context_ref, bf16[1024,4096]{1,0:T(8,128)(2,1)S(1)} %stage.1.weight_ref), custom_call_target="tpu_custom_call" | custom-call | flops 1 | bytes 1 | tf_op jit(solution)/shard_map/project/pallas_call | solution.py:339
  38.9 0.6 %collective-permute-start.16 = (bf16[64,1280]{1,0:T(8,128)(2,1)S(1)}, bf16[64,1280]{1,0:T(8,128)(2,1)S(1)}, u32[]{:S(2)}, u32[]{:S(2)}) collective-permute-start(bf16[64,1280]{1,0:T(8,128)(2,1)S(1)} %get-tuple-element.57), channel_id=1, source_target_pairs={{0,1},{1,0},{2,3},{3,2},{4,5},{5,4},{6,7},{7,6},{8,9},{9,8},{10,11... | collective-permute-start | bytes 491528 | tf_op jit(solution)/shard_map/ppermute | solution.py:493
  39.5 0.5 %project.3 = (bf16[64,1280]{1,0:T(8,128)(2,1)S(1)}, bf16[64,1280]{1,0:T(8,128)(2,1)S(1)}) custom-call(bf16[128,1024]{1,0:T(8,128)(2,1)S(1)} %get-tuple-element.53.context_ref, bf16[1024,4096]{1,0:T(8,128)(2,1)S(1)} %stage.1.weight_ref), custom_call_target="tpu_custom_call" | custom-call | flops 1 | bytes 1 | tf_op jit(solution)/shard_map/project/pallas_call | solution.py:339
  40.0 1.6 %collective-permute-start.15 = (bf16[64,1280]{1,0:T(8,128)(2,1)S(1)}, bf16[64,1280]{1,0:T(8,128)(2,1)S(1)}, u32[]{:S(2)}, u32[]{:S(2)}) collective-permute-start(bf16[64,1280]{1,0:T(8,128)(2,1)S(1)} %get-tuple-element.56), channel_id=1, source_target_pairs={{0,1},{1,0},{2,3},{3,2},{4,5},{5,4},{6,7},{7,6},{8,9},{9,8},{10,11... | collective-permute-start | bytes 491528 | tf_op jit(solution)/shard_map/ppermute | solution.py:493
  41.6 0.2 base.1.base_ref
  41.8 2.8 %collective-permute-done.17.refs_0_ = bf16[64,1536]{1,0:T(8,128)(2,1)S(1)} collective-permute-done((bf16[64,1536]{1,0:T(8,128)(2,1)S(1)}, bf16[64,1536]{1,0:T(8,128)(2,1)S(1)}, u32[]{:S(2)}, u32[]{:S(2)}) %collective-permute-start.17) | collective-permute-done | bytes 196640 | tf_op jit(solution)/shard_map/ppermute | solution.py:493
  44.6 0.7 %finish.3.refs_1_ = bf16[64,4096]{1,0:T(8,128)(2,1)} custom-call(f32[64,4096]{1,0:T(8,128)S(1)} %base.1.base_ref, bf16[64,1536]{1,0:T(8,128)(2,1)S(1)} %collective-permute-done.17.refs_0_), custom_call_target="tpu_custom_call" | custom-call | flops 1 | bytes 1 | tf_op jit(solution)/shard_map/finish/pallas_call | solution.py:403
  45.3 2.8 %collective-permute-done.16.refs_0_ = bf16[64,1280]{1,0:T(8,128)(2,1)S(1)} collective-permute-done((bf16[64,1280]{1,0:T(8,128)(2,1)S(1)}, bf16[64,1280]{1,0:T(8,128)(2,1)S(1)}, u32[]{:S(2)}, u32[]{:S(2)}) %collective-permute-start.16) | collective-permute-done | bytes 163872 | tf_op jit(solution)/shard_map/ppermute | solution.py:493
  48.1 0.7 %finish.4.refs_1_ = bf16[64,4096]{1,0:T(8,128)(2,1)} custom-call(f32[64,4096]{1,0:T(8,128)S(1)} %base.1.base_ref, bf16[64,1280]{1,0:T(8,128)(2,1)S(1)} %collective-permute-done.16.refs_0_, bf16[64,4096]{1,0:T(8,128)(2,1)} %finish.3.refs_1_), custom_call_target="tpu_custom_call", output_to_operand_aliasing={{}: (2, {})} | custom-call | flops 1 | bytes 1 | tf_op jit(solution)/shard_map/finish/pallas_call | solution.py:403
  48.8 2.0 %collective-permute-done.15.refs_0_ = bf16[64,1280]{1,0:T(8,128)(2,1)S(1)} collective-permute-done((bf16[64,1280]{1,0:T(8,128)(2,1)S(1)}, bf16[64,1280]{1,0:T(8,128)(2,1)S(1)}, u32[]{:S(2)}, u32[]{:S(2)}) %collective-permute-start.15) | collective-permute-done | bytes 163872 | tf_op jit(solution)/shard_map/ppermute | solution.py:493
  50.8 0.7 %finish.5 = bf16[64,4096]{1,0:T(8,128)(2,1)} custom-call(f32[64,4096]{1,0:T(8,128)S(1)} %base.1.base_ref, bf16[64,1280]{1,0:T(8,128)(2,1)S(1)} %collective-permute-done.15.refs_0_, bf16[64,4096]{1,0:T(8,128)(2,1)} %finish.4.refs_1_), custom_call_target="tpu_custom_call", output_to_operand_aliasing={{}: (2, {})} | custom-call | flops 1 | bytes 1 | tf_op jit(solution)/shard_map/finish/pallas_call | solution.py:403
  (39 shorter events, 0.4 us)
Async XLA Ops:
  0.6 14.3 %copy-start = (s32[16,16,2]{1,2,0:T(2,128)S(1)}, s32[16,16,2]{1,2,0:T(2,128)}, u32[]{:S(2)}) copy-start(s32[16,16,2]{1,2,0:T(2,128)} %param.13) | copy-start | bytes 6148
  0.6 12.5 %collective-permute-start.1 = (bf16[4,2,16,1024]{3,2,1,0:T(8,128)(2,1)}, bf16[4,2,16,1024]{3,2,1,0:T(8,128)(2,1)S(1)}, u32[]{:S(2)}, u32[]{:S(2)}) collective-permute-start(bf16[4,2,16,1024]{3,2,1,0:T(8,128)(2,1)} %pool_ref.1), channel_id=1, source_target_pairs={{0,8},{2,10},{4,12},{6,14},{8,16},{10,18},{12,20},{14,22},{16,24},... | collective-permute-start | bytes 786440 | tf_op jit(solution)/shard_map/ppermute | solution.py:432
  3.7 9.4 %collective-permute-start.2 = (bf16[4,2,16,1024]{3,2,1,0:T(8,128)(2,1)}, bf16[4,2,16,1024]{3,2,1,0:T(8,128)(2,1)S(1)}, u32[]{:S(2)}, u32[]{:S(2)}) collective-permute-start(bf16[4,2,16,1024]{3,2,1,0:T(8,128)(2,1)} %pool_ref.1), channel_id=1, source_target_pairs={{0,4},{2,6},{4,0},{6,2},{8,12},{10,14},{12,8},{14,10},{16,20},{18,... | collective-permute-start | bytes 786440 | tf_op jit(solution)/shard_map/ppermute | solution.py:435
  5.2 14.7 %collective-permute-start = (bf16[4,2,16,1024]{3,2,1,0:T(8,128)(2,1)}, bf16[4,2,16,1024]{3,2,1,0:T(8,128)(2,1)S(1)}, u32[]{:S(2)}, u32[]{:S(2)}) collective-permute-start(bf16[4,2,16,1024]{3,2,1,0:T(8,128)(2,1)} %pool_ref.1), channel_id=1, source_target_pairs={{0,24},{2,26},{4,28},{6,30},{8,0},{10,2},{12,4},{14,6},{16,8},{18,... | collective-permute-start | bytes 786440 | tf_op jit(solution)/shard_map/ppermute | solution.py:432
  13.1 7.4 %collective-permute-start.3 = (bf16[4,2,16,1024]{3,2,1,0:T(8,128)(2,1)S(1)}, bf16[4,2,16,1024]{3,2,1,0:T(8,128)(2,1)S(1)}, u32[]{:S(2)}, u32[]{:S(2)}) collective-permute-start(bf16[4,2,16,1024]{3,2,1,0:T(8,128)(2,1)S(1)} %collective-permute-done.1.refs_2_), channel_id=1, source_target_pairs={{0,4},{2,6},{4,0},{6,2},{8,12},{10,14},{12,8},{14,10},{16,20},{18,... | collective-permute-start | bytes 786440 | tf_op jit(solution)/shard_map/ppermute | solution.py:435
  14.9 9.6 %collective-permute-start.4 = (bf16[4,2,16,1024]{3,2,1,0:T(8,128)(2,1)S(1)}, bf16[4,2,16,1024]{3,2,1,0:T(8,128)(2,1)S(1)}, u32[]{:S(2)}, u32[]{:S(2)}) collective-permute-start(bf16[4,2,16,1024]{3,2,1,0:T(8,128)(2,1)S(1)} %collective-permute-done.1.refs_2_), channel_id=1, source_target_pairs={{0,8},{2,10},{4,12},{6,14},{8,16},{10,18},{12,20},{14,22},{16,24},... | collective-permute-start | bytes 786440 | tf_op jit(solution)/shard_map/ppermute | solution.py:432
  14.9 10.2 %collective-permute-start.7 = (bf16[4,2,16,1024]{3,2,1,0:T(8,128)(2,1)}, bf16[4,2,16,1024]{3,2,1,0:T(8,128)(2,1)S(1)}, u32[]{:S(2)}, u32[]{:S(2)}) collective-permute-start(bf16[4,2,16,1024]{3,2,1,0:T(8,128)(2,1)} %pool_ref.1), channel_id=1, source_target_pairs={{0,2},{2,0},{4,6},{6,4},{8,10},{10,8},{12,14},{14,12},{16,18},{18,... | collective-permute-start | bytes 786440 | tf_op jit(solution)/shard_map/ppermute | solution.py:438
  15.8 3.4 %copy-start.1 = (bf16[1024,4096]{1,0:T(8,128)(2,1)S(1)}, bf16[1024,4096]{1,0:T(8,128)(2,1)}, u32[]{:S(2)}) copy-start(bf16[1024,4096]{1,0:T(8,128)(2,1)} %source_ref) | copy-start | bytes 25165828
  19.2 7.0 %copy-start.2 = (bf16[128,1024]{1,0:T(8,128)(2,1)S(1)}, bf16[128,1024]{1,0:T(8,128)(2,1)}, u32[]{:S(2)}) copy-start(bf16[128,1024]{1,0:T(8,128)(2,1)} %get-tuple-element.36.query_ref) | copy-start | bytes 786436
  19.2 7.0 %copy-start.4 = (f32[128,128]{1,0:T(8,128)S(1)}, f32[128,128]{1,0:T(8,128)}, u32[]{:S(2)}) copy-start(f32[128,128]{1,0:T(8,128)} %get-tuple-element.35.column_ref) | copy-start | bytes 196612
  19.2 7.0 %copy-start.5 = (bf16[128,1024]{1,0:T(8,128)(2,1)S(1)}, bf16[128,1024]{1,0:T(8,128)(2,1)}, u32[]{:S(2)}) copy-start(bf16[128,1024]{1,0:T(8,128)(2,1)} %get-tuple-element.40.key_ref) | copy-start | bytes 786436
  19.2 7.0 %copy-start.6 = (bf16[128,1024]{1,0:T(8,128)(2,1)S(1)}, bf16[128,1024]{1,0:T(8,128)(2,1)}, u32[]{:S(2)}) copy-start(bf16[128,1024]{1,0:T(8,128)(2,1)} %get-tuple-element.41.value_ref) | copy-start | bytes 786436
  19.2 7.0 %copy-start.7 = (bf16[4,2,16,1024]{3,2,1,0:T(8,128)(2,1)S(1)}, bf16[4,2,16,1024]{3,2,1,0:T(8,128)(2,1)}, u32[]{:S(2)}) copy-start(bf16[4,2,16,1024]{3,2,1,0:T(8,128)(2,1)} %get-tuple-element.42.refs_0_) | copy-start | bytes 786436
  19.2 7.0 %copy-start.8 = (s32[1,128]{1,0:T(1,128)S(1)}, s32[1,128]{1,0:T(1,128)}, u32[]{:S(2)}) copy-start(s32[1,128]{1,0:T(1,128)} %segments_ref.3) | copy-start | bytes 1540
  19.9 6.3 %collective-permute-start.9 = (bf16[4,2,16,1024]{3,2,1,0:T(8,128)(2,1)S(1)}, bf16[4,2,16,1024]{3,2,1,0:T(8,128)(2,1)S(1)}, u32[]{:S(2)}, u32[]{:S(2)}) collective-permute-start(bf16[4,2,16,1024]{3,2,1,0:T(8,128)(2,1)S(1)} %collective-permute-done.refs_4_), channel_id=1, source_target_pairs={{0,2},{2,0},{4,6},{6,4},{8,10},{10,8},{12,14},{14,12},{16,18},{18,... | collective-permute-start | bytes 786440 | tf_op jit(solution)/shard_map/ppermute | solution.py:438
  20.5 5.7 %collective-permute-start.10 = (bf16[4,2,16,1024]{3,2,1,0:T(8,128)(2,1)S(1)}, bf16[4,2,16,1024]{3,2,1,0:T(8,128)(2,1)S(1)}, u32[]{:S(2)}, u32[]{:S(2)}) collective-permute-start(bf16[4,2,16,1024]{3,2,1,0:T(8,128)(2,1)S(1)} %collective-permute-done.2.refs_6_), channel_id=1, source_target_pairs={{0,2},{2,0},{4,6},{6,4},{8,10},{10,8},{12,14},{14,12},{16,18},{18,... | collective-permute-start | bytes 786440 | tf_op jit(solution)/shard_map/ppermute | solution.py:438
  20.6 5.6 %collective-permute-start.8 = (bf16[4,2,16,1024]{3,2,1,0:T(8,128)(2,1)S(1)}, bf16[4,2,16,1024]{3,2,1,0:T(8,128)(2,1)S(1)}, u32[]{:S(2)}, u32[]{:S(2)}) collective-permute-start(bf16[4,2,16,1024]{3,2,1,0:T(8,128)(2,1)S(1)} %collective-permute-done.1.refs_2_), channel_id=1, source_target_pairs={{0,2},{2,0},{4,6},{6,4},{8,10},{10,8},{12,14},{14,12},{16,18},{18,... | collective-permute-start | bytes 786440 | tf_op jit(solution)/shard_map/ppermute | solution.py:438
  24.5 6.4 %collective-permute-start.6 = (bf16[4,2,16,1024]{3,2,1,0:T(8,128)(2,1)S(1)}, bf16[4,2,16,1024]{3,2,1,0:T(8,128)(2,1)S(1)}, u32[]{:S(2)}, u32[]{:S(2)}) collective-permute-start(bf16[4,2,16,1024]{3,2,1,0:T(8,128)(2,1)S(1)} %collective-permute-done.refs_4_), channel_id=1, source_target_pairs={{0,4},{2,6},{4,0},{6,2},{8,12},{10,14},{12,8},{14,10},{16,20},{18,... | collective-permute-start | bytes 786440 | tf_op jit(solution)/shard_map/ppermute | solution.py:435
  25.1 8.2 %collective-permute-start.5 = (bf16[4,2,16,1024]{3,2,1,0:T(8,128)(2,1)S(1)}, bf16[4,2,16,1024]{3,2,1,0:T(8,128)(2,1)S(1)}, u32[]{:S(2)}, u32[]{:S(2)}) collective-permute-start(bf16[4,2,16,1024]{3,2,1,0:T(8,128)(2,1)S(1)} %collective-permute-done.3.refs_2_), channel_id=1, source_target_pairs={{0,8},{2,10},{4,12},{6,14},{8,16},{10,18},{12,20},{14,22},{16,24},... | collective-permute-start | bytes 786440 | tf_op jit(solution)/shard_map/ppermute | solution.py:432
  30.9 2.4 %collective-permute-start.13 = (bf16[4,2,16,1024]{3,2,1,0:T(8,128)(2,1)S(1)}, bf16[4,2,16,1024]{3,2,1,0:T(8,128)(2,1)S(1)}, u32[]{:S(2)}, u32[]{:S(2)}) collective-permute-start(bf16[4,2,16,1024]{3,2,1,0:T(8,128)(2,1)S(1)} %collective-permute-done.6.refs_4_), channel_id=1, source_target_pairs={{0,2},{2,0},{4,6},{6,4},{8,10},{10,8},{12,14},{14,12},{16,18},{18,... | collective-permute-start | bytes 786440 | tf_op jit(solution)/shard_map/ppermute | solution.py:438
  30.9 2.4 %collective-permute-start.11 = (bf16[4,2,16,1024]{3,2,1,0:T(8,128)(2,1)S(1)}, bf16[4,2,16,1024]{3,2,1,0:T(8,128)(2,1)S(1)}, u32[]{:S(2)}, u32[]{:S(2)}) collective-permute-start(bf16[4,2,16,1024]{3,2,1,0:T(8,128)(2,1)S(1)} %collective-permute-done.4.refs_0_), channel_id=1, source_target_pairs={{0,2},{2,0},{4,6},{6,4},{8,10},{10,8},{12,14},{14,12},{16,18},{18,... | collective-permute-start | bytes 786440 | tf_op jit(solution)/shard_map/ppermute | solution.py:438
  31.4 1.9 %collective-permute-start.12 = (bf16[4,2,16,1024]{3,2,1,0:T(8,128)(2,1)S(1)}, bf16[4,2,16,1024]{3,2,1,0:T(8,128)(2,1)S(1)}, u32[]{:S(2)}, u32[]{:S(2)}) collective-permute-start(bf16[4,2,16,1024]{3,2,1,0:T(8,128)(2,1)S(1)} %collective-permute-done.3.refs_2_), channel_id=1, source_target_pairs={{0,2},{2,0},{4,6},{6,4},{8,10},{10,8},{12,14},{14,12},{16,18},{18,... | collective-permute-start | bytes 786440 | tf_op jit(solution)/shard_map/ppermute | solution.py:438
  33.3 1.5 %collective-permute-start.14 = (bf16[4,2,16,1024]{3,2,1,0:T(8,128)(2,1)S(1)}, bf16[4,2,16,1024]{3,2,1,0:T(8,128)(2,1)S(1)}, u32[]{:S(2)}, u32[]{:S(2)}) collective-permute-start(bf16[4,2,16,1024]{3,2,1,0:T(8,128)(2,1)S(1)} %collective-permute-done.5.refs_6_), channel_id=1, source_target_pairs={{0,2},{2,0},{4,6},{6,4},{8,10},{10,8},{12,14},{14,12},{16,18},{18,... | collective-permute-start | bytes 786440 | tf_op jit(solution)/shard_map/ppermute | solution.py:438
  36.8 7.8 %collective-permute-start.17 = (bf16[64,1536]{1,0:T(8,128)(2,1)S(1)}, bf16[64,1536]{1,0:T(8,128)(2,1)S(1)}, u32[]{:S(2)}, u32[]{:S(2)}) collective-permute-start(bf16[64,1536]{1,0:T(8,128)(2,1)S(1)} %get-tuple-element.58), channel_id=1, source_target_pairs={{0,1},{1,0},{2,3},{3,2},{4,5},{5,4},{6,7},{7,6},{8,9},{9,8},{10,11... | collective-permute-start | bytes 589832 | tf_op jit(solution)/shard_map/ppermute | solution.py:493
  38.3 3.3 %copy-start.9 = (bf16[4096]{0:T(1024)(128)(2,1)S(1)}, bf16[4096]{0:T(1024)(128)(2,1)}, u32[]{:S(2)}) copy-start(bf16[4096]{0:T(1024)(128)(2,1)} %param.17) | copy-start | bytes 24580
  38.3 3.3 %copy-start.3 = (bf16[64,4096]{1,0:T(8,128)(2,1)S(1)}, bf16[64,4096]{1,0:T(8,128)(2,1)}, u32[]{:S(2)}) copy-start(bf16[64,4096]{1,0:T(8,128)(2,1)} %residual_ref.1) | copy-start | bytes 1572868
  38.9 9.2 %collective-permute-start.16 = (bf16[64,1280]{1,0:T(8,128)(2,1)S(1)}, bf16[64,1280]{1,0:T(8,128)(2,1)S(1)}, u32[]{:S(2)}, u32[]{:S(2)}) collective-permute-start(bf16[64,1280]{1,0:T(8,128)(2,1)S(1)} %get-tuple-element.57), channel_id=1, source_target_pairs={{0,1},{1,0},{2,3},{3,2},{4,5},{5,4},{6,7},{7,6},{8,9},{9,8},{10,11... | collective-permute-start | bytes 491528 | tf_op jit(solution)/shard_map/ppermute | solution.py:493
  40.0 10.8 %collective-permute-start.15 = (bf16[64,1280]{1,0:T(8,128)(2,1)S(1)}, bf16[64,1280]{1,0:T(8,128)(2,1)S(1)}, u32[]{:S(2)}, u32[]{:S(2)}) collective-permute-start(bf16[64,1280]{1,0:T(8,128)(2,1)S(1)} %get-tuple-element.56), channel_id=1, source_target_pairs={{0,1},{1,0},{2,3},{3,2},{4,5},{5,4},{6,7},{7,6},{8,9},{9,8},{10,11... | collective-permute-start | bytes 491528 | tf_op jit(solution)/shard_map/ppermute | solution.py:493

commit v5 on v4

--- a/solution.py
+++ b/solution.py
@@ -440,7 +440,7 @@
     wanted = lax.dynamic_index_in_dim(fetch_pages, group, axis=0, keepdims=False).reshape(-1)
     table = jnp.concatenate([wanted, page_owner.reshape(-1)])
     wide = out_weight.shape[1] // 16
-    widths = (6 * wide, 5 * wide, 5 * wide)
+    widths = (5 * wide, 4 * wide, 4 * wide, 3 * wide)
     after = lax.optimization_barrier
     ups = {0: kv_pool, 1: along(kv_pool, 1), -1: along(kv_pool, -1)}
     over = {0: across(kv_pool)}

time: 51.7 us -> 51.6 us (level)
  waiting for transfers between devices: 19.6 us -> 18 us
  Pallas kernels: 11.1 us -> 12 us
  starting transfers between devices: 15.6 us -> 16.2 us
    ppermute x3 -> x4, waiting for transfers between devices: 7.58 us -> 6.02 us  [body(): pieces.append(lax.ppermute(values, 'tensor', pairs))]
    pallas_call x3 -> x4, Pallas kernels: 2.15 us -> 2.76 us  [finish(): pl.pallas_call(functools.partial(finish_kernel, first, len(received)), ou...]
    ppermute x3 -> x4, starting transfers between devices: 3.71 us -> 4.32 us  [body(): pieces.append(lax.ppermute(values, 'tensor', pairs))]
    pallas_call x2 -> x3, Pallas kernels: 1.09 us -> 1.35 us  [project(): pl.pallas_call(functools.partial(project_kernel, peers, first), out_shape...]
  transfers between devices with their start and end apart: 18 -> 19, of which waited for: 8 -> 9; matrix products, arithmetic and copies ran while one was open for 2% -> 2% of each run, Pallas kernels for 16% -> 18%
where the time goes in v5:
time: 51.6 us; the launch traced here: 51.4 us
  waiting for transfers between devices  18 us (35%)
  starting transfers between devices  16.2 us (31%)
  Pallas kernels  12 us (23%)
  local copies, waits for them, and re-layouts  3.62 us (7%)
  between operations  0.85 us (2%)
  other arithmetic  0.73 us (1%)
    ppermute x4, waiting for transfers between devices, along(): return lax.ppermute(values, 'dp', pairs)  7.45 us
    ppermute x4, starting transfers between devices, along(): return lax.ppermute(values, 'dp', pairs)  6.46 us
    ppermute x4, waiting for transfers between devices, body(): pieces.append(lax.ppermute(values, 'tensor', pairs))  6.02 us
    ppermute x4, starting transfers between devices, body(): pieces.append(lax.ppermute(values, 'tensor', pairs))  4.32 us
    ppermute x3, starting transfers between devices, across(): return lax.ppermute(values, 'dp', [(d, d ^ 2) for d in range(groups)])  3.82 us
    pallas_call x1, Pallas kernels, rotate(): pl.pallas_call(functools.partial(rotary_kernel, page), out_shape=(jax.Sha...  3.56 us
    unnamed x20, local copies, waits for them, and re-layouts  3.43 us
    ppermute x3, waiting for transfers between devices, across(): return lax.ppermute(values, 'dp', [(d, d ^ 2) for d in range(groups)])  3.04 us
  transfers between devices with their start and end apart: 19, of which 9 were waited for; matrix products, arithmetic and copies ran while one was open for 2% of the time, Pallas kernels for 18%

profile of v5, /device:TPU:0, one launch (start us, length us, event | category | flops | bytes accessed | tf_op | source)
XLA Modules:
  0.0 51.4 jit_solution(14704236309110826722)
XLA Ops:
  0.6 3.1 %collective-permute-start.1 = (bf16[4,2,16,1024]{3,2,1,0:T(8,128)(2,1)}, bf16[4,2,16,1024]{3,2,1,0:T(8,128)(2,1)S(1)}, u32[]{:S(2)}, u32[]{:S(2)}) collective-permute-start(bf16[4,2,16,1024]{3,2,1,0:T(8,128)(2,1)} %pool_ref.1), channel_id=1, source_target_pairs={{0,8},{2,10},{4,12},{6,14},{8,16},{10,18},{12,20},{14,22},{16,24},... | collective-permute-start | bytes 786440 | tf_op jit(solution)/shard_map/ppermute | solution.py:432
  3.7 1.5 %collective-permute-start.2 = (bf16[4,2,16,1024]{3,2,1,0:T(8,128)(2,1)}, bf16[4,2,16,1024]{3,2,1,0:T(8,128)(2,1)S(1)}, u32[]{:S(2)}, u32[]{:S(2)}) collective-permute-start(bf16[4,2,16,1024]{3,2,1,0:T(8,128)(2,1)} %pool_ref.1), channel_id=1, source_target_pairs={{0,4},{2,6},{4,0},{6,2},{8,12},{10,14},{12,8},{14,10},{16,20},{18,... | collective-permute-start | bytes 786440 | tf_op jit(solution)/shard_map/ppermute | solution.py:435
  5.2 2.2 %collective-permute-start = (bf16[4,2,16,1024]{3,2,1,0:T(8,128)(2,1)}, bf16[4,2,16,1024]{3,2,1,0:T(8,128)(2,1)S(1)}, u32[]{:S(2)}, u32[]{:S(2)}) collective-permute-start(bf16[4,2,16,1024]{3,2,1,0:T(8,128)(2,1)} %pool_ref.1), channel_id=1, source_target_pairs={{0,24},{2,26},{4,28},{6,30},{8,0},{10,2},{12,4},{14,6},{16,8},{18,... | collective-permute-start | bytes 786440 | tf_op jit(solution)/shard_map/ppermute | solution.py:432
  7.5 3.6 %rotary.1 = (f32[128,128]{1,0:T(8,128)}, bf16[128,1024]{1,0:T(8,128)(2,1)}, bf16[128,1024]{1,0:T(8,128)(2,1)}, bf16[128,1024]{1,0:T(8,128)(2,1)}, bf16[4,2,16,10...) custom-call(s32[1,128]{1,0:T(1,128)} %segments_ref.3, s32[1,32]{1,0:T(1,128)} %owners_ref.1, bf16[128,1024]{1,0:T(8,128)(2,1)} %query_ref.1, ...), custom_call_target="tpu_custom_call" | custom-call | flops 1 | bytes 1 | tf_op jit(solution)/shard_map/rotary/pallas_call | solution.py:99
  11.1 2.1 %collective-permute-done.1.refs_2_ = bf16[4,2,16,1024]{3,2,1,0:T(8,128)(2,1)S(1)} collective-permute-done((bf16[4,2,16,1024]{3,2,1,0:T(8,128)(2,1)}, bf16[4,2,16,1024]{3,2,1,0:T(8,128)(2,1)S(1)}, u32[]{:S(2)}, u32[]{:S(2)}) %collective-permute-start.1) | collective-permute-done | bytes 262176 | tf_op jit(solution)/shard_map/ppermute | solution.py:432
  13.1 1.8 %collective-permute-start.3 = (bf16[4,2,16,1024]{3,2,1,0:T(8,128)(2,1)S(1)}, bf16[4,2,16,1024]{3,2,1,0:T(8,128)(2,1)S(1)}, u32[]{:S(2)}, u32[]{:S(2)}) collective-permute-start(bf16[4,2,16,1024]{3,2,1,0:T(8,128)(2,1)S(1)} %collective-permute-done.1.refs_2_), channel_id=1, source_target_pairs={{0,4},{2,6},{4,0},{6,2},{8,12},{10,14},{12,8},{14,10},{16,20},{18,... | collective-permute-start | bytes 786440 | tf_op jit(solution)/shard_map/ppermute | solution.py:435
  15.1 0.7 %pad_add_fusion.table_ref = s32[64]{0:T(128)S(1)} fusion(s32[32]{0:T(128)} %bitcast.1, s32[32]{0:T(128)S(1)} %reshape.15), kind=kLoop, calls=%fused_computation | loop fusion | flops 64 | bytes 512 | tf_op jit(solution)/shard_map/concatenate | solution.py:441
  15.8 3.4 %copy-done.1 = bf16[1024,4096]{1,0:T(8,128)(2,1)S(1)} copy-done((bf16[1024,4096]{1,0:T(8,128)(2,1)S(1)}, bf16[1024,4096]{1,0:T(8,128)(2,1)}, u32[]{:S(2)}) %copy-start.1) | copy-done | bytes 8388632
  19.3 0.7 %stage.1.weight_ref = bf16[1024,4096]{1,0:T(8,128)(2,1)S(1)} custom-call(bf16[1024,4096]{1,0:T(8,128)(2,1)S(1)} %copy-done.1), custom_call_target="tpu_custom_call" | custom-call | flops 1 | bytes 1 | tf_op jit(solution)/shard_map/stage/pallas_call | solution.py:141
  19.9 0.6 %collective-permute-start.9 = (bf16[4,2,16,1024]{3,2,1,0:T(8,128)(2,1)S(1)}, bf16[4,2,16,1024]{3,2,1,0:T(8,128)(2,1)S(1)}, u32[]{:S(2)}, u32[]{:S(2)}) collective-permute-start(bf16[4,2,16,1024]{3,2,1,0:T(8,128)(2,1)S(1)} %collective-permute-done.refs_4_), channel_id=1, source_target_pairs={{0,2},{2,0},{4,6},{6,4},{8,10},{10,8},{12,14},{14,12},{16,18},{18,... | collective-permute-start | bytes 786440 | tf_op jit(solution)/shard_map/ppermute | solution.py:438
  21.0 3.5 %collective-permute-done.4.refs_0_ = bf16[4,2,16,1024]{3,2,1,0:T(8,128)(2,1)S(1)} collective-permute-done((bf16[4,2,16,1024]{3,2,1,0:T(8,128)(2,1)S(1)}, bf16[4,2,16,1024]{3,2,1,0:T(8,128)(2,1)S(1)}, u32[]{:S(2)}, u32[]{:S(2)}) %collective-permute-start.4) | collective-permute-done | bytes 262176 | tf_op jit(solution)/shard_map/ppermute | solution.py:432
  24.5 0.5 %collective-permute-start.6 = (bf16[4,2,16,1024]{3,2,1,0:T(8,128)(2,1)S(1)}, bf16[4,2,16,1024]{3,2,1,0:T(8,128)(2,1)S(1)}, u32[]{:S(2)}, u32[]{:S(2)}) collective-permute-start(bf16[4,2,16,1024]{3,2,1,0:T(8,128)(2,1)S(1)} %collective-permute-done.refs_4_), channel_id=1, source_target_pairs={{0,4},{2,6},{4,0},{6,2},{8,12},{10,14},{12,8},{14,10},{16,20},{18,... | collective-permute-start | bytes 786440 | tf_op jit(solution)/shard_map/ppermute | solution.py:435
  25.1 1.1 %collective-permute-start.5 = (bf16[4,2,16,1024]{3,2,1,0:T(8,128)(2,1)S(1)}, bf16[4,2,16,1024]{3,2,1,0:T(8,128)(2,1)S(1)}, u32[]{:S(2)}, u32[]{:S(2)}) collective-permute-start(bf16[4,2,16,1024]{3,2,1,0:T(8,128)(2,1)S(1)} %collective-permute-done.3.refs_2_), channel_id=1, source_target_pairs={{0,8},{2,10},{4,12},{6,14},{8,16},{10,18},{12,20},{14,22},{16,24},... | collective-permute-start | bytes 786440 | tf_op jit(solution)/shard_map/ppermute | solution.py:432
  26.3 1.6 %early.1 = (f32[128,2048]{1,0:T(8,128)S(1)}, f32[128,1024]{1,0:T(8,128)S(1)}) custom-call(s32[64]{0:T(128)S(1)} %pad_add_fusion.table_ref, s32[1,128]{1,0:T(1,128)S(1)} %copy-done.8, f32[128,128]{1,0:T(8,128)S(1)} %copy-done.4, bf16[128,1024]{1,0:T(8,128)(2,1)S(1)} %copy-done.2, bf16[128,1024]{1,0:T(8,128)(2,1)S(1)} %copy-done.5, ...), custom_call_target="tpu_custom_call" | custom-call | flops 1 | bytes 1 | tf_op jit(solution)/shard_map/early/pallas_call | solution.py:296
  27.9 3.0 %collective-permute-done.6.refs_4_ = bf16[4,2,16,1024]{3,2,1,0:T(8,128)(2,1)S(1)} collective-permute-done((bf16[4,2,16,1024]{3,2,1,0:T(8,128)(2,1)S(1)}, bf16[4,2,16,1024]{3,2,1,0:T(8,128)(2,1)S(1)}, u32[]{:S(2)}, u32[]{:S(2)}) %collective-permute-start.6) | collective-permute-done | bytes 262176 | tf_op jit(solution)/shard_map/ppermute | solution.py:435
  30.9 0.5 collective-permute-start.11
  31.4 1.8 %collective-permute-done.5.refs_6_ = bf16[4,2,16,1024]{3,2,1,0:T(8,128)(2,1)S(1)} collective-permute-done((bf16[4,2,16,1024]{3,2,1,0:T(8,128)(2,1)S(1)}, bf16[4,2,16,1024]{3,2,1,0:T(8,128)(2,1)S(1)}, u32[]{:S(2)}, u32[]{:S(2)}) %collective-permute-start.5) | collective-permute-done | bytes 262176 | tf_op jit(solution)/shard_map/ppermute | solution.py:432
  33.3 1.5 %collective-permute-done.14.refs_7_ = bf16[4,2,16,1024]{3,2,1,0:T(8,128)(2,1)S(1)} collective-permute-done((bf16[4,2,16,1024]{3,2,1,0:T(8,128)(2,1)S(1)}, bf16[4,2,16,1024]{3,2,1,0:T(8,128)(2,1)S(1)}, u32[]{:S(2)}, u32[]{:S(2)}) %collective-permute-start.14) | collective-permute-done | bytes 262176 | tf_op jit(solution)/shard_map/ppermute | solution.py:438
  34.8 1.9 %late.1 = (bf16[128,1024]{1,0:T(8,128)(2,1)S(1)}, bf16[64,1280]{1,0:T(8,128)(2,1)S(1)}, bf16[64,1280]{1,0:T(8,128)(2,1)S(1)}) custom-call(s32[64]{0:T(128)S(1)} %pad_add_fusion.table_ref, f32[128,128]{1,0:T(8,128)S(1)} %copy-done.4, bf16[128,1024]{1,0:T(8,128)(2,1)S(1)} %copy-done.2, f32[128,2048]{1,0:T(8,128)S(1)} %get-tuple-element.48.mixed_ref, ...), custom_call_target="tpu_custom_call" | custom-call | flops 1 | bytes 1 | tf_op jit(solution)/shard_map/late/pallas_call | solution.py:317
  36.7 1.6 %collective-permute-start.18 = (bf16[64,1280]{1,0:T(8,128)(2,1)S(1)}, bf16[64,1280]{1,0:T(8,128)(2,1)S(1)}, u32[]{:S(2)}, u32[]{:S(2)}) collective-permute-start(bf16[64,1280]{1,0:T(8,128)(2,1)S(1)} %get-tuple-element.62), channel_id=1, source_target_pairs={{0,1},{1,0},{2,3},{3,2},{4,5},{5,4},{6,7},{7,6},{8,9},{9,8},{10,11... | collective-permute-start | bytes 491528 | tf_op jit(solution)/shard_map/ppermute | solution.py:493
  38.3 0.5 project.3
  38.8 0.6 %collective-permute-start.17 = (bf16[64,1024]{1,0:T(8,128)(2,1)S(1)}, bf16[64,1024]{1,0:T(8,128)(2,1)S(1)}, u32[]{:S(2)}, u32[]{:S(2)}) collective-permute-start(bf16[64,1024]{1,0:T(8,128)(2,1)S(1)} %get-tuple-element.61), channel_id=1, source_target_pairs={{0,1},{1,0},{2,3},{3,2},{4,5},{5,4},{6,7},{7,6},{8,9},{9,8},{10,11... | collective-permute-start | bytes 393224 | tf_op jit(solution)/shard_map/ppermute | solution.py:493
  39.8 1.6 %collective-permute-start.16 = (bf16[64,1024]{1,0:T(8,128)(2,1)S(1)}, bf16[64,1024]{1,0:T(8,128)(2,1)S(1)}, u32[]{:S(2)}, u32[]{:S(2)}) collective-permute-start(bf16[64,1024]{1,0:T(8,128)(2,1)S(1)} %get-tuple-element.60), channel_id=1, source_target_pairs={{0,1},{1,0},{2,3},{3,2},{4,5},{5,4},{6,7},{7,6},{8,9},{9,8},{10,11... | collective-permute-start | bytes 393224 | tf_op jit(solution)/shard_map/ppermute | solution.py:493
  41.8 0.6 %collective-permute-start.15 = (bf16[64,768]{1,0:T(8,128)(2,1)S(1)}, bf16[64,768]{1,0:T(8,128)(2,1)S(1)}, u32[]{:S(2)}, u32[]{:S(2)}) collective-permute-start(bf16[64,768]{1,0:T(8,128)(2,1)S(1)} %get-tuple-element.59), channel_id=1, source_target_pairs={{0,1},{1,0},{2,3},{3,2},{4,5},{5,4},{6,7},{7,6},{8,9},{9,8},{10,11... | collective-permute-start | bytes 294920 | tf_op jit(solution)/shard_map/ppermute | solution.py:493
  42.6 1.2 %collective-permute-done.18.refs_0_ = bf16[64,1280]{1,0:T(8,128)(2,1)S(1)} collective-permute-done((bf16[64,1280]{1,0:T(8,128)(2,1)S(1)}, bf16[64,1280]{1,0:T(8,128)(2,1)S(1)}, u32[]{:S(2)}, u32[]{:S(2)}) %collective-permute-start.18) | collective-permute-done | bytes 163872 | tf_op jit(solution)/shard_map/ppermute | solution.py:493
  43.8 0.7 %finish.4.refs_1_ = bf16[64,4096]{1,0:T(8,128)(2,1)} custom-call(f32[64,4096]{1,0:T(8,128)S(1)} %base.1.base_ref, bf16[64,1280]{1,0:T(8,128)(2,1)S(1)} %collective-permute-done.18.refs_0_), custom_call_target="tpu_custom_call" | custom-call | flops 1 | bytes 1 | tf_op jit(solution)/shard_map/finish/pallas_call | solution.py:403
  44.5 2.1 %collective-permute-done.17.refs_0_ = bf16[64,1024]{1,0:T(8,128)(2,1)S(1)} collective-permute-done((bf16[64,1024]{1,0:T(8,128)(2,1)S(1)}, bf16[64,1024]{1,0:T(8,128)(2,1)S(1)}, u32[]{:S(2)}, u32[]{:S(2)}) %collective-permute-start.17) | collective-permute-done | bytes 131104 | tf_op jit(solution)/shard_map/ppermute | solution.py:493
  46.6 0.7 %finish.5.refs_1_ = bf16[64,4096]{1,0:T(8,128)(2,1)} custom-call(f32[64,4096]{1,0:T(8,128)S(1)} %base.1.base_ref, bf16[64,1024]{1,0:T(8,128)(2,1)S(1)} %collective-permute-done.17.refs_0_, bf16[64,4096]{1,0:T(8,128)(2,1)} %finish.4.refs_1_), custom_call_target="tpu_custom_call", output_to_operand_aliasing={{}: (2, {})} | custom-call | flops 1 | bytes 1 | tf_op jit(solution)/shard_map/finish/pallas_call | solution.py:403
  47.3 2.1 %collective-permute-done.16.refs_0_ = bf16[64,1024]{1,0:T(8,128)(2,1)S(1)} collective-permute-done((bf16[64,1024]{1,0:T(8,128)(2,1)S(1)}, bf16[64,1024]{1,0:T(8,128)(2,1)S(1)}, u32[]{:S(2)}, u32[]{:S(2)}) %collective-permute-start.16) | collective-permute-done | bytes 131104 | tf_op jit(solution)/shard_map/ppermute | solution.py:493
  49.4 0.7 %finish.6.refs_1_ = bf16[64,4096]{1,0:T(8,128)(2,1)} custom-call(f32[64,4096]{1,0:T(8,128)S(1)} %base.1.base_ref, bf16[64,1024]{1,0:T(8,128)(2,1)S(1)} %collective-permute-done.16.refs_0_, bf16[64,4096]{1,0:T(8,128)(2,1)} %finish.5.refs_1_), custom_call_target="tpu_custom_call", output_to_operand_aliasing={{}: (2, {})} | custom-call | flops 1 | bytes 1 | tf_op jit(solution)/shard_map/finish/pallas_call | solution.py:403
  50.1 0.6 %collective-permute-done.15.refs_0_ = bf16[64,768]{1,0:T(8,128)(2,1)S(1)} collective-permute-done((bf16[64,768]{1,0:T(8,128)(2,1)S(1)}, bf16[64,768]{1,0:T(8,128)(2,1)S(1)}, u32[]{:S(2)}, u32[]{:S(2)}) %collective-permute-start.15) | collective-permute-done | bytes 98336 | tf_op jit(solution)/shard_map/ppermute | solution.py:493
  50.7 0.7 %finish.7 = bf16[64,4096]{1,0:T(8,128)(2,1)} custom-call(f32[64,4096]{1,0:T(8,128)S(1)} %base.1.base_ref, bf16[64,768]{1,0:T(8,128)(2,1)S(1)} %collective-permute-done.15.refs_0_, bf16[64,4096]{1,0:T(8,128)(2,1)} %finish.6.refs_1_), custom_call_target="tpu_custom_call", output_to_operand_aliasing={{}: (2, {})} | custom-call | flops 1 | bytes 1 | tf_op jit(solution)/shard_map/finish/pallas_call | solution.py:403
  (43 shorter events, 1.8 us)
Async XLA Ops:
  0.6 14.3 %copy-start = (s32[16,16,2]{1,2,0:T(2,128)S(1)}, s32[16,16,2]{1,2,0:T(2,128)}, u32[]{:S(2)}) copy-start(s32[16,16,2]{1,2,0:T(2,128)} %param.13) | copy-start | bytes 6148
  0.6 12.5 %collective-permute-start.1 = (bf16[4,2,16,1024]{3,2,1,0:T(8,128)(2,1)}, bf16[4,2,16,1024]{3,2,1,0:T(8,128)(2,1)S(1)}, u32[]{:S(2)}, u32[]{:S(2)}) collective-permute-start(bf16[4,2,16,1024]{3,2,1,0:T(8,128)(2,1)} %pool_ref.1), channel_id=1, source_target_pairs={{0,8},{2,10},{4,12},{6,14},{8,16},{10,18},{12,20},{14,22},{16,24},... | collective-permute-start | bytes 786440 | tf_op jit(solution)/shard_map/ppermute | solution.py:432
  3.7 9.4 %collective-permute-start.2 = (bf16[4,2,16,1024]{3,2,1,0:T(8,128)(2,1)}, bf16[4,2,16,1024]{3,2,1,0:T(8,128)(2,1)S(1)}, u32[]{:S(2)}, u32[]{:S(2)}) collective-permute-start(bf16[4,2,16,1024]{3,2,1,0:T(8,128)(2,1)} %pool_ref.1), channel_id=1, source_target_pairs={{0,4},{2,6},{4,0},{6,2},{8,12},{10,14},{12,8},{14,10},{16,20},{18,... | collective-permute-start | bytes 786440 | tf_op jit(solution)/shard_map/ppermute | solution.py:435
  5.2 14.7 %collective-permute-start = (bf16[4,2,16,1024]{3,2,1,0:T(8,128)(2,1)}, bf16[4,2,16,1024]{3,2,1,0:T(8,128)(2,1)S(1)}, u32[]{:S(2)}, u32[]{:S(2)}) collective-permute-start(bf16[4,2,16,1024]{3,2,1,0:T(8,128)(2,1)} %pool_ref.1), channel_id=1, source_target_pairs={{0,24},{2,26},{4,28},{6,30},{8,0},{10,2},{12,4},{14,6},{16,8},{18,... | collective-permute-start | bytes 786440 | tf_op jit(solution)/shard_map/ppermute | solution.py:432
  13.1 7.4 %collective-permute-start.3 = (bf16[4,2,16,1024]{3,2,1,0:T(8,128)(2,1)S(1)}, bf16[4,2,16,1024]{3,2,1,0:T(8,128)(2,1)S(1)}, u32[]{:S(2)}, u32[]{:S(2)}) collective-permute-start(bf16[4,2,16,1024]{3,2,1,0:T(8,128)(2,1)S(1)} %collective-permute-done.1.refs_2_), channel_id=1, source_target_pairs={{0,4},{2,6},{4,0},{6,2},{8,12},{10,14},{12,8},{14,10},{16,20},{18,... | collective-permute-start | bytes 786440 | tf_op jit(solution)/shard_map/ppermute | solution.py:435
  14.9 9.6 %collective-permute-start.4 = (bf16[4,2,16,1024]{3,2,1,0:T(8,128)(2,1)S(1)}, bf16[4,2,16,1024]{3,2,1,0:T(8,128)(2,1)S(1)}, u32[]{:S(2)}, u32[]{:S(2)}) collective-permute-start(bf16[4,2,16,1024]{3,2,1,0:T(8,128)(2,1)S(1)} %collective-permute-done.1.refs_2_), channel_id=1, source_target_pairs={{0,8},{2,10},{4,12},{6,14},{8,16},{10,18},{12,20},{14,22},{16,24},... | collective-permute-start | bytes 786440 | tf_op jit(solution)/shard_map/ppermute | solution.py:432
  14.9 10.2 %collective-permute-start.7 = (bf16[4,2,16,1024]{3,2,1,0:T(8,128)(2,1)}, bf16[4,2,16,1024]{3,2,1,0:T(8,128)(2,1)S(1)}, u32[]{:S(2)}, u32[]{:S(2)}) collective-permute-start(bf16[4,2,16,1024]{3,2,1,0:T(8,128)(2,1)} %pool_ref.1), channel_id=1, source_target_pairs={{0,2},{2,0},{4,6},{6,4},{8,10},{10,8},{12,14},{14,12},{16,18},{18,... | collective-permute-start | bytes 786440 | tf_op jit(solution)/shard_map/ppermute | solution.py:438
  15.8 3.4 %copy-start.1 = (bf16[1024,4096]{1,0:T(8,128)(2,1)S(1)}, bf16[1024,4096]{1,0:T(8,128)(2,1)}, u32[]{:S(2)}) copy-start(bf16[1024,4096]{1,0:T(8,128)(2,1)} %source_ref) | copy-start | bytes 25165828
  19.2 7.0 %copy-start.2 = (bf16[128,1024]{1,0:T(8,128)(2,1)S(1)}, bf16[128,1024]{1,0:T(8,128)(2,1)}, u32[]{:S(2)}) copy-start(bf16[128,1024]{1,0:T(8,128)(2,1)} %get-tuple-element.38.query_ref) | copy-start | bytes 786436
  19.2 7.0 %copy-start.4 = (f32[128,128]{1,0:T(8,128)S(1)}, f32[128,128]{1,0:T(8,128)}, u32[]{:S(2)}) copy-start(f32[128,128]{1,0:T(8,128)} %get-tuple-element.37.column_ref) | copy-start | bytes 196612
  19.2 7.0 %copy-start.5 = (bf16[128,1024]{1,0:T(8,128)(2,1)S(1)}, bf16[128,1024]{1,0:T(8,128)(2,1)}, u32[]{:S(2)}) copy-start(bf16[128,1024]{1,0:T(8,128)(2,1)} %get-tuple-element.42.key_ref) | copy-start | bytes 786436
  19.2 7.0 %copy-start.6 = (bf16[128,1024]{1,0:T(8,128)(2,1)S(1)}, bf16[128,1024]{1,0:T(8,128)(2,1)}, u32[]{:S(2)}) copy-start(bf16[128,1024]{1,0:T(8,128)(2,1)} %get-tuple-element.43.value_ref) | copy-start | bytes 786436
  19.2 7.0 %copy-start.7 = (bf16[4,2,16,1024]{3,2,1,0:T(8,128)(2,1)S(1)}, bf16[4,2,16,1024]{3,2,1,0:T(8,128)(2,1)}, u32[]{:S(2)}) copy-start(bf16[4,2,16,1024]{3,2,1,0:T(8,128)(2,1)} %get-tuple-element.44.refs_0_) | copy-start | bytes 786436
  19.2 7.0 %copy-start.8 = (s32[1,128]{1,0:T(1,128)S(1)}, s32[1,128]{1,0:T(1,128)}, u32[]{:S(2)}) copy-start(s32[1,128]{1,0:T(1,128)} %segments_ref.3) | copy-start | bytes 1540
  19.9 6.3 %collective-permute-start.9 = (bf16[4,2,16,1024]{3,2,1,0:T(8,128)(2,1)S(1)}, bf16[4,2,16,1024]{3,2,1,0:T(8,128)(2,1)S(1)}, u32[]{:S(2)}, u32[]{:S(2)}) collective-permute-start(bf16[4,2,16,1024]{3,2,1,0:T(8,128)(2,1)S(1)} %collective-permute-done.refs_4_), channel_id=1, source_target_pairs={{0,2},{2,0},{4,6},{6,4},{8,10},{10,8},{12,14},{14,12},{16,18},{18,... | collective-permute-start | bytes 786440 | tf_op jit(solution)/shard_map/ppermute | solution.py:438
  20.5 5.7 %collective-permute-start.10 = (bf16[4,2,16,1024]{3,2,1,0:T(8,128)(2,1)S(1)}, bf16[4,2,16,1024]{3,2,1,0:T(8,128)(2,1)S(1)}, u32[]{:S(2)}, u32[]{:S(2)}) collective-permute-start(bf16[4,2,16,1024]{3,2,1,0:T(8,128)(2,1)S(1)} %collective-permute-done.2.refs_6_), channel_id=1, source_target_pairs={{0,2},{2,0},{4,6},{6,4},{8,10},{10,8},{12,14},{14,12},{16,18},{18,... | collective-permute-start | bytes 786440 | tf_op jit(solution)/shard_map/ppermute | solution.py:438
  20.6 5.6 %collective-permute-start.8 = (bf16[4,2,16,1024]{3,2,1,0:T(8,128)(2,1)S(1)}, bf16[4,2,16,1024]{3,2,1,0:T(8,128)(2,1)S(1)}, u32[]{:S(2)}, u32[]{:S(2)}) collective-permute-start(bf16[4,2,16,1024]{3,2,1,0:T(8,128)(2,1)S(1)} %collective-permute-done.1.refs_2_), channel_id=1, source_target_pairs={{0,2},{2,0},{4,6},{6,4},{8,10},{10,8},{12,14},{14,12},{16,18},{18,... | collective-permute-start | bytes 786440 | tf_op jit(solution)/shard_map/ppermute | solution.py:438
  24.5 6.4 %collective-permute-start.6 = (bf16[4,2,16,1024]{3,2,1,0:T(8,128)(2,1)S(1)}, bf16[4,2,16,1024]{3,2,1,0:T(8,128)(2,1)S(1)}, u32[]{:S(2)}, u32[]{:S(2)}) collective-permute-start(bf16[4,2,16,1024]{3,2,1,0:T(8,128)(2,1)S(1)} %collective-permute-done.refs_4_), channel_id=1, source_target_pairs={{0,4},{2,6},{4,0},{6,2},{8,12},{10,14},{12,8},{14,10},{16,20},{18,... | collective-permute-start | bytes 786440 | tf_op jit(solution)/shard_map/ppermute | solution.py:435
  25.1 8.2 %collective-permute-start.5 = (bf16[4,2,16,1024]{3,2,1,0:T(8,128)(2,1)S(1)}, bf16[4,2,16,1024]{3,2,1,0:T(8,128)(2,1)S(1)}, u32[]{:S(2)}, u32[]{:S(2)}) collective-permute-start(bf16[4,2,16,1024]{3,2,1,0:T(8,128)(2,1)S(1)} %collective-permute-done.3.refs_2_), channel_id=1, source_target_pairs={{0,8},{2,10},{4,12},{6,14},{8,16},{10,18},{12,20},{14,22},{16,24},... | collective-permute-start | bytes 786440 | tf_op jit(solution)/shard_map/ppermute | solution.py:432
  30.9 2.4 %collective-permute-start.13 = (bf16[4,2,16,1024]{3,2,1,0:T(8,128)(2,1)S(1)}, bf16[4,2,16,1024]{3,2,1,0:T(8,128)(2,1)S(1)}, u32[]{:S(2)}, u32[]{:S(2)}) collective-permute-start(bf16[4,2,16,1024]{3,2,1,0:T(8,128)(2,1)S(1)} %collective-permute-done.6.refs_4_), channel_id=1, source_target_pairs={{0,2},{2,0},{4,6},{6,4},{8,10},{10,8},{12,14},{14,12},{16,18},{18,... | collective-permute-start | bytes 786440 | tf_op jit(solution)/shard_map/ppermute | solution.py:438
  30.9 2.4 %collective-permute-start.11 = (bf16[4,2,16,1024]{3,2,1,0:T(8,128)(2,1)S(1)}, bf16[4,2,16,1024]{3,2,1,0:T(8,128)(2,1)S(1)}, u32[]{:S(2)}, u32[]{:S(2)}) collective-permute-start(bf16[4,2,16,1024]{3,2,1,0:T(8,128)(2,1)S(1)} %collective-permute-done.4.refs_0_), channel_id=1, source_target_pairs={{0,2},{2,0},{4,6},{6,4},{8,10},{10,8},{12,14},{14,12},{16,18},{18,... | collective-permute-start | bytes 786440 | tf_op jit(solution)/shard_map/ppermute | solution.py:438
  31.4 1.9 %collective-permute-start.12 = (bf16[4,2,16,1024]{3,2,1,0:T(8,128)(2,1)S(1)}, bf16[4,2,16,1024]{3,2,1,0:T(8,128)(2,1)S(1)}, u32[]{:S(2)}, u32[]{:S(2)}) collective-permute-start(bf16[4,2,16,1024]{3,2,1,0:T(8,128)(2,1)S(1)} %collective-permute-done.3.refs_2_), channel_id=1, source_target_pairs={{0,2},{2,0},{4,6},{6,4},{8,10},{10,8},{12,14},{14,12},{16,18},{18,... | collective-permute-start | bytes 786440 | tf_op jit(solution)/shard_map/ppermute | solution.py:438
  33.3 1.5 %collective-permute-start.14 = (bf16[4,2,16,1024]{3,2,1,0:T(8,128)(2,1)S(1)}, bf16[4,2,16,1024]{3,2,1,0:T(8,128)(2,1)S(1)}, u32[]{:S(2)}, u32[]{:S(2)}) collective-permute-start(bf16[4,2,16,1024]{3,2,1,0:T(8,128)(2,1)S(1)} %collective-permute-done.5.refs_6_), channel_id=1, source_target_pairs={{0,2},{2,0},{4,6},{6,4},{8,10},{10,8},{12,14},{14,12},{16,18},{18,... | collective-permute-start | bytes 786440 | tf_op jit(solution)/shard_map/ppermute | solution.py:438
  36.7 7.1 %collective-permute-start.18 = (bf16[64,1280]{1,0:T(8,128)(2,1)S(1)}, bf16[64,1280]{1,0:T(8,128)(2,1)S(1)}, u32[]{:S(2)}, u32[]{:S(2)}) collective-permute-start(bf16[64,1280]{1,0:T(8,128)(2,1)S(1)} %get-tuple-element.62), channel_id=1, source_target_pairs={{0,1},{1,0},{2,3},{3,2},{4,5},{5,4},{6,7},{7,6},{8,9},{9,8},{10,11... | collective-permute-start | bytes 491528 | tf_op jit(solution)/shard_map/ppermute | solution.py:493
  38.7 3.7 %copy-start.9 = (bf16[4096]{0:T(1024)(128)(2,1)S(1)}, bf16[4096]{0:T(1024)(128)(2,1)}, u32[]{:S(2)}) copy-start(bf16[4096]{0:T(1024)(128)(2,1)} %param.17) | copy-start | bytes 24580
  38.8 3.7 %copy-start.3 = (bf16[64,4096]{1,0:T(8,128)(2,1)S(1)}, bf16[64,4096]{1,0:T(8,128)(2,1)}, u32[]{:S(2)}) copy-start(bf16[64,4096]{1,0:T(8,128)(2,1)} %residual_ref.1) | copy-start | bytes 1572868
  38.8 7.9 %collective-permute-start.17 = (bf16[64,1024]{1,0:T(8,128)(2,1)S(1)}, bf16[64,1024]{1,0:T(8,128)(2,1)S(1)}, u32[]{:S(2)}, u32[]{:S(2)}) collective-permute-start(bf16[64,1024]{1,0:T(8,128)(2,1)S(1)} %get-tuple-element.61), channel_id=1, source_target_pairs={{0,1},{1,0},{2,3},{3,2},{4,5},{5,4},{6,7},{7,6},{8,9},{9,8},{10,11... | collective-permute-start | bytes 393224 | tf_op jit(solution)/shard_map/ppermute | solution.py:493
  39.8 9.6 %collective-permute-start.16 = (bf16[64,1024]{1,0:T(8,128)(2,1)S(1)}, bf16[64,1024]{1,0:T(8,128)(2,1)S(1)}, u32[]{:S(2)}, u32[]{:S(2)}) collective-permute-start(bf16[64,1024]{1,0:T(8,128)(2,1)S(1)} %get-tuple-element.60), channel_id=1, source_target_pairs={{0,1},{1,0},{2,3},{3,2},{4,5},{5,4},{6,7},{7,6},{8,9},{9,8},{10,11... | collective-permute-start | bytes 393224 | tf_op jit(solution)/shard_map/ppermute | solution.py:493
  41.8 8.9 %collective-permute-start.15 = (bf16[64,768]{1,0:T(8,128)(2,1)S(1)}, bf16[64,768]{1,0:T(8,128)(2,1)S(1)}, u32[]{:S(2)}, u32[]{:S(2)}) collective-permute-start(bf16[64,768]{1,0:T(8,128)(2,1)S(1)} %get-tuple-element.59), channel_id=1, source_target_pairs={{0,1},{1,0},{2,3},{3,2},{4,5},{5,4},{6,7},{7,6},{8,9},{9,8},{10,11... | collective-permute-start | bytes 294920 | tf_op jit(solution)/shard_map/ppermute | solution.py:493

commit v6 on v5

--- a/solution.py
+++ b/solution.py
@@ -440,7 +440,7 @@
     wanted = lax.dynamic_index_in_dim(fetch_pages, group, axis=0, keepdims=False).reshape(-1)
     table = jnp.concatenate([wanted, page_owner.reshape(-1)])
     wide = out_weight.shape[1] // 16
-    widths = (5 * wide, 4 * wide, 4 * wide, 3 * wide)
+    widths = (6 * wide, 5 * wide, 3 * wide, 2 * wide)
     after = lax.optimization_barrier
     ups = {0: kv_pool, 1: along(kv_pool, 1), -1: along(kv_pool, -1)}
     over = {0: across(kv_pool)}

time: 51.6 us -> 51.6 us (level)
  transfers between devices with their start and end apart: 19 -> 19, of which waited for: 9 -> 8; matrix products, arithmetic and copies ran while one was open for 2% -> 2% of each run, Pallas kernels for 18% -> 18%
where the time goes in v6:
time: 51.6 us; the launch traced here: 51.4 us
  waiting for transfers between devices  18.1 us (35%)
  starting transfers between devices  16.2 us (31%)
  Pallas kernels  12 us (23%)
  local copies, waits for them, and re-layouts  3.62 us (7%)
  between operations  0.86 us (2%)
  other arithmetic  0.73 us (1%)
    ppermute x4, waiting for transfers between devices, along(): return lax.ppermute(values, 'dp', pairs)  7.45 us
    ppermute x4, starting transfers between devices, along(): return lax.ppermute(values, 'dp', pairs)  6.46 us
    ppermute x4, waiting for transfers between devices, body(): pieces.append(lax.ppermute(values, 'tensor', pairs))  6.07 us
    ppermute x4, starting transfers between devices, body(): pieces.append(lax.ppermute(values, 'tensor', pairs))  4.31 us
    ppermute x3, starting transfers between devices, across(): return lax.ppermute(values, 'dp', [(d, d ^ 2) for d in range(groups)])  3.82 us
    pallas_call x1, Pallas kernels, rotate(): pl.pallas_call(functools.partial(rotary_kernel, page), out_shape=(jax.Sha...  3.56 us
    unnamed x20, local copies, waits for them, and re-layouts  3.43 us
    ppermute x3, waiting for transfers between devices, across(): return lax.ppermute(values, 'dp', [(d, d ^ 2) for d in range(groups)])  3.04 us
  transfers between devices with their start and end apart: 19, of which 8 were waited for; matrix products, arithmetic and copies ran while one was open for 2% of the time, Pallas kernels for 18%

profile of v6, /device:TPU:0, one launch (start us, length us, event | category | flops | bytes accessed | tf_op | source)
XLA Modules:
  0.0 51.4 jit_solution(2514200566610967025)
XLA Ops:
  0.6 3.1 %collective-permute-start.1 = (bf16[4,2,16,1024]{3,2,1,0:T(8,128)(2,1)}, bf16[4,2,16,1024]{3,2,1,0:T(8,128)(2,1)S(1)}, u32[]{:S(2)}, u32[]{:S(2)}) collective-permute-start(bf16[4,2,16,1024]{3,2,1,0:T(8,128)(2,1)} %pool_ref.1), channel_id=1, source_target_pairs={{0,8},{2,10},{4,12},{6,14},{8,16},{10,18},{12,20},{14,22},{16,24},... | collective-permute-start | bytes 786440 | tf_op jit(solution)/shard_map/ppermute | solution.py:432
  3.7 1.5 %collective-permute-start.2 = (bf16[4,2,16,1024]{3,2,1,0:T(8,128)(2,1)}, bf16[4,2,16,1024]{3,2,1,0:T(8,128)(2,1)S(1)}, u32[]{:S(2)}, u32[]{:S(2)}) collective-permute-start(bf16[4,2,16,1024]{3,2,1,0:T(8,128)(2,1)} %pool_ref.1), channel_id=1, source_target_pairs={{0,4},{2,6},{4,0},{6,2},{8,12},{10,14},{12,8},{14,10},{16,20},{18,... | collective-permute-start | bytes 786440 | tf_op jit(solution)/shard_map/ppermute | solution.py:435
  5.2 2.2 %collective-permute-start = (bf16[4,2,16,1024]{3,2,1,0:T(8,128)(2,1)}, bf16[4,2,16,1024]{3,2,1,0:T(8,128)(2,1)S(1)}, u32[]{:S(2)}, u32[]{:S(2)}) collective-permute-start(bf16[4,2,16,1024]{3,2,1,0:T(8,128)(2,1)} %pool_ref.1), channel_id=1, source_target_pairs={{0,24},{2,26},{4,28},{6,30},{8,0},{10,2},{12,4},{14,6},{16,8},{18,... | collective-permute-start | bytes 786440 | tf_op jit(solution)/shard_map/ppermute | solution.py:432
  7.5 3.6 %rotary.1 = (f32[128,128]{1,0:T(8,128)}, bf16[128,1024]{1,0:T(8,128)(2,1)}, bf16[128,1024]{1,0:T(8,128)(2,1)}, bf16[128,1024]{1,0:T(8,128)(2,1)}, bf16[4,2,16,10...) custom-call(s32[1,128]{1,0:T(1,128)} %segments_ref.3, s32[1,32]{1,0:T(1,128)} %owners_ref.1, bf16[128,1024]{1,0:T(8,128)(2,1)} %query_ref.1, ...), custom_call_target="tpu_custom_call" | custom-call | flops 1 | bytes 1 | tf_op jit(solution)/shard_map/rotary/pallas_call | solution.py:99
  11.1 2.1 %collective-permute-done.1.refs_2_ = bf16[4,2,16,1024]{3,2,1,0:T(8,128)(2,1)S(1)} collective-permute-done((bf16[4,2,16,1024]{3,2,1,0:T(8,128)(2,1)}, bf16[4,2,16,1024]{3,2,1,0:T(8,128)(2,1)S(1)}, u32[]{:S(2)}, u32[]{:S(2)}) %collective-permute-start.1) | collective-permute-done | bytes 262176 | tf_op jit(solution)/shard_map/ppermute | solution.py:432
  13.1 1.8 %collective-permute-start.3 = (bf16[4,2,16,1024]{3,2,1,0:T(8,128)(2,1)S(1)}, bf16[4,2,16,1024]{3,2,1,0:T(8,128)(2,1)S(1)}, u32[]{:S(2)}, u32[]{:S(2)}) collective-permute-start(bf16[4,2,16,1024]{3,2,1,0:T(8,128)(2,1)S(1)} %collective-permute-done.1.refs_2_), channel_id=1, source_target_pairs={{0,4},{2,6},{4,0},{6,2},{8,12},{10,14},{12,8},{14,10},{16,20},{18,... | collective-permute-start | bytes 786440 | tf_op jit(solution)/shard_map/ppermute | solution.py:435
  15.1 0.7 %pad_add_fusion.table_ref = s32[64]{0:T(128)S(1)} fusion(s32[32]{0:T(128)} %bitcast.1, s32[32]{0:T(128)S(1)} %reshape.15), kind=kLoop, calls=%fused_computation | loop fusion | flops 64 | bytes 512 | tf_op jit(solution)/shard_map/concatenate | solution.py:441
  15.8 3.4 %copy-done.1 = bf16[1024,4096]{1,0:T(8,128)(2,1)S(1)} copy-done((bf16[1024,4096]{1,0:T(8,128)(2,1)S(1)}, bf16[1024,4096]{1,0:T(8,128)(2,1)}, u32[]{:S(2)}) %copy-start.1) | copy-done | bytes 8388632
  19.3 0.7 %stage.1.weight_ref = bf16[1024,4096]{1,0:T(8,128)(2,1)S(1)} custom-call(bf16[1024,4096]{1,0:T(8,128)(2,1)S(1)} %copy-done.1), custom_call_target="tpu_custom_call" | custom-call | flops 1 | bytes 1 | tf_op jit(solution)/shard_map/stage/pallas_call | solution.py:141
  19.9 0.6 %collective-permute-start.9 = (bf16[4,2,16,1024]{3,2,1,0:T(8,128)(2,1)S(1)}, bf16[4,2,16,1024]{3,2,1,0:T(8,128)(2,1)S(1)}, u32[]{:S(2)}, u32[]{:S(2)}) collective-permute-start(bf16[4,2,16,1024]{3,2,1,0:T(8,128)(2,1)S(1)} %collective-permute-done.refs_4_), channel_id=1, source_target_pairs={{0,2},{2,0},{4,6},{6,4},{8,10},{10,8},{12,14},{14,12},{16,18},{18,... | collective-permute-start | bytes 786440 | tf_op jit(solution)/shard_map/ppermute | solution.py:438
  20.6 0.4 collective-permute-start.8
  21.0 3.5 %collective-permute-done.4.refs_0_ = bf16[4,2,16,1024]{3,2,1,0:T(8,128)(2,1)S(1)} collective-permute-done((bf16[4,2,16,1024]{3,2,1,0:T(8,128)(2,1)S(1)}, bf16[4,2,16,1024]{3,2,1,0:T(8,128)(2,1)S(1)}, u32[]{:S(2)}, u32[]{:S(2)}) %collective-permute-start.4) | collective-permute-done | bytes 262176 | tf_op jit(solution)/shard_map/ppermute | solution.py:432
  24.5 0.5 %collective-permute-start.6 = (bf16[4,2,16,1024]{3,2,1,0:T(8,128)(2,1)S(1)}, bf16[4,2,16,1024]{3,2,1,0:T(8,128)(2,1)S(1)}, u32[]{:S(2)}, u32[]{:S(2)}) collective-permute-start(bf16[4,2,16,1024]{3,2,1,0:T(8,128)(2,1)S(1)} %collective-permute-done.refs_4_), channel_id=1, source_target_pairs={{0,4},{2,6},{4,0},{6,2},{8,12},{10,14},{12,8},{14,10},{16,20},{18,... | collective-permute-start | bytes 786440 | tf_op jit(solution)/shard_map/ppermute | solution.py:435
  25.1 1.1 %collective-permute-start.5 = (bf16[4,2,16,1024]{3,2,1,0:T(8,128)(2,1)S(1)}, bf16[4,2,16,1024]{3,2,1,0:T(8,128)(2,1)S(1)}, u32[]{:S(2)}, u32[]{:S(2)}) collective-permute-start(bf16[4,2,16,1024]{3,2,1,0:T(8,128)(2,1)S(1)} %collective-permute-done.3.refs_2_), channel_id=1, source_target_pairs={{0,8},{2,10},{4,12},{6,14},{8,16},{10,18},{12,20},{14,22},{16,24},... | collective-permute-start | bytes 786440 | tf_op jit(solution)/shard_map/ppermute | solution.py:432
  26.3 1.6 %early.1 = (f32[128,2048]{1,0:T(8,128)S(1)}, f32[128,1024]{1,0:T(8,128)S(1)}) custom-call(s32[64]{0:T(128)S(1)} %pad_add_fusion.table_ref, s32[1,128]{1,0:T(1,128)S(1)} %copy-done.8, f32[128,128]{1,0:T(8,128)S(1)} %copy-done.4, bf16[128,1024]{1,0:T(8,128)(2,1)S(1)} %copy-done.2, bf16[128,1024]{1,0:T(8,128)(2,1)S(1)} %copy-done.5, ...), custom_call_target="tpu_custom_call" | custom-call | flops 1 | bytes 1 | tf_op jit(solution)/shard_map/early/pallas_call | solution.py:296
  27.9 3.0 %collective-permute-done.6.refs_4_ = bf16[4,2,16,1024]{3,2,1,0:T(8,128)(2,1)S(1)} collective-permute-done((bf16[4,2,16,1024]{3,2,1,0:T(8,128)(2,1)S(1)}, bf16[4,2,16,1024]{3,2,1,0:T(8,128)(2,1)S(1)}, u32[]{:S(2)}, u32[]{:S(2)}) %collective-permute-start.6) | collective-permute-done | bytes 262176 | tf_op jit(solution)/shard_map/ppermute | solution.py:435
  30.9 0.5 collective-permute-start.11
  31.4 1.8 %collective-permute-done.5.refs_6_ = bf16[4,2,16,1024]{3,2,1,0:T(8,128)(2,1)S(1)} collective-permute-done((bf16[4,2,16,1024]{3,2,1,0:T(8,128)(2,1)S(1)}, bf16[4,2,16,1024]{3,2,1,0:T(8,128)(2,1)S(1)}, u32[]{:S(2)}, u32[]{:S(2)}) %collective-permute-start.5) | collective-permute-done | bytes 262176 | tf_op jit(solution)/shard_map/ppermute | solution.py:432
  33.3 1.5 %collective-permute-done.14.refs_7_ = bf16[4,2,16,1024]{3,2,1,0:T(8,128)(2,1)S(1)} collective-permute-done((bf16[4,2,16,1024]{3,2,1,0:T(8,128)(2,1)S(1)}, bf16[4,2,16,1024]{3,2,1,0:T(8,128)(2,1)S(1)}, u32[]{:S(2)}, u32[]{:S(2)}) %collective-permute-start.14) | collective-permute-done | bytes 262176 | tf_op jit(solution)/shard_map/ppermute | solution.py:438
  34.8 2.0 %late.1 = (bf16[128,1024]{1,0:T(8,128)(2,1)S(1)}, bf16[64,1536]{1,0:T(8,128)(2,1)S(1)}, bf16[64,1536]{1,0:T(8,128)(2,1)S(1)}) custom-call(s32[64]{0:T(128)S(1)} %pad_add_fusion.table_ref, f32[128,128]{1,0:T(8,128)S(1)} %copy-done.4, bf16[128,1024]{1,0:T(8,128)(2,1)S(1)} %copy-done.2, f32[128,2048]{1,0:T(8,128)S(1)} %get-tuple-element.48.mixed_ref, ...), custom_call_target="tpu_custom_call" | custom-call | flops 1 | bytes 1 | tf_op jit(solution)/shard_map/late/pallas_call | solution.py:317
  36.8 1.5 %collective-permute-start.18 = (bf16[64,1536]{1,0:T(8,128)(2,1)S(1)}, bf16[64,1536]{1,0:T(8,128)(2,1)S(1)}, u32[]{:S(2)}, u32[]{:S(2)}) collective-permute-start(bf16[64,1536]{1,0:T(8,128)(2,1)S(1)} %get-tuple-element.62), channel_id=1, source_target_pairs={{0,1},{1,0},{2,3},{3,2},{4,5},{5,4},{6,7},{7,6},{8,9},{9,8},{10,11... | collective-permute-start | bytes 589832 | tf_op jit(solution)/shard_map/ppermute | solution.py:493
  38.3 0.6 %project.3 = (bf16[64,1280]{1,0:T(8,128)(2,1)S(1)}, bf16[64,1280]{1,0:T(8,128)(2,1)S(1)}) custom-call(bf16[128,1024]{1,0:T(8,128)(2,1)S(1)} %get-tuple-element.55.context_ref, bf16[1024,4096]{1,0:T(8,128)(2,1)S(1)} %stage.1.weight_ref), custom_call_target="tpu_custom_call" | custom-call | flops 1 | bytes 1 | tf_op jit(solution)/shard_map/project/pallas_call | solution.py:339
  38.9 0.6 %collective-permute-start.17 = (bf16[64,1280]{1,0:T(8,128)(2,1)S(1)}, bf16[64,1280]{1,0:T(8,128)(2,1)S(1)}, u32[]{:S(2)}, u32[]{:S(2)}) collective-permute-start(bf16[64,1280]{1,0:T(8,128)(2,1)S(1)} %get-tuple-element.61), channel_id=1, source_target_pairs={{0,1},{1,0},{2,3},{3,2},{4,5},{5,4},{6,7},{7,6},{8,9},{9,8},{10,11... | collective-permute-start | bytes 491528 | tf_op jit(solution)/shard_map/ppermute | solution.py:493
  39.9 1.5 %collective-permute-start.16 = (bf16[64,768]{1,0:T(8,128)(2,1)S(1)}, bf16[64,768]{1,0:T(8,128)(2,1)S(1)}, u32[]{:S(2)}, u32[]{:S(2)}) collective-permute-start(bf16[64,768]{1,0:T(8,128)(2,1)S(1)} %get-tuple-element.60), channel_id=1, source_target_pairs={{0,1},{1,0},{2,3},{3,2},{4,5},{5,4},{6,7},{7,6},{8,9},{9,8},{10,11... | collective-permute-start | bytes 294920 | tf_op jit(solution)/shard_map/ppermute | solution.py:493
  41.8 0.6 %collective-permute-start.15 = (bf16[64,512]{1,0:T(8,128)(2,1)S(1)}, bf16[64,512]{1,0:T(8,128)(2,1)S(1)}, u32[]{:S(2)}, u32[]{:S(2)}) collective-permute-start(bf16[64,512]{1,0:T(8,128)(2,1)S(1)} %get-tuple-element.59), channel_id=1, source_target_pairs={{0,1},{1,0},{2,3},{3,2},{4,5},{5,4},{6,7},{7,6},{8,9},{9,8},{10,11... | collective-permute-start | bytes 196616 | tf_op jit(solution)/shard_map/ppermute | solution.py:493
  42.6 2.0 %collective-permute-done.18.refs_0_ = bf16[64,1536]{1,0:T(8,128)(2,1)S(1)} collective-permute-done((bf16[64,1536]{1,0:T(8,128)(2,1)S(1)}, bf16[64,1536]{1,0:T(8,128)(2,1)S(1)}, u32[]{:S(2)}, u32[]{:S(2)}) %collective-permute-start.18) | collective-permute-done | bytes 196640 | tf_op jit(solution)/shard_map/ppermute | solution.py:493
  44.6 0.7 %finish.4.refs_1_ = bf16[64,4096]{1,0:T(8,128)(2,1)} custom-call(f32[64,4096]{1,0:T(8,128)S(1)} %base.1.base_ref, bf16[64,1536]{1,0:T(8,128)(2,1)S(1)} %collective-permute-done.18.refs_0_), custom_call_target="tpu_custom_call" | custom-call | flops 1 | bytes 1 | tf_op jit(solution)/shard_map/finish/pallas_call | solution.py:403
  45.3 2.8 %collective-permute-done.17.refs_0_ = bf16[64,1280]{1,0:T(8,128)(2,1)S(1)} collective-permute-done((bf16[64,1280]{1,0:T(8,128)(2,1)S(1)}, bf16[64,1280]{1,0:T(8,128)(2,1)S(1)}, u32[]{:S(2)}, u32[]{:S(2)}) %collective-permute-start.17) | collective-permute-done | bytes 163872 | tf_op jit(solution)/shard_map/ppermute | solution.py:493
  48.1 0.7 %finish.5.refs_1_ = bf16[64,4096]{1,0:T(8,128)(2,1)} custom-call(f32[64,4096]{1,0:T(8,128)S(1)} %base.1.base_ref, bf16[64,1280]{1,0:T(8,128)(2,1)S(1)} %collective-permute-done.17.refs_0_, bf16[64,4096]{1,0:T(8,128)(2,1)} %finish.4.refs_1_), custom_call_target="tpu_custom_call", output_to_operand_aliasing={{}: (2, {})} | custom-call | flops 1 | bytes 1 | tf_op jit(solution)/shard_map/finish/pallas_call | solution.py:403
  48.8 1.3 %collective-permute-done.16.refs_0_ = bf16[64,768]{1,0:T(8,128)(2,1)S(1)} collective-permute-done((bf16[64,768]{1,0:T(8,128)(2,1)S(1)}, bf16[64,768]{1,0:T(8,128)(2,1)S(1)}, u32[]{:S(2)}, u32[]{:S(2)}) %collective-permute-start.16) | collective-permute-done | bytes 98336 | tf_op jit(solution)/shard_map/ppermute | solution.py:493
  50.1 0.7 %finish.6.refs_1_ = bf16[64,4096]{1,0:T(8,128)(2,1)} custom-call(f32[64,4096]{1,0:T(8,128)S(1)} %base.1.base_ref, bf16[64,768]{1,0:T(8,128)(2,1)S(1)} %collective-permute-done.16.refs_0_, bf16[64,4096]{1,0:T(8,128)(2,1)} %finish.5.refs_1_), custom_call_target="tpu_custom_call", output_to_operand_aliasing={{}: (2, {})} | custom-call | flops 1 | bytes 1 | tf_op jit(solution)/shard_map/finish/pallas_call | solution.py:403
  50.8 0.7 %finish.7 = bf16[64,4096]{1,0:T(8,128)(2,1)} custom-call(f32[64,4096]{1,0:T(8,128)S(1)} %base.1.base_ref, bf16[64,512]{1,0:T(8,128)(2,1)S(1)} %collective-permute-done.15.refs_0_, bf16[64,4096]{1,0:T(8,128)(2,1)} %finish.6.refs_1_), custom_call_target="tpu_custom_call", output_to_operand_aliasing={{}: (2, {})} | custom-call | flops 1 | bytes 1 | tf_op jit(solution)/shard_map/finish/pallas_call | solution.py:403
  (43 shorter events, 1.3 us)
Async XLA Ops:
  0.6 14.3 %copy-start = (s32[16,16,2]{1,2,0:T(2,128)S(1)}, s32[16,16,2]{1,2,0:T(2,128)}, u32[]{:S(2)}) copy-start(s32[16,16,2]{1,2,0:T(2,128)} %param.13) | copy-start | bytes 6148
  0.6 12.5 %collective-permute-start.1 = (bf16[4,2,16,1024]{3,2,1,0:T(8,128)(2,1)}, bf16[4,2,16,1024]{3,2,1,0:T(8,128)(2,1)S(1)}, u32[]{:S(2)}, u32[]{:S(2)}) collective-permute-start(bf16[4,2,16,1024]{3,2,1,0:T(8,128)(2,1)} %pool_ref.1), channel_id=1, source_target_pairs={{0,8},{2,10},{4,12},{6,14},{8,16},{10,18},{12,20},{14,22},{16,24},... | collective-permute-start | bytes 786440 | tf_op jit(solution)/shard_map/ppermute | solution.py:432
  3.7 9.4 %collective-permute-start.2 = (bf16[4,2,16,1024]{3,2,1,0:T(8,128)(2,1)}, bf16[4,2,16,1024]{3,2,1,0:T(8,128)(2,1)S(1)}, u32[]{:S(2)}, u32[]{:S(2)}) collective-permute-start(bf16[4,2,16,1024]{3,2,1,0:T(8,128)(2,1)} %pool_ref.1), channel_id=1, source_target_pairs={{0,4},{2,6},{4,0},{6,2},{8,12},{10,14},{12,8},{14,10},{16,20},{18,... | collective-permute-start | bytes 786440 | tf_op jit(solution)/shard_map/ppermute | solution.py:435
  5.2 14.7 %collective-permute-start = (bf16[4,2,16,1024]{3,2,1,0:T(8,128)(2,1)}, bf16[4,2,16,1024]{3,2,1,0:T(8,128)(2,1)S(1)}, u32[]{:S(2)}, u32[]{:S(2)}) collective-permute-start(bf16[4,2,16,1024]{3,2,1,0:T(8,128)(2,1)} %pool_ref.1), channel_id=1, source_target_pairs={{0,24},{2,26},{4,28},{6,30},{8,0},{10,2},{12,4},{14,6},{16,8},{18,... | collective-permute-start | bytes 786440 | tf_op jit(solution)/shard_map/ppermute | solution.py:432
  13.1 7.4 %collective-permute-start.3 = (bf16[4,2,16,1024]{3,2,1,0:T(8,128)(2,1)S(1)}, bf16[4,2,16,1024]{3,2,1,0:T(8,128)(2,1)S(1)}, u32[]{:S(2)}, u32[]{:S(2)}) collective-permute-start(bf16[4,2,16,1024]{3,2,1,0:T(8,128)(2,1)S(1)} %collective-permute-done.1.refs_2_), channel_id=1, source_target_pairs={{0,4},{2,6},{4,0},{6,2},{8,12},{10,14},{12,8},{14,10},{16,20},{18,... | collective-permute-start | bytes 786440 | tf_op jit(solution)/shard_map/ppermute | solution.py:435
  14.9 9.6 %collective-permute-start.4 = (bf16[4,2,16,1024]{3,2,1,0:T(8,128)(2,1)S(1)}, bf16[4,2,16,1024]{3,2,1,0:T(8,128)(2,1)S(1)}, u32[]{:S(2)}, u32[]{:S(2)}) collective-permute-start(bf16[4,2,16,1024]{3,2,1,0:T(8,128)(2,1)S(1)} %collective-permute-done.1.refs_2_), channel_id=1, source_target_pairs={{0,8},{2,10},{4,12},{6,14},{8,16},{10,18},{12,20},{14,22},{16,24},... | collective-permute-start | bytes 786440 | tf_op jit(solution)/shard_map/ppermute | solution.py:432
  14.9 10.2 %collective-permute-start.7 = (bf16[4,2,16,1024]{3,2,1,0:T(8,128)(2,1)}, bf16[4,2,16,1024]{3,2,1,0:T(8,128)(2,1)S(1)}, u32[]{:S(2)}, u32[]{:S(2)}) collective-permute-start(bf16[4,2,16,1024]{3,2,1,0:T(8,128)(2,1)} %pool_ref.1), channel_id=1, source_target_pairs={{0,2},{2,0},{4,6},{6,4},{8,10},{10,8},{12,14},{14,12},{16,18},{18,... | collective-permute-start | bytes 786440 | tf_op jit(solution)/shard_map/ppermute | solution.py:438
  15.8 3.4 %copy-start.1 = (bf16[1024,4096]{1,0:T(8,128)(2,1)S(1)}, bf16[1024,4096]{1,0:T(8,128)(2,1)}, u32[]{:S(2)}) copy-start(bf16[1024,4096]{1,0:T(8,128)(2,1)} %source_ref) | copy-start | bytes 25165828
  19.2 7.0 %copy-start.2 = (bf16[128,1024]{1,0:T(8,128)(2,1)S(1)}, bf16[128,1024]{1,0:T(8,128)(2,1)}, u32[]{:S(2)}) copy-start(bf16[128,1024]{1,0:T(8,128)(2,1)} %get-tuple-element.38.query_ref) | copy-start | bytes 786436
  19.2 7.0 %copy-start.4 = (f32[128,128]{1,0:T(8,128)S(1)}, f32[128,128]{1,0:T(8,128)}, u32[]{:S(2)}) copy-start(f32[128,128]{1,0:T(8,128)} %get-tuple-element.37.column_ref) | copy-start | bytes 196612
  19.2 7.0 %copy-start.5 = (bf16[128,1024]{1,0:T(8,128)(2,1)S(1)}, bf16[128,1024]{1,0:T(8,128)(2,1)}, u32[]{:S(2)}) copy-start(bf16[128,1024]{1,0:T(8,128)(2,1)} %get-tuple-element.42.key_ref) | copy-start | bytes 786436
  19.2 7.0 %copy-start.6 = (bf16[128,1024]{1,0:T(8,128)(2,1)S(1)}, bf16[128,1024]{1,0:T(8,128)(2,1)}, u32[]{:S(2)}) copy-start(bf16[128,1024]{1,0:T(8,128)(2,1)} %get-tuple-element.43.value_ref) | copy-start | bytes 786436
  19.2 7.0 %copy-start.7 = (bf16[4,2,16,1024]{3,2,1,0:T(8,128)(2,1)S(1)}, bf16[4,2,16,1024]{3,2,1,0:T(8,128)(2,1)}, u32[]{:S(2)}) copy-start(bf16[4,2,16,1024]{3,2,1,0:T(8,128)(2,1)} %get-tuple-element.44.refs_0_) | copy-start | bytes 786436
  19.2 7.0 %copy-start.8 = (s32[1,128]{1,0:T(1,128)S(1)}, s32[1,128]{1,0:T(1,128)}, u32[]{:S(2)}) copy-start(s32[1,128]{1,0:T(1,128)} %segments_ref.3) | copy-start | bytes 1540
  19.9 6.3 %collective-permute-start.9 = (bf16[4,2,16,1024]{3,2,1,0:T(8,128)(2,1)S(1)}, bf16[4,2,16,1024]{3,2,1,0:T(8,128)(2,1)S(1)}, u32[]{:S(2)}, u32[]{:S(2)}) collective-permute-start(bf16[4,2,16,1024]{3,2,1,0:T(8,128)(2,1)S(1)} %collective-permute-done.refs_4_), channel_id=1, source_target_pairs={{0,2},{2,0},{4,6},{6,4},{8,10},{10,8},{12,14},{14,12},{16,18},{18,... | collective-permute-start | bytes 786440 | tf_op jit(solution)/shard_map/ppermute | solution.py:438
  20.5 5.7 %collective-permute-start.10 = (bf16[4,2,16,1024]{3,2,1,0:T(8,128)(2,1)S(1)}, bf16[4,2,16,1024]{3,2,1,0:T(8,128)(2,1)S(1)}, u32[]{:S(2)}, u32[]{:S(2)}) collective-permute-start(bf16[4,2,16,1024]{3,2,1,0:T(8,128)(2,1)S(1)} %collective-permute-done.2.refs_6_), channel_id=1, source_target_pairs={{0,2},{2,0},{4,6},{6,4},{8,10},{10,8},{12,14},{14,12},{16,18},{18,... | collective-permute-start | bytes 786440 | tf_op jit(solution)/shard_map/ppermute | solution.py:438
  20.6 5.6 %collective-permute-start.8 = (bf16[4,2,16,1024]{3,2,1,0:T(8,128)(2,1)S(1)}, bf16[4,2,16,1024]{3,2,1,0:T(8,128)(2,1)S(1)}, u32[]{:S(2)}, u32[]{:S(2)}) collective-permute-start(bf16[4,2,16,1024]{3,2,1,0:T(8,128)(2,1)S(1)} %collective-permute-done.1.refs_2_), channel_id=1, source_target_pairs={{0,2},{2,0},{4,6},{6,4},{8,10},{10,8},{12,14},{14,12},{16,18},{18,... | collective-permute-start | bytes 786440 | tf_op jit(solution)/shard_map/ppermute | solution.py:438
  24.5 6.4 %collective-permute-start.6 = (bf16[4,2,16,1024]{3,2,1,0:T(8,128)(2,1)S(1)}, bf16[4,2,16,1024]{3,2,1,0:T(8,128)(2,1)S(1)}, u32[]{:S(2)}, u32[]{:S(2)}) collective-permute-start(bf16[4,2,16,1024]{3,2,1,0:T(8,128)(2,1)S(1)} %collective-permute-done.refs_4_), channel_id=1, source_target_pairs={{0,4},{2,6},{4,0},{6,2},{8,12},{10,14},{12,8},{14,10},{16,20},{18,... | collective-permute-start | bytes 786440 | tf_op jit(solution)/shard_map/ppermute | solution.py:435
  25.1 8.2 %collective-permute-start.5 = (bf16[4,2,16,1024]{3,2,1,0:T(8,128)(2,1)S(1)}, bf16[4,2,16,1024]{3,2,1,0:T(8,128)(2,1)S(1)}, u32[]{:S(2)}, u32[]{:S(2)}) collective-permute-start(bf16[4,2,16,1024]{3,2,1,0:T(8,128)(2,1)S(1)} %collective-permute-done.3.refs_2_), channel_id=1, source_target_pairs={{0,8},{2,10},{4,12},{6,14},{8,16},{10,18},{12,20},{14,22},{16,24},... | collective-permute-start | bytes 786440 | tf_op jit(solution)/shard_map/ppermute | solution.py:432
  30.9 2.4 %collective-permute-start.13 = (bf16[4,2,16,1024]{3,2,1,0:T(8,128)(2,1)S(1)}, bf16[4,2,16,1024]{3,2,1,0:T(8,128)(2,1)S(1)}, u32[]{:S(2)}, u32[]{:S(2)}) collective-permute-start(bf16[4,2,16,1024]{3,2,1,0:T(8,128)(2,1)S(1)} %collective-permute-done.6.refs_4_), channel_id=1, source_target_pairs={{0,2},{2,0},{4,6},{6,4},{8,10},{10,8},{12,14},{14,12},{16,18},{18,... | collective-permute-start | bytes 786440 | tf_op jit(solution)/shard_map/ppermute | solution.py:438
  30.9 2.4 %collective-permute-start.11 = (bf16[4,2,16,1024]{3,2,1,0:T(8,128)(2,1)S(1)}, bf16[4,2,16,1024]{3,2,1,0:T(8,128)(2,1)S(1)}, u32[]{:S(2)}, u32[]{:S(2)}) collective-permute-start(bf16[4,2,16,1024]{3,2,1,0:T(8,128)(2,1)S(1)} %collective-permute-done.4.refs_0_), channel_id=1, source_target_pairs={{0,2},{2,0},{4,6},{6,4},{8,10},{10,8},{12,14},{14,12},{16,18},{18,... | collective-permute-start | bytes 786440 | tf_op jit(solution)/shard_map/ppermute | solution.py:438
  31.4 1.9 %collective-permute-start.12 = (bf16[4,2,16,1024]{3,2,1,0:T(8,128)(2,1)S(1)}, bf16[4,2,16,1024]{3,2,1,0:T(8,128)(2,1)S(1)}, u32[]{:S(2)}, u32[]{:S(2)}) collective-permute-start(bf16[4,2,16,1024]{3,2,1,0:T(8,128)(2,1)S(1)} %collective-permute-done.3.refs_2_), channel_id=1, source_target_pairs={{0,2},{2,0},{4,6},{6,4},{8,10},{10,8},{12,14},{14,12},{16,18},{18,... | collective-permute-start | bytes 786440 | tf_op jit(solution)/shard_map/ppermute | solution.py:438
  33.3 1.5 %collective-permute-start.14 = (bf16[4,2,16,1024]{3,2,1,0:T(8,128)(2,1)S(1)}, bf16[4,2,16,1024]{3,2,1,0:T(8,128)(2,1)S(1)}, u32[]{:S(2)}, u32[]{:S(2)}) collective-permute-start(bf16[4,2,16,1024]{3,2,1,0:T(8,128)(2,1)S(1)} %collective-permute-done.5.refs_6_), channel_id=1, source_target_pairs={{0,2},{2,0},{4,6},{6,4},{8,10},{10,8},{12,14},{14,12},{16,18},{18,... | collective-permute-start | bytes 786440 | tf_op jit(solution)/shard_map/ppermute | solution.py:438
  36.8 7.8 %collective-permute-start.18 = (bf16[64,1536]{1,0:T(8,128)(2,1)S(1)}, bf16[64,1536]{1,0:T(8,128)(2,1)S(1)}, u32[]{:S(2)}, u32[]{:S(2)}) collective-permute-start(bf16[64,1536]{1,0:T(8,128)(2,1)S(1)} %get-tuple-element.62), channel_id=1, source_target_pairs={{0,1},{1,0},{2,3},{3,2},{4,5},{5,4},{6,7},{7,6},{8,9},{9,8},{10,11... | collective-permute-start | bytes 589832 | tf_op jit(solution)/shard_map/ppermute | solution.py:493
  38.9 3.5 %copy-start.9 = (bf16[4096]{0:T(1024)(128)(2,1)S(1)}, bf16[4096]{0:T(1024)(128)(2,1)}, u32[]{:S(2)}) copy-start(bf16[4096]{0:T(1024)(128)(2,1)} %param.17) | copy-start | bytes 24580
  38.9 3.5 %copy-start.3 = (bf16[64,4096]{1,0:T(8,128)(2,1)S(1)}, bf16[64,4096]{1,0:T(8,128)(2,1)}, u32[]{:S(2)}) copy-start(bf16[64,4096]{1,0:T(8,128)(2,1)} %residual_ref.1) | copy-start | bytes 1572868
  38.9 9.2 %collective-permute-start.17 = (bf16[64,1280]{1,0:T(8,128)(2,1)S(1)}, bf16[64,1280]{1,0:T(8,128)(2,1)S(1)}, u32[]{:S(2)}, u32[]{:S(2)}) collective-permute-start(bf16[64,1280]{1,0:T(8,128)(2,1)S(1)} %get-tuple-element.61), channel_id=1, source_target_pairs={{0,1},{1,0},{2,3},{3,2},{4,5},{5,4},{6,7},{7,6},{8,9},{9,8},{10,11... | collective-permute-start | bytes 491528 | tf_op jit(solution)/shard_map/ppermute | solution.py:493
  39.9 10.2 %collective-permute-start.16 = (bf16[64,768]{1,0:T(8,128)(2,1)S(1)}, bf16[64,768]{1,0:T(8,128)(2,1)S(1)}, u32[]{:S(2)}, u32[]{:S(2)}) collective-permute-start(bf16[64,768]{1,0:T(8,128)(2,1)S(1)} %get-tuple-element.60), channel_id=1, source_target_pairs={{0,1},{1,0},{2,3},{3,2},{4,5},{5,4},{6,7},{7,6},{8,9},{9,8},{10,11... | collective-permute-start | bytes 294920 | tf_op jit(solution)/shard_map/ppermute | solution.py:493
  41.8 9.0 %collective-permute-start.15 = (bf16[64,512]{1,0:T(8,128)(2,1)S(1)}, bf16[64,512]{1,0:T(8,128)(2,1)S(1)}, u32[]{:S(2)}, u32[]{:S(2)}) collective-permute-start(bf16[64,512]{1,0:T(8,128)(2,1)S(1)} %get-tuple-element.59), channel_id=1, source_target_pairs={{0,1},{1,0},{2,3},{3,2},{4,5},{5,4},{6,7},{7,6},{8,9},{9,8},{10,11... | collective-permute-start | bytes 196616 | tf_op jit(solution)/shard_map/ppermute | solution.py:493
